TPU v7x, 32 devices: a whole 2x2x4 slice. The times are simulated.
32 devices in a mesh: dp: 8 (over z, x), expert: 4 (over y, core).
Axes of the slice: x: 2, y: 2, z: 4, core: 2. Of those that a mesh axis runs over, the one named last changes fastest.
Arguments:
- tokens: bfloat16 [8192, 768], P(('dp', 'expert')), may hold values from -6 to 6
- conditioning: bfloat16 [8, 4, 768], P('dp'), may hold values from -6 to 6
- routes: int32 [8192, 2], P(('dp', 'expert')), may hold values from 0 to 3, as said below
- gate_weights: float32 [8192, 2], P(('dp', 'expert')), may hold values from 0.25 to 0.75
- image_counts: int32 [8], P('dp'), may hold values from 1 to 4
- image_lengths: int32 [8, 4], P('dp'), may hold values from 0 to 1024, as said below
- cotangent: bfloat16 [8192, 768], P(('dp', 'expert')), may hold values from -6 to 6
- qkv_weight: bfloat16 [768, 2304], P('dp'), may hold values from -0.21875 to 0.21875
- qv_bias: bfloat16 [1536], P('dp'), may hold values from -1.5 to 1.5
- proj_weight: bfloat16 [768, 768], P('dp'), may hold values from -1.75 to 1.75
- proj_bias: bfloat16 [768], P('dp'), may hold values from -1.5 to 1.5
- ada_weight: bfloat16 [768, 4608], P('dp'), may hold values from -0.21875 to 0.21875
- ada_bias: bfloat16 [4608], P('dp'), may hold values from -1.5 to 1.5
- up_weight: bfloat16 [768, 3072], P('dp'), may hold values from -0.21875 to 0.21875
- up_bias: bfloat16 [3072], P('dp'), may hold values from -1.5 to 1.5
- down_weight: bfloat16 [3072, 768], P('dp'), may hold values from -0.109375 to 0.109375
- down_bias: bfloat16 [768], P('dp'), may hold values from -1.5 to 1.5
- routed_up: bfloat16 [4, 768, 3072], P('expert', 'dp'), may hold values from -0.21875 to 0.21875
- routed_upbias: bfloat16 [4, 3072], P('expert', 'dp'), may hold values from -1.5 to 1.5
- routed_down: bfloat16 [4, 3072, 768], P('expert', 'dp'), may hold values from -0.109375 to 0.109375
- routed_downbias: bfloat16 [4, 768], P('expert', 'dp'), may hold values from -1.5 to 1.5
Outputs:
- output: bfloat16 [8192, 768], P(('dp', 'expert'))
- tokens_grad: float32 [8192, 768], P(('dp', 'expert'))
- conditioning_grad: float32 [8, 4, 768], P('dp')
- qkv_grad: float32 [768, 2304], P('dp')
- qvbias_grad: float32 [1536], P('dp')
- proj_grad: float32 [768, 768], P('dp')
- projbias_grad: float32 [768], P('dp')
- ada_grad: float32 [768, 4608], P('dp')
- adabias_grad: float32 [4608], P('dp')
- up_grad: float32 [768, 3072], P('dp')
- upbias_grad: float32 [3072], P('dp')
- down_grad: float32 [3072, 768], P('dp')
- downbias_grad: float32 [768], P('dp')
- routedup_grad: float32 [4, 768, 3072], P('expert', 'dp')
- routedupbias_grad: float32 [4, 3072], P('expert', 'dp')
- routeddown_grad: float32 [4, 3072, 768], P('expert', 'dp')
- routeddownbias_grad: float32 [4, 768], P('expert', 'dp')
- expert_counts: int32 [4], replicated
Inputs may be any that keep to these rules, and one draw needn't show every extreme that they name: `routes`: each row names two different experts. `image_lengths`: in each row the first image_counts entries are 256 or 1024 and add up to 1024; the other entries are 0.
All inputs are finite; a program needn't handle non-finite values.
Results may differ from a plain program's by a relative error of at most 0.014.
The roundings to bfloat16 on the way count: a program that leaves them out, or rounds other values in their place, can miss the bound.
Values may be sent and summed in bfloat16 or wider, within the bound.
No kernel may reach another device: no remote copies, remote signals or barrier semaphores. Data moves between devices by JAX's collectives and lax.ppermute only.
A program may use at most 256 MiB of HBM per device.

v0:
```python
import jax
import jax.numpy as jnp
from jax import lax
from jax.sharding import PartitionSpec as P

HEADS = 12
HEAD_DIM = 64
CAP = 128


highest_precision = lax.Precision.HIGHEST
epsilon = 1e-06
gelu_root = 0.7978845608028654
gelu_cubic = 0.044715


def norm_parts(values):
    centered = values - jnp.mean(values, axis=-1, keepdims=True)
    inv_std = lax.rsqrt(jnp.mean(centered * centered, axis=-1, keepdims=True) + epsilon)
    return (centered * inv_std, inv_std)


def norm_back(grad_normed, normed, inv_std):
    mean_grad = jnp.mean(grad_normed, axis=-1, keepdims=True)
    mean_cross = jnp.mean(grad_normed * normed, axis=-1, keepdims=True)
    return inv_std * (grad_normed - mean_grad - normed * mean_cross)


def gelu_parts(values):
    inner_arg = gelu_root * (values + gelu_cubic * values * values * values)
    tangent = jnp.tanh(inner_arg)
    activation = 0.5 * values * (1.0 + tangent)
    slope = 0.5 * (1.0 + tangent) + 0.5 * values * (1.0 - tangent * tangent) * gelu_root * (
        1.0 + 3.0 * gelu_cubic * values * values
    )
    return (activation, slope)


def body(
    tokens,
    conditioning,
    routes,
    gate_weights,
    image_counts,
    image_lengths,
    cotangent,
    qkv_weight,
    qv_bias,
    proj_weight,
    proj_bias,
    ada_weight,
    ada_bias,
    up_weight,
    up_bias,
    down_weight,
    down_bias,
    routed_up,
    routed_upbias,
    routed_down,
    routed_downbias,
):
    group_size = lax.axis_size("expert")
    position = lax.axis_index("expert")
    token_rows = tokens.shape[0]
    model_width = tokens.shape[1]
    group_rows = group_size * token_rows
    score_scale = HEAD_DIM ** (-0.5)

    def gather_weights():
        return (
            lax.all_gather(qkv_weight, "dp", axis=0, tiled=True),
            lax.all_gather(qv_bias, "dp", axis=0, tiled=True),
            lax.all_gather(proj_weight, "dp", axis=0, tiled=True),
            lax.all_gather(proj_bias, "dp", axis=0, tiled=True),
            lax.all_gather(ada_weight, "dp", axis=0, tiled=True),
            lax.all_gather(ada_bias, "dp", axis=0, tiled=True),
            lax.all_gather(up_weight, "dp", axis=0, tiled=True),
            lax.all_gather(up_bias, "dp", axis=0, tiled=True),
            lax.all_gather(down_weight, "dp", axis=0, tiled=True),
            lax.all_gather(down_bias, "dp", axis=0, tiled=True),
            lax.all_gather(routed_up, "dp", axis=1, tiled=True),
            lax.all_gather(routed_upbias, "dp", axis=1, tiled=True),
            lax.all_gather(routed_down, "dp", axis=1, tiled=True),
            lax.all_gather(routed_downbias, "dp", axis=1, tiled=True),
        )

    gathered = gather_weights()
    (
        qkv_full,
        qvb_full,
        proj_full,
        projb_full,
        ada_full,
        adab_full,
        up_full,
        upb_full,
        down_full,
        downb_full,
        expert_up_complete,
        eupb_full,
        edown_full,
        edownb_full,
    ) = gathered
    experts_per_device = expert_up_complete.shape[0]
    experts_all = experts_per_device * group_size
    lengths = image_lengths[0]
    image_total = image_counts[0]
    slot_count = lengths.shape[0]
    starts = jnp.cumsum(lengths, dtype=jnp.int32) - lengths
    slot_ids = jnp.arange(slot_count, dtype=jnp.int32)
    live_slot = (slot_ids >= 1) & (slot_ids < image_total)
    all_places = jnp.arange(group_rows, dtype=jnp.int32)
    covered = live_slot[None, :] & (starts[None, :] <= all_places[:, None])
    segment_all = jnp.sum(covered.astype(jnp.int32), axis=1, dtype=jnp.int32)
    segment_own = lax.dynamic_slice_in_dim(segment_all, position * token_rows, token_rows)
    image_hot = (segment_own[:, None] == slot_ids[None, :]).astype(jnp.float32)
    same_image = segment_own[:, None] == segment_all[None, :]
    cond_value = conditioning[0].astype(jnp.float32)
    cond_act = jax.nn.silu(cond_value).astype(jnp.bfloat16)
    modulation = jnp.dot(cond_act, ada_full, preferred_element_type=jnp.float32) + adab_full.astype(
        jnp.float32
    )
    per_token = jnp.dot(
        image_hot, modulation, precision=highest_precision, preferred_element_type=jnp.float32
    )
    shift_a = per_token[:, 0:model_width]
    scale_a = per_token[:, model_width : 2 * model_width]
    gate_a = per_token[:, 2 * model_width : 3 * model_width]
    shift_b = per_token[:, 3 * model_width : 4 * model_width]
    scale_b = per_token[:, 4 * model_width : 5 * model_width]
    gate_b = per_token[:, 5 * model_width : 6 * model_width]
    residual = tokens.astype(jnp.float32)
    normed_a, inv_std_a = norm_parts(residual)
    hidden_a = (normed_a * (1.0 + scale_a) + shift_a).astype(jnp.bfloat16)
    bias_three = jnp.concatenate(
        [qvb_full[:model_width], jnp.zeros((model_width,), jnp.bfloat16), qvb_full[model_width:]]
    ).astype(jnp.float32)
    projected = (
        jnp.dot(hidden_a, qkv_full, preferred_element_type=jnp.float32) + bias_three
    ).astype(jnp.bfloat16)
    query_part = projected[:, 0:model_width]
    key_part = projected[:, model_width : 2 * model_width]
    value_part = projected[:, 2 * model_width : 3 * model_width]
    keys_full, values_full = (
        lax.all_gather(key_part, "expert", axis=0, tiled=True),
        lax.all_gather(value_part, "expert", axis=0, tiled=True),
    )
    query_heads = query_part.reshape(token_rows, HEADS, HEAD_DIM)
    key_heads = keys_full.reshape(group_rows, HEADS, HEAD_DIM)
    value_heads = values_full.reshape(group_rows, HEADS, HEAD_DIM)

    def attention_logits():
        scores = (
            jnp.einsum("qhd,khd->hqk", query_heads, key_heads, preferred_element_type=jnp.float32)
            * score_scale
        )
        return jnp.where(same_image[None, :, :], scores, -1e30)

    masked = attention_logits()
    row_top = jnp.max(masked, axis=-1, keepdims=True)
    exponent = jnp.exp(masked - row_top)
    row_total = jnp.sum(exponent, axis=-1, keepdims=True)
    probabilities = exponent / row_total
    logsum = row_top + jnp.log(row_total)
    attended = (
        jnp.einsum(
            "hqk,khd->qhd",
            probabilities.astype(jnp.bfloat16),
            value_heads,
            preferred_element_type=jnp.float32,
        )
        .reshape(token_rows, model_width)
        .astype(jnp.bfloat16)
    )
    attn_out = jnp.dot(attended, proj_full, preferred_element_type=jnp.float32) + projb_full.astype(
        jnp.float32
    )
    residual_mid = residual + gate_a * attn_out
    normed_b, inv_std_b = norm_parts(residual_mid)
    hidden_b = (normed_b * (1.0 + scale_b) + shift_b).astype(jnp.bfloat16)
    shared_pre = jnp.dot(hidden_b, up_full, preferred_element_type=jnp.float32) + upb_full.astype(
        jnp.float32
    )
    shared_act, shared_slope = gelu_parts(shared_pre)
    shared_hid = shared_act.astype(jnp.bfloat16)
    shared_out = jnp.dot(
        shared_hid, down_full, preferred_element_type=jnp.float32
    ) + downb_full.astype(jnp.float32)
    expert_ids = jnp.arange(experts_all, dtype=jnp.int32)
    choose = (routes[:, :, None] == expert_ids[None, None, :]).astype(jnp.float32)
    route_hot = jnp.sum(choose, axis=1)
    gate_hot = jnp.sum(choose * gate_weights[:, :, None], axis=1)
    row_ids = jnp.arange(token_rows, dtype=jnp.int32)
    earlier_rows = (row_ids[:, None] > row_ids[None, :]).astype(jnp.float32)
    slot_rank = jnp.dot(
        earlier_rows, route_hot, precision=highest_precision, preferred_element_type=jnp.float32
    )
    kept_pairs = route_hot * (slot_rank < CAP).astype(jnp.float32)
    capacity_ids = jnp.arange(CAP, dtype=jnp.int32).astype(jnp.float32)
    slot_table = kept_pairs.T[:, None, :] * (
        slot_rank.T[:, None, :] == capacity_ids[None, :, None]
    ).astype(jnp.float32)
    table_low = slot_table.astype(jnp.bfloat16)
    exchange_buffer = jnp.einsum(
        "ect,td->ecd", table_low, hidden_b, preferred_element_type=jnp.float32
    ).astype(jnp.bfloat16)
    exchange_buffer = exchange_buffer.reshape(group_size, experts_per_device, CAP, model_width)
    counts_local = jnp.sum(kept_pairs, axis=0).astype(jnp.int32)
    expert_counts = lax.psum(counts_local, ("dp", "expert"))
    received_rows = lax.all_to_all(
        exchange_buffer, "expert", split_axis=0, concat_axis=0, tiled=True
    )
    preactivation = jnp.einsum(
        "pmti,mil->pmtl", received_rows, expert_up_complete, preferred_element_type=jnp.float32
    )
    preactivation = preactivation + eupb_full.astype(jnp.float32)[None, :, None, :]
    activation, unused_slope = gelu_parts(preactivation)
    expert_made = jnp.einsum(
        "sknf,kfd->sknd",
        activation.astype(jnp.bfloat16),
        edown_full,
        preferred_element_type=jnp.float32,
    )
    expert_made = (expert_made + edownb_full.astype(jnp.float32)[None, :, None, :]).astype(
        jnp.bfloat16
    )
    returned = lax.all_to_all(expert_made, "expert", split_axis=0, concat_axis=0, tiled=True)
    selected = jnp.einsum(
        "ect,ecd->ted",
        table_low,
        returned.reshape(experts_all, CAP, model_width),
        preferred_element_type=jnp.float32,
    )
    routed = jnp.sum(gate_hot[:, :, None] * selected, axis=1)
    combined = shared_out + routed
    output = (residual_mid + gate_b * combined).astype(jnp.bfloat16)
    weights_for_backward = gather_weights()
    qkv_back = weights_for_backward[0]
    proj_back = weights_for_backward[2]
    ada_back = weights_for_backward[4]
    up_back = weights_for_backward[6]
    down_back = weights_for_backward[8]
    expert_up_returned = weights_for_backward[10]
    edown_back = weights_for_backward[12]
    upstream = cotangent.astype(jnp.float32)
    grad_gate_b = upstream * combined
    grad_comb = gate_b * upstream
    grad_comb_low = grad_comb.astype(jnp.bfloat16)
    down_grad = jnp.einsum(
        "tf,td->fd", shared_hid, grad_comb_low, preferred_element_type=jnp.float32
    )
    downbias_grad = jnp.sum(grad_comb_low.astype(jnp.float32), axis=0)
    grad_shared_hid = jnp.einsum(
        "td,fd->tf", grad_comb_low, down_back, preferred_element_type=jnp.float32
    )
    grad_shared_pre = (grad_shared_hid * shared_slope).astype(jnp.bfloat16)
    up_grad = jnp.einsum("td,tf->df", hidden_b, grad_shared_pre, preferred_element_type=jnp.float32)
    upbias_grad = jnp.sum(grad_shared_pre.astype(jnp.float32), axis=0)
    grad_hidden_b = jnp.einsum(
        "tf,df->td", grad_shared_pre, up_back, preferred_element_type=jnp.float32
    )
    pair_grads = gate_hot[:, :, None] * grad_comb[:, None, :]
    slot_grad = jnp.einsum(
        "ect,ted->ecd",
        slot_table,
        pair_grads,
        precision=highest_precision,
        preferred_element_type=jnp.float32,
    ).astype(jnp.bfloat16)
    slot_grad = slot_grad.reshape(group_size, experts_per_device, CAP, model_width)
    arrived = lax.all_to_all(slot_grad, "expert", split_axis=0, concat_axis=0, tiled=True)
    expert_act, expert_slope = gelu_parts(preactivation)
    routeddown_grad = jnp.einsum(
        "skcf,skcd->kfd",
        expert_act.astype(jnp.bfloat16),
        arrived,
        preferred_element_type=jnp.float32,
    )
    routeddownbias_grad = jnp.sum(arrived.astype(jnp.float32), axis=(0, 2))
    grad_expert_hid = jnp.einsum(
        "skcd,kfd->skcf", arrived, edown_back, preferred_element_type=jnp.float32
    )
    expert_preactivation_grad = (grad_expert_hid * expert_slope).astype(jnp.bfloat16)
    routedup_grad = jnp.einsum(
        "skcd,skcf->kdf",
        received_rows,
        expert_preactivation_grad,
        preferred_element_type=jnp.float32,
    )
    routedupbias_grad = jnp.sum(expert_preactivation_grad.astype(jnp.float32), axis=(0, 2))
    grad_buffer = jnp.einsum(
        "jrng,rzg->jrnz",
        expert_preactivation_grad,
        expert_up_returned,
        preferred_element_type=jnp.float32,
    ).astype(jnp.bfloat16)
    sent_back = lax.all_to_all(grad_buffer, "expert", split_axis=0, concat_axis=0, tiled=True)
    grad_hidden_b = grad_hidden_b + jnp.einsum(
        "ect,ecd->td",
        table_low,
        sent_back.reshape(experts_all, CAP, model_width),
        preferred_element_type=jnp.float32,
    )
    grad_scale_b = grad_hidden_b * normed_b
    grad_mid = upstream + norm_back(grad_hidden_b * (1.0 + scale_b), normed_b, inv_std_b)
    grad_gate_a = grad_mid * attn_out
    grad_attn = (gate_a * grad_mid).astype(jnp.bfloat16)
    proj_grad = jnp.einsum("td,te->de", attended, grad_attn, preferred_element_type=jnp.float32)
    projbias_grad = jnp.sum(grad_attn.astype(jnp.float32), axis=0)
    grad_attended = jnp.einsum(
        "te,de->td", grad_attn, proj_back, preferred_element_type=jnp.float32
    )
    grad_attended = grad_attended.astype(jnp.bfloat16).reshape(token_rows, HEADS, HEAD_DIM)
    again_logits = attention_logits()
    again_probs = jnp.exp(again_logits - logsum)
    grad_value_full = jnp.einsum(
        "hqk,qhd->khd",
        again_probs.astype(jnp.bfloat16),
        grad_attended,
        preferred_element_type=jnp.float32,
    )
    grad_probs = jnp.einsum(
        "qhd,khd->hqk", grad_attended, value_heads, preferred_element_type=jnp.float32
    )
    inner_sum = jnp.sum(again_probs * grad_probs, axis=-1, keepdims=True)
    grad_scores = (again_probs * (grad_probs - inner_sum)).astype(jnp.bfloat16)
    grad_query = (
        jnp.einsum("hqk,khd->qhd", grad_scores, key_heads, preferred_element_type=jnp.float32)
        * score_scale
    )
    grad_key_full = (
        jnp.einsum("hqk,qhd->khd", grad_scores, query_heads, preferred_element_type=jnp.float32)
        * score_scale
    )
    grad_key, grad_value = (
        lax.psum_scatter(
            grad_key_full.reshape(group_rows, model_width).astype(jnp.bfloat16),
            "expert",
            scatter_dimension=0,
            tiled=True,
        ).astype(jnp.float32),
        lax.psum_scatter(
            grad_value_full.reshape(group_rows, model_width).astype(jnp.bfloat16),
            "expert",
            scatter_dimension=0,
            tiled=True,
        ).astype(jnp.float32),
    )
    grad_projected = jnp.concatenate(
        [grad_query.reshape(token_rows, model_width), grad_key, grad_value], axis=1
    ).astype(jnp.bfloat16)
    qkv_grad = jnp.einsum("td,te->de", hidden_a, grad_projected, preferred_element_type=jnp.float32)
    bias_sums = jnp.sum(grad_projected.astype(jnp.float32), axis=0)
    qvbias_grad = jnp.concatenate(
        [bias_sums[0:model_width], bias_sums[2 * model_width : 3 * model_width]]
    )
    grad_hidden_a = jnp.einsum(
        "te,de->td", grad_projected, qkv_back, preferred_element_type=jnp.float32
    )
    grad_scale_a = grad_hidden_a * normed_a
    tokens_grad = grad_mid + norm_back(grad_hidden_a * (1.0 + scale_a), normed_a, inv_std_a)
    grad_per_token = jnp.concatenate(
        [grad_hidden_a, grad_scale_a, grad_gate_a, grad_hidden_b, grad_scale_b, grad_gate_b], axis=1
    )
    grad_mod_local = jnp.einsum(
        "ts,tm->sm",
        image_hot,
        grad_per_token,
        precision=highest_precision,
        preferred_element_type=jnp.float32,
    )
    grad_modulation = lax.psum(grad_mod_local.astype(jnp.bfloat16), "expert")
    first_only = (position == 0).astype(jnp.float32)
    ada_grad = (
        jnp.einsum("sd,sm->dm", cond_act, grad_modulation, preferred_element_type=jnp.float32)
        * first_only
    )
    adabias_grad = jnp.sum(grad_modulation.astype(jnp.float32), axis=0) * first_only
    grad_cond_act = jnp.einsum(
        "sm,dm->sd", grad_modulation, ada_back, preferred_element_type=jnp.float32
    )
    sigmoid_cond = jax.nn.sigmoid(cond_value)
    conditioning_grad = (grad_cond_act * sigmoid_cond * (1.0 + cond_value * (1.0 - sigmoid_cond)))[
        None
    ]
    summed = (
        lax.psum_scatter(qkv_grad, "dp", scatter_dimension=0, tiled=True),
        lax.psum_scatter(qvbias_grad, "dp", scatter_dimension=0, tiled=True),
        lax.psum_scatter(proj_grad, "dp", scatter_dimension=0, tiled=True),
        lax.psum_scatter(projbias_grad, "dp", scatter_dimension=0, tiled=True),
        lax.psum_scatter(ada_grad, "dp", scatter_dimension=0, tiled=True),
        lax.psum_scatter(adabias_grad, "dp", scatter_dimension=0, tiled=True),
        lax.psum_scatter(up_grad, "dp", scatter_dimension=0, tiled=True),
        lax.psum_scatter(upbias_grad, "dp", scatter_dimension=0, tiled=True),
        lax.psum_scatter(down_grad, "dp", scatter_dimension=0, tiled=True),
        lax.psum_scatter(downbias_grad, "dp", scatter_dimension=0, tiled=True),
        lax.psum_scatter(routedup_grad, "dp", scatter_dimension=1, tiled=True),
        lax.psum_scatter(routedupbias_grad, "dp", scatter_dimension=1, tiled=True),
        lax.psum_scatter(routeddown_grad, "dp", scatter_dimension=1, tiled=True),
        lax.psum_scatter(routeddownbias_grad, "dp", scatter_dimension=1, tiled=True),
    )
    dense_done = (
        lax.psum(summed[0].astype(jnp.bfloat16), "expert").astype(jnp.float32),
        lax.psum(summed[1].astype(jnp.bfloat16), "expert").astype(jnp.float32),
        lax.psum(summed[2].astype(jnp.bfloat16), "expert").astype(jnp.float32),
        lax.psum(summed[3].astype(jnp.bfloat16), "expert").astype(jnp.float32),
        lax.psum(summed[4].astype(jnp.bfloat16), "expert").astype(jnp.float32),
        lax.psum(summed[5].astype(jnp.bfloat16), "expert").astype(jnp.float32),
        lax.psum(summed[6].astype(jnp.bfloat16), "expert").astype(jnp.float32),
        lax.psum(summed[7].astype(jnp.bfloat16), "expert").astype(jnp.float32),
        lax.psum(summed[8].astype(jnp.bfloat16), "expert").astype(jnp.float32),
        lax.psum(summed[9].astype(jnp.bfloat16), "expert").astype(jnp.float32),
    )
    expert_done = (summed[10], summed[11], summed[12], summed[13])
    return (
        output,
        tokens_grad,
        conditioning_grad,
        dense_done[0],
        dense_done[1],
        dense_done[2],
        dense_done[3],
        dense_done[4],
        dense_done[5],
        dense_done[6],
        dense_done[7],
        dense_done[8],
        dense_done[9],
        expert_done[0],
        expert_done[1],
        expert_done[2],
        expert_done[3],
        expert_counts,
    )


def solution(mesh):
    in_specs = (
        P(("dp", "expert"), None),
        P("dp", None, None),
        P(("dp", "expert"), None),
        P(("dp", "expert"), None),
        P("dp"),
        P("dp", None),
        P(("dp", "expert"), None),
        P("dp", None),
        P("dp"),
        P("dp", None),
        P("dp"),
        P("dp", None),
        P("dp"),
        P("dp", None),
        P("dp"),
        P("dp", None),
        P("dp"),
        P("expert", "dp", None),
        P("expert", "dp"),
        P("expert", "dp", None),
        P("expert", "dp"),
    )
    out_specs = (
        P(("dp", "expert"), None),
        P(("dp", "expert"), None),
        P("dp", None, None),
        P("dp", None),
        P("dp"),
        P("dp", None),
        P("dp"),
        P("dp", None),
        P("dp"),
        P("dp", None),
        P("dp"),
        P("dp", None),
        P("dp"),
        P("expert", "dp", None),
        P("expert", "dp"),
        P("expert", "dp", None),
        P("expert", "dp"),
        P(),
    )
    return jax.shard_map(body, mesh=mesh, in_specs=in_specs, out_specs=out_specs, check_vma=False)
```

profile of v0, /device:TPU:0, one launch (start us, length us, event | category | flops | bytes accessed | tf_op | source)
XLA Modules:
  0.0 2030.5 jit_solution(6699863523650907279)
XLA Ops:
  17.7 40.0 %all-reduce.11 = (bf16[4608]{0:T(1024)(128)(2,1)S(1)}, bf16[1536]{0:T(1024)(128)(2,1)S(1)}, bf16[768]{0:T(1024)(128)(2,1)S(1)}, bf16[768]{0:T(1024)(128)(2,1)S(1)}, bf16[768]{0:T(1024)(128)(2,1)S(1)}) all-reduce(bf16[4608]{0:T(1024)(128)(2,1)S(1)} %dynamic-update-slice, ...), channel_id=1, replica_groups=mesh['dp'=8,'expert'=4] {'dp'}, use_global_device_ids=true, to_apply=%add | all-reduce | flops 8448 | bytes 33792
  61.2 61.2 %all-gather.11.cloned.1.call-done = bf16[768,4608]{1,0:T(8,128)(2,1)} async-done(((bf16[96,4608]{1,0:T(8,128)(2,1)}), bf16[768,4608]{1,0:T(8,128)(2,1)}) %all-gather.11.cloned.1.call-update) | async-done | bytes 7077904 | tf_op jit(solution)/shard_map/all_gather | solution.py:75
  130.9 57.0 %all-gather.13.cloned.1.call-done = bf16[768,2304]{1,0:T(8,128)(2,1)} async-done(((bf16[96,2304]{1,0:T(8,128)(2,1)}), bf16[768,2304]{1,0:T(8,128)(2,1)}) %all-gather.13.cloned.1.call-update) | async-done | bytes 3538960 | tf_op jit(solution)/shard_map/all_gather | solution.py:71
  197.2 25.9 %all-gather = bf16[8,1,384]{2,1,0:T(2,128)(2,1)S(1)} all-gather(bf16[1,1,384]{2,1,0:T(2,128)(2,1)S(1)} %reshape.269), channel_id=1, replica_groups=mesh['dp'=8,'expert'=4] {'dp'}, dimensions={0}, use_global_device_ids=true | all-gather | bytes 6912 | tf_op jit(solution)/shard_map/all_gather | solution.py:78
  223.7 26.3 %all_gather.68 = bf16[1,3072]{1,0:T(2,128)(2,1)S(1)} all-gather(bf16[1,384]{1,0:T(2,128)(2,1)S(1)} %copy-done.57), channel_id=1, replica_groups=mesh['dp'=8,'expert'=4] {'dp'}, dimensions={1}, use_global_device_ids=true | all-gather | bytes 6912 | tf_op jit(solution)/shard_map/all_gather | solution.py:82
  296.1 59.7 %all-gather.21.cloned.1.call-done = bf16[768,3072]{1,0:T(8,128)(2,1)} async-done(((bf16[96,3072]{1,0:T(8,128)(2,1)}), bf16[768,3072]{1,0:T(8,128)(2,1)}) %all-gather.21.cloned.1.call-update) | async-done | bytes 4718608 | tf_op jit(solution)/shard_map/all_gather | solution.py:77
  361.4 74.7 %all-gather.23.cloned.1.call-done = bf16[3072,768]{1,0:T(8,128)(2,1)} async-done(((bf16[384,768]{1,0:T(8,128)(2,1)}), bf16[3072,768]{1,0:T(8,128)(2,1)}) %all-gather.23.cloned.1.call-update) | async-done | bytes 4718608 | tf_op jit(solution)/shard_map/all_gather | solution.py:79
  448.3 68.0 %all-gather.25.cloned.1.call-done = bf16[1,768,3072]{2,1,0:T(8,128)(2,1)} async-done(((bf16[1,96,3072]{2,1,0:T(8,128)(2,1)}), bf16[1,768,3072]{2,1,0:T(8,128)(2,1)}) %all-gather.25.cloned.1.call-update) | async-done | bytes 4718608 | tf_op jit(solution)/shard_map/all_gather | solution.py:81
  524.1 72.5 %all-gather.27.cloned.1.call-done = bf16[1,3072,768]{2,1,0:T(8,128)(2,1)} async-done(((bf16[1,384,768]{2,1,0:T(8,128)(2,1)}), bf16[1,3072,768]{2,1,0:T(8,128)(2,1)}) %all-gather.27.cloned.1.call-update) | async-done | bytes 4718608 | tf_op jit(solution)/shard_map/all_gather | solution.py:83
  609.9 9.3 convert_reduce_fusion
  695.1 28.8 %reduce-scatter.16.cloned.1.call-done = bf16[256,768]{0,1:T(8,128)(2,1)} async-done(((bf16[1024,768]{0,1:T(8,128)(2,1)}), bf16[256,768]{0,1:T(8,128)(2,1)}) %reduce-scatter.16.cloned.1.call-update) | async-done | bytes 393232 | tf_op jit(solution)/shard_map/reduce_scatter | solution.py:336
  754.4 10.9 psum.84
  776.5 19.7 reduce-scatter.22.cloned.1.call-done
  797.8 130.1 %reduce-scatter.20.cloned.1.call-done = f32[96,2304]{1,0:T(8,128)} async-done(((f32[768,2304]{1,0:T(8,128)}), f32[96,2304]{1,0:T(8,128)}) %reduce-scatter.20.cloned.1.call-update) | async-done | bytes 884752 | tf_op jit(solution)/shard_map/reduce_scatter | solution.py:387
  930.0 164.3 %reduce-scatter.28.cloned.1.call-done = f32[384,768]{1,0:T(8,128)} async-done(((f32[3072,768]{1,0:T(8,128)}), f32[384,768]{1,0:T(8,128)}) %reduce-scatter.28.cloned.1.call-update) | async-done | bytes 1179664 | tf_op jit(solution)/shard_map/reduce_scatter | solution.py:395
  1096.4 164.2 %reduce-scatter.26.cloned.1.call-done = f32[96,3072]{1,0:T(8,128)} async-done(((f32[768,3072]{1,0:T(8,128)}), f32[96,3072]{1,0:T(8,128)}) %reduce-scatter.26.cloned.1.call-update) | async-done | bytes 1179664 | tf_op jit(solution)/shard_map/reduce_scatter | solution.py:393
  1262.7 230.1 %reduce-scatter.24.cloned.1.call-done = f32[96,4608]{1,0:T(8,128)} async-done(((f32[768,4608]{1,0:T(8,128)}), f32[96,4608]{1,0:T(8,128)}) %reduce-scatter.24.cloned.1.call-update) | async-done | bytes 1769488 | tf_op jit(solution)/shard_map/reduce_scatter | solution.py:391
  1495.3 10.3 convolution_bitcast_fusion
  1515.1 39.4 %psum.95 = s32[4]{0:T(128)} all-reduce(s32[4]{0:T(128)S(1)} %convert_element_type.317), channel_id=1, replica_groups=mesh['dp'=8,'expert'=4] {'dp','expert'}, use_global_device_ids=true, to_apply=%region_51.52 | all-reduce | flops 4 | bytes 32 | tf_op jit(solution)/shard_map/psum | solution.py:209
  1558.5 66.5 %reduce-scatter.34.cloned.1.call-done = f32[384,1]{1,0:T(8,128)} async-done(((f32[3072,1]{1,0:T(8,128)}), f32[384,1]{1,0:T(8,128)}) %reduce-scatter.34.cloned.1.call-update) | async-done | bytes 1552
  1627.1 35.5 %all-reduce.10 = (bf16[1536]{0:T(1024)(128)(2,1)S(1)}, bf16[768]{0:T(1024)(128)(2,1)S(1)}, bf16[4608]{0:T(1024)(128)(2,1)S(1)}, bf16[3072]{0:T(1024)(128)(2,1)S(1)}, bf16[768]{0:T(1024)(128)(2,1)S(1)}) all-reduce(f32[1536]{0:T(1024)S(1)} %pad_maximum_fusion.1, ...), channel_id=5, replica_groups=mesh['dp'=8,'expert'=4] {'dp'}, use_global_device_ids=true, to_apply=%region_22.23.clone | all-reduce | flops 10752 | bytes 64512
  1677.7 11.5 all-reduce.16.cloned.1.call-done
  1698.6 158.0 %reduce-scatter.32.cloned.1.call-done = f32[1,384,768]{2,1,0:T(8,128)} async-done(((f32[1,3072,768]{2,1,0:T(8,128)}), f32[1,384,768]{2,1,0:T(8,128)}) %reduce-scatter.32.cloned.1.call-update) | async-done | bytes 1179664 | tf_op jit(solution)/shard_map/reduce_scatter | solution.py:399
  1856.6 166.8 %reduce-scatter.30.cloned.1.call-done = f32[1,96,3072]{2,1,0:T(8,128)} async-done(((f32[1,768,3072]{2,1,0:T(8,128)}), f32[1,96,3072]{2,1,0:T(8,128)}) %reduce-scatter.30.cloned.1.call-update) | async-done | bytes 1179664 | tf_op jit(solution)/shard_map/reduce_scatter | solution.py:397
  (294 shorter events, 279.0 us)
Async XLA Ops:
  7.2 115.1 %all-gather.11.cloned.1.call-start = ((), (), s32[]{:S(2)}) async-start(), calls=%async_computation.15 | async-start | bytes 7962624 | tf_op jit(solution)/shard_map/all_gather | solution.py:75
  7.9 180.0 %all-gather.13.cloned.1.call-start = ((), (), s32[]{:S(2)}) async-start(), calls=%async_computation.16 | async-start | bytes 3981312 | tf_op jit(solution)/shard_map/all_gather | solution.py:71
  8.7 242.7 %all-gather.17.cloned.1.call-start = ((), (), s32[]{:S(2)}) async-start(), calls=%async_computation.18 | async-start | bytes 1966080 | tf_op jit(solution)/shard_map/all_gather | solution.py:145
  192.0 61.2 %all-gather.15.cloned.1.call-start = ((), (), s32[]{:S(2)}) async-start(), calls=%async_computation.17 | async-start | bytes 1966080 | tf_op jit(solution)/shard_map/all_gather | solution.py:146
  192.6 82.5 %all-gather.19.cloned.1.call-start = ((), (), s32[]{:S(2)}) async-start(), calls=%async_computation.19 | async-start | bytes 1327104 | tf_op jit(solution)/shard_map/all_gather | solution.py:73
  193.2 162.7 %all-gather.21.cloned.1.call-start = ((), (), s32[]{:S(2)}) async-start(), calls=%async_computation.20 | async-start | bytes 5308416 | tf_op jit(solution)/shard_map/all_gather | solution.py:77
  193.7 242.3 %all-gather.23.cloned.1.call-start = ((), (), s32[]{:S(2)}) async-start(), calls=%async_computation.21 | async-start | bytes 5308416 | tf_op jit(solution)/shard_map/all_gather | solution.py:79
  194.5 321.8 %all-gather.25.cloned.1.call-start = ((), (), s32[]{:S(2)}) async-start(), calls=%async_computation.22 | async-start | bytes 5308416 | tf_op jit(solution)/shard_map/all_gather | solution.py:81
  195.2 401.3 %all-gather.27.cloned.1.call-start = ((), (), s32[]{:S(2)}) async-start(), calls=%async_computation.23 | async-start | bytes 5308416 | tf_op jit(solution)/shard_map/all_gather | solution.py:83
  285.3 158.8 %all-to-all-start = ((bf16[4,1,128,768]{3,2,1,0:T(8,128)(2,1)}), bf16[4,1,128,768]{3,2,1,0:T(8,128)(2,1)}, u32[]{:S(2)}, u32[]{:S(2)}) async-start(bf16[4,1,128,768]{3,2,1,0:T(8,128)(2,1)} %fusion.67), calls=%async_computation | async-start | bytes 1572864 | tf_op jit(solution)/shard_map/all_to_all | solution.py:210
  444.1 161.5 %all-to-all-start.2 = ((bf16[4,1,128,768]{3,2,1,0:T(8,128)(2,1)}), bf16[4,1,128,768]{3,2,1,0:T(8,128)(2,1)}, u32[]{:S(2)}, u32[]{:S(2)}) async-start(bf16[4,1,128,768]{3,2,1,0:T(8,128)(2,1)} %fusion.59), calls=%async_computation.2 | async-start | bytes 1572864 | tf_op jit(solution)/shard_map/all_to_all | solution.py:271
  605.5 21.3 %all-to-all-start.1 = ((bf16[4,1,128,768]{3,2,1,0:T(8,128)(2,1)}), bf16[4,1,128,768]{3,2,1,0:T(8,128)(2,1)}, u32[]{:S(2)}, u32[]{:S(2)}) async-start(bf16[4,1,128,768]{3,2,1,0:T(8,128)(2,1)} %fusion.62), calls=%async_computation.1 | async-start | bytes 1572864 | tf_op jit(solution)/shard_map/all_to_all | solution.py:227
  631.1 64.0 %reduce-scatter.18.cloned.1.call-start = ((), (), s32[]{:S(2)}) async-start(), calls=%async_computation.25 | async-start | bytes 1966080 | tf_op jit(solution)/shard_map/reduce_scatter | solution.py:342
  666.7 57.2 %reduce-scatter.16.cloned.1.call-start = ((), (), s32[]{:S(2)}) async-start(), calls=%async_computation.24 | async-start | bytes 1966080 | tf_op jit(solution)/shard_map/reduce_scatter | solution.py:336
  686.4 109.8 %reduce-scatter.22.cloned.1.call-start = ((), (), s32[]{:S(2)}) async-start(), calls=%async_computation.27 | async-start | bytes 2654208 | tf_op jit(solution)/shard_map/reduce_scatter | solution.py:389
  689.4 238.5 %reduce-scatter.20.cloned.1.call-start = ((), (), s32[]{:S(2)}) async-start(), calls=%async_computation.26 | async-start | bytes 7962624 | tf_op jit(solution)/shard_map/reduce_scatter | solution.py:387
  729.3 364.9 %reduce-scatter.28.cloned.1.call-start = ((), (), s32[]{:S(2)}) async-start(), calls=%async_computation.30 | async-start | bytes 10616832 | tf_op jit(solution)/shard_map/reduce_scatter | solution.py:395
  737.1 523.4 %reduce-scatter.26.cloned.1.call-start = ((), (), s32[]{:S(2)}) async-start(), calls=%async_computation.29 | async-start | bytes 10616832 | tf_op jit(solution)/shard_map/reduce_scatter | solution.py:393
  744.5 748.3 %reduce-scatter.24.cloned.1.call-start = ((), (), s32[]{:S(2)}) async-start(), calls=%async_computation.28 | async-start | bytes 15925248 | tf_op jit(solution)/shard_map/reduce_scatter | solution.py:391
  772.4 784.7 %reduce-scatter.36.cloned.1.call-start = ((), (), s32[]{:S(2)}) async-start(), calls=%async_computation.34 | async-start | bytes 442368
  774.7 850.3 %reduce-scatter.34.cloned.1.call-start = ((), (), s32[]{:S(2)}) async-start(), calls=%async_computation.33 | async-start | bytes 1769472
  776.4 912.8 %all-reduce.16.cloned.1.call-start = ((), (), s32[]{:S(2)}) async-start(), calls=%async_computation.35 | async-start | bytes 5308416 | tf_op jit(solution)/shard_map/psum | solution.py:403
  1495.3 361.4 %reduce-scatter.32.cloned.1.call-start = ((), (), s32[]{:S(2)}) async-start(), calls=%async_computation.32 | async-start | bytes 10616832 | tf_op jit(solution)/shard_map/reduce_scatter | solution.py:399
  1505.7 517.8 %reduce-scatter.30.cloned.1.call-start = ((), (), s32[]{:S(2)}) async-start(), calls=%async_computation.31 | async-start | bytes 10616832 | tf_op jit(solution)/shard_map/reduce_scatter | solution.py:397
  (60 other events, 2110.8 us)
Sparse Core Ops, SparseCore 0:
  10.2 112.0 all-gather.10
  124.5 63.3 all-gather.12
  192.1 18.1 all-gather.16
  212.3 19.6 all-gather.14
  234.0 41.0 all-gather.18
  277.1 78.6 all-gather.20
  358.0 78.0 all-gather.22
  438.2 78.0 all-gather.24
  518.5 78.0 all-gather.26
  666.8 25.5 reduce-scatter.17
  695.6 28.1 reduce-scatter.15
  727.2 68.9 reduce-scatter.21
  799.8 128.0 reduce-scatter.19
  931.8 162.3 reduce-scatter.27
  1098.1 162.3 reduce-scatter.25
  1264.5 228.2 reduce-scatter.23
  1496.2 60.5 reduce-scatter.35
  1561.0 63.9 reduce-scatter.33
  1628.9 60.3 all-reduce.15
  1693.3 163.3 reduce-scatter.31
  1860.8 162.5 reduce-scatter.29
where the time goes:
time: 2040 us; the launch traced here: 2030 us
  waiting for transfers between devices  1550 us (76%)
  blocking collectives  184 us (9%)
  matrix products  178 us (9%)
  other arithmetic  49.2 us (2%)
  local copies, waits for them, and re-layouts  31.1 us (2%)
  between operations  20.7 us (1%)
    reduce_scatter x1, waiting for transfers between devices, body(): lax.psum_scatter(ada_grad, 'dp', scatter_dimension=0, tiled=True)  230 us
    reduce_scatter x1, waiting for transfers between devices, body(): lax.psum_scatter(routedup_grad, 'dp', scatter_dimension=1, tiled=True)  167 us
    reduce_scatter x1, waiting for transfers between devices, body(): lax.psum_scatter(down_grad, 'dp', scatter_dimension=0, tiled=True)  164 us
    reduce_scatter x1, waiting for transfers between devices, body(): lax.psum_scatter(up_grad, 'dp', scatter_dimension=0, tiled=True)  164 us
    reduce_scatter x1, waiting for transfers between devices, body(): lax.psum_scatter(routeddown_grad, 'dp', scatter_dimension=1, tiled=True)  158 us
    reduce_scatter x1, waiting for transfers between devices, body(): lax.psum_scatter(qkv_grad, 'dp', scatter_dimension=0, tiled=True)  130 us
    unnamed x2, blocking collectives  75.6 us
    all_gather x1, waiting for transfers between devices, gather_weights(): lax.all_gather(down_weight, 'dp', axis=0, tiled=True)  74.7 us
  transfers between devices with their start and end apart: 25, of which 18 were waited for; matrix products, arithmetic and copies ran while one was open for 11% of the time, Pallas kernels for 0%

commit v1 on v0

v1 whole, which is shorter than its diff:
```python
import jax
import jax.numpy as jnp
from jax import lax
from jax.sharding import PartitionSpec as P

HEADS = 12
HEAD_DIM = 64
CAP = 128

epsilon = 1e-06
gelu_root = 0.7978845608028654
gelu_cubic = 0.044715

bf16 = jnp.bfloat16
f32 = jnp.float32


def norm_parts(values):
    centered = values - jnp.mean(values, axis=-1, keepdims=True)
    inv_std = lax.rsqrt(jnp.mean(centered * centered, axis=-1, keepdims=True) + epsilon)
    return (centered * inv_std, inv_std)


def norm_back(grad_normed, normed, inv_std):
    mean_grad = jnp.mean(grad_normed, axis=-1, keepdims=True)
    mean_cross = jnp.mean(grad_normed * normed, axis=-1, keepdims=True)
    return inv_std * (grad_normed - mean_grad - normed * mean_cross)


def gelu_parts(values):
    inner_arg = gelu_root * (values + gelu_cubic * values * values * values)
    tangent = jnp.tanh(inner_arg)
    activation = 0.5 * values * (1.0 + tangent)
    slope = 0.5 * (1.0 + tangent) + 0.5 * values * (1.0 - tangent * tangent) * gelu_root * (
        1.0 + 3.0 * gelu_cubic * values * values
    )
    return (activation, slope)


def mm(spec, a, b):
    return jnp.einsum(spec, a, b, preferred_element_type=f32)


def swap(value, mask):
    size = lax.axis_size("expert")
    return lax.ppermute(value, "expert", [(i, i ^ mask) for i in range(size)])


def gather_group(value):
    across = swap(value, 2)
    beside = swap(jnp.stack([value, across]), 1)
    return jnp.stack([value, beside[0], across, beside[1]])


def reduce_group(parts):
    beside = swap(jnp.stack([parts[1], parts[3]]).astype(bf16), 1).astype(f32)
    own = parts[0] + beside[0]
    other = (parts[2] + beside[1]).astype(bf16)
    return own + swap(other, 2).astype(f32)


def in_order(relative, position):
    return jnp.stack(
        [
            lax.dynamic_index_in_dim(relative, position ^ a, 0, keepdims=False)
            for a in range(relative.shape[0])
        ]
    )


def body(
    tokens,
    conditioning,
    routes,
    gate_weights,
    image_counts,
    image_lengths,
    cotangent,
    qkv_weight,
    qv_bias,
    proj_weight,
    proj_bias,
    ada_weight,
    ada_bias,
    up_weight,
    up_bias,
    down_weight,
    down_bias,
    routed_up,
    routed_upbias,
    routed_down,
    routed_downbias,
):
    group = lax.axis_size("expert")
    copies = lax.axis_size("dp")
    position = lax.axis_index("expert")
    place = lax.axis_index("dp")
    rows, width = tokens.shape
    group_rows = group * rows
    score_scale = HEAD_DIM ** (-0.5)
    heads_own = HEADS // group
    cols_own = heads_own * HEAD_DIM
    d_rows = qkv_weight.shape[0]
    f_rows = down_weight.shape[0]
    f_own = f_rows // group
    hidden_units = f_rows * copies
    quarter = hidden_units // group
    chunks = hidden_units // width

    qkv_share = lax.dynamic_index_in_dim(
        qkv_weight.reshape(d_rows, 3, group, cols_own), position, 2, keepdims=False
    ).reshape(d_rows, 3 * cols_own)
    first_share = jnp.concatenate([proj_weight, qkv_share], axis=1)
    wide = first_share.shape[1]
    bias_list = [qv_bias, proj_bias, up_bias, down_bias, routed_upbias[0], routed_downbias[0]]
    bias_sizes = [b.shape[0] for b in bias_list]
    bias_flat = jnp.concatenate(bias_list)
    bias_rows = 16
    bias_flat = jnp.pad(bias_flat, (0, bias_rows * wide - bias_flat.shape[0])).reshape(
        bias_rows, wide
    )
    first_all = lax.all_gather(jnp.concatenate([first_share, bias_flat]), "dp", axis=0)
    proj_full = first_all[:, :d_rows, :width].reshape(width, width)
    qkv_own = first_all[:, :d_rows, width:].reshape(width, 3 * cols_own)
    bias_all = first_all[:, d_rows:, :].reshape(copies, bias_rows * wide)
    offsets = [sum(bias_sizes[:i]) for i in range(len(bias_sizes))]
    qvb, projb, upb, downb, rupb, rdownb = (
        bias_all[:, o : o + n].reshape(copies * n).astype(f32)
        for o, n in zip(offsets, bias_sizes)
    )

    up_share = lax.dynamic_index_in_dim(
        up_weight.reshape(d_rows, copies, group, f_own), position, 2, keepdims=False
    ).reshape(d_rows, quarter)
    down_share = lax.dynamic_slice_in_dim(down_weight, position * f_own, f_own, axis=0)
    rup_share = [routed_up[0, :, c * width : (c + 1) * width] for c in range(chunks)]
    second_share = jnp.concatenate([*rup_share, up_share, routed_down[0], down_share], axis=0)
    second_all = lax.all_gather(second_share, "dp", axis=0)

    def piece(at, count):
        return second_all[:, at : at + count, :].reshape(copies * count, width)

    rup = jnp.concatenate([piece(c * d_rows, d_rows) for c in range(chunks)], axis=1)
    up_own = piece(chunks * d_rows, d_rows)
    rdown = piece((chunks + 1) * d_rows, f_rows)
    down_own = piece((chunks + 1) * d_rows + f_rows, f_own)

    both = gather_group(jnp.concatenate([tokens, cotangent], axis=1))
    residual = both[:, :, :width].astype(f32)
    upstream = both[:, :, width:].astype(f32)
    pairs = gather_group(jnp.concatenate([routes.astype(f32).T, gate_weights.T], axis=0))

    lengths = image_lengths[0]
    image_total = image_counts[0]
    slots = lengths.shape[0]
    slot_ids = jnp.arange(slots, dtype=jnp.int32)
    starts = jnp.sum(
        jnp.where(slot_ids[None, :] < slot_ids[:, None], lengths[None, :], 0), axis=1
    )
    live = (slot_ids >= 1) & (slot_ids < image_total)
    block_ids = position ^ jnp.arange(group, dtype=jnp.int32)
    segment = jnp.sum(
        (live[None, :] & (starts[None, :] <= (block_ids * rows)[:, None])).astype(jnp.int32),
        axis=1,
    )
    block_hot = segment[:, None] == slot_ids[None, :]

    chosen = (pairs[:, 0:2, :] == position.astype(f32)).astype(f32)
    hot = chosen[:, 0] + chosen[:, 1]
    gate_own = chosen[:, 0] * pairs[:, 2] + chosen[:, 1] * pairs[:, 3]
    row_ids = jnp.arange(rows, dtype=jnp.int32)
    earlier = (row_ids[:, None] < row_ids[None, :]).astype(bf16)
    rank = mm("bu,ut->bt", hot.astype(bf16), earlier)
    kept = hot * (rank < CAP).astype(f32)
    cap_ids = jnp.arange(CAP, dtype=jnp.int32).astype(f32)
    table = (kept[:, None, :] * (rank[:, None, :] == cap_ids[None, :, None]).astype(f32)).astype(
        bf16
    )
    count_own = jnp.sum(kept)

    cond_value = conditioning[0].astype(f32)
    cond_act = jax.nn.silu(cond_value).astype(bf16)
    act_parts = lax.all_to_all(
        cond_act.reshape(slots, copies, d_rows).transpose(1, 0, 2),
        "dp",
        split_axis=0,
        concat_axis=0,
        tiled=True,
    ).reshape(copies * slots, d_rows)
    mod_width = ada_weight.shape[1]
    bias_line = lax.dynamic_update_slice(
        jnp.zeros((mod_width,), f32), ada_bias.astype(f32), (place * ada_bias.shape[0],)
    )
    mod_parts = mm("sd,dm->sm", act_parts, ada_weight) + bias_line[None, :]
    mod_parts = jnp.concatenate(
        [mod_parts, jnp.full((copies * slots, 128), count_own, f32)], axis=1
    ).reshape(copies, slots, mod_width + 128)
    mod_sum = jnp.sum(
        lax.all_to_all(mod_parts, "dp", split_axis=0, concat_axis=0, tiled=True), axis=0
    )
    modulation = mod_sum[:, :mod_width]
    expert_total = mod_sum[0, mod_width:]
    per_block = jnp.sum(
        jnp.where(block_hot[:, :, None], modulation[None, :, :], 0.0), axis=1
    )
    shift_a, scale_a, gate_a, shift_b, scale_b, gate_b = (
        per_block[:, None, i * width : (i + 1) * width] for i in range(6)
    )

    normed_a, inv_std_a = norm_parts(residual)
    hidden_a = (normed_a * (1.0 + scale_a) + shift_a).astype(bf16).reshape(group_rows, width)
    q_bias = lax.dynamic_slice_in_dim(qvb, position * cols_own, cols_own)
    v_bias = lax.dynamic_slice_in_dim(qvb, width + position * cols_own, cols_own)
    bias_three = jnp.concatenate([q_bias, jnp.zeros((cols_own,), f32), v_bias])
    projected = (mm("td,de->te", hidden_a, qkv_own) + bias_three).astype(bf16)
    query, key, value = (
        projected[:, i * cols_own : (i + 1) * cols_own].reshape(group_rows, heads_own, HEAD_DIM)
        for i in range(3)
    )
    segment_rows = jnp.repeat(segment, rows)
    same_image = segment_rows[:, None] == segment_rows[None, :]
    scores = mm("qhd,khd->hqk", query, key) * score_scale
    masked = jnp.where(same_image[None], scores, -1e30)
    row_top = jnp.max(masked, axis=-1, keepdims=True)
    exponent = jnp.exp(masked - row_top)
    row_total = jnp.sum(exponent, axis=-1, keepdims=True)
    logsum = row_top + jnp.log(row_total)
    attended_own = (
        mm("hqk,khd->qhd", (exponent / row_total).astype(bf16), value)
        .reshape(group, rows, cols_own)
        .astype(bf16)
    )
    heads_all = gather_group(attended_own)
    attended = jnp.concatenate(
        [
            jnp.concatenate([heads_all[k, m ^ k] for k in range(group)], axis=1)
            for m in range(group)
        ],
        axis=0,
    )
    proj_rel = in_order(proj_full.reshape(group, cols_own, width), position)
    attn_out = mm("td,de->te", attended, proj_rel.reshape(width, width)) + projb
    attn_out = attn_out.reshape(group, rows, width)
    residual_mid = residual + gate_a * attn_out
    normed_b, inv_std_b = norm_parts(residual_mid)
    hidden_b3 = (normed_b * (1.0 + scale_b) + shift_b).astype(bf16)
    hidden_b = hidden_b3.reshape(group_rows, width)

    upb_own = lax.dynamic_index_in_dim(
        upb.reshape(copies, group, f_own), position, 1, keepdims=False
    ).reshape(quarter)
    shared_pre = mm("td,df->tf", hidden_b, up_own) + upb_own
    shared_act, shared_slope = gelu_parts(shared_pre)
    shared_hid = shared_act.astype(bf16)
    buffer = mm("bct,btd->bcd", table, hidden_b3).astype(bf16).reshape(group * CAP, width)
    expert_pre = mm("sd,df->sf", buffer, rup) + rupb
    expert_act, expert_slope = gelu_parts(expert_pre)
    expert_hid = expert_act.astype(bf16)

    grad_comb = gate_b * upstream
    grad_comb_low = grad_comb.astype(bf16).reshape(group_rows, width)
    pair_grad = (gate_own[:, :, None] * grad_comb).astype(bf16)
    slot_grad = mm("bct,btd->bcd", table, pair_grad).astype(bf16).reshape(group * CAP, width)

    def scatter(value):
        return lax.psum_scatter(value, "dp", scatter_dimension=0, tiled=False)

    rdown_grad = mm("sf,sd->fd", expert_hid, slot_grad).astype(bf16)
    down_grad = mm("tf,td->fd", shared_hid, grad_comb_low).astype(bf16)
    sums_one = scatter(
        jnp.concatenate(
            [
                rdown_grad.reshape(copies, f_rows, width),
                down_grad.reshape(copies, f_own, width),
            ],
            axis=1,
        )
    )

    grad_shared_hid = mm("td,fd->tf", grad_comb_low, down_own)
    grad_shared_pre = (grad_shared_hid * shared_slope).astype(bf16)
    grad_expert_hid = mm("sd,fd->sf", slot_grad, rdown)
    grad_expert_pre = (grad_expert_hid * expert_slope).astype(bf16)
    rup_grad = mm("sd,sf->df", buffer, grad_expert_pre).astype(bf16)
    up_grad = mm("td,tf->df", hidden_b, grad_shared_pre).astype(bf16)
    bias_row = jnp.concatenate(
        [
            jnp.sum(grad_expert_pre.astype(f32), axis=0).reshape(copies, f_rows),
            jnp.sum(grad_shared_pre.astype(f32), axis=0).reshape(copies, f_own),
            jnp.sum(slot_grad.astype(f32), axis=0).reshape(copies, d_rows),
            jnp.sum(grad_comb_low.astype(f32), axis=0).reshape(copies, d_rows),
        ],
        axis=1,
    ).astype(bf16)
    bias_used = bias_row.shape[1]
    bias_row = jnp.pad(bias_row, ((0, 0), (0, width - bias_used)))[:, None, :]
    bias_row = jnp.pad(bias_row, ((0, 0), (0, 15), (0, 0)))
    sums_two = scatter(
        jnp.concatenate(
            [
                *(
                    rup_grad[:, c * width : (c + 1) * width].reshape(copies, d_rows, width)
                    for c in range(chunks)
                ),
                up_grad.reshape(copies, d_rows, quarter),
                bias_row,
            ],
            axis=1,
        )
    )

    grad_buffer = mm("sf,df->sd", grad_expert_pre, rup).astype(bf16).reshape(group, CAP, width)
    hidden_parts = mm("tf,df->td", grad_shared_pre, up_own).reshape(group, rows, width) + mm(
        "bct,bcd->btd", table, grad_buffer
    )
    grad_hidden_b = reduce_group(hidden_parts)

    expert_out = (mm("sf,fd->sd", expert_hid, rdown) + rdownb).astype(bf16)
    routed_parts = gate_own[:, :, None] * mm(
        "bct,bcd->btd", table, expert_out.reshape(group, CAP, width)
    )
    shared_parts = mm("tf,fd->td", shared_hid, down_own).reshape(group, rows, width)
    combined = reduce_group(shared_parts + routed_parts) + downb
    output = (residual_mid[0] + gate_b[0] * combined).astype(bf16)

    grad_gate_b = upstream[0] * combined
    grad_scale_b = grad_hidden_b * normed_b[0]
    grad_mid = upstream[0] + norm_back(
        grad_hidden_b * (1.0 + scale_b[0]), normed_b[0], inv_std_b[0]
    )
    grad_gate_a = grad_mid * attn_out[0]
    grad_attn_own = (gate_a[0] * grad_mid).astype(bf16)
    grad_attn = gather_group(grad_attn_own).reshape(group_rows, width)

    grad_attn_cols = lax.dynamic_slice_in_dim(grad_attn, position * cols_own, cols_own, axis=1)
    proj_grad = in_order(
        mm("td,te->de", attended, grad_attn_cols).reshape(group, cols_own, cols_own), position
    ).reshape(copies, d_rows, cols_own)
    grad_attended = (
        mm("te,de->td", grad_attn, proj_rel[0]).astype(bf16).reshape(group_rows, heads_own, HEAD_DIM)
    )
    again = jnp.where(same_image[None], mm("qhd,khd->hqk", query, key) * score_scale, -1e30)
    again_probs = jnp.exp(again - logsum)
    grad_value = mm("hqk,qhd->khd", again_probs.astype(bf16), grad_attended)
    grad_probs = mm("qhd,khd->hqk", grad_attended, value)
    inner_sum = jnp.sum(again_probs * grad_probs, axis=-1, keepdims=True)
    grad_scores = (again_probs * (grad_probs - inner_sum)).astype(bf16)
    grad_query = mm("hqk,khd->qhd", grad_scores, key) * score_scale
    grad_key = mm("hqk,qhd->khd", grad_scores, query) * score_scale
    grad_projected = jnp.concatenate(
        [g.reshape(group_rows, cols_own) for g in (grad_query, grad_key, grad_value)], axis=1
    ).astype(bf16)
    qkv_grad = mm("td,te->de", hidden_a, grad_projected)
    sums_qkv = jnp.sum(grad_projected.astype(f32), axis=0)
    qv_line = lax.dynamic_update_slice(
        jnp.zeros((2 * width,), f32), sums_qkv[:cols_own], (position * cols_own,)
    )
    qv_line = lax.dynamic_update_slice(
        qv_line, sums_qkv[2 * cols_own :], (width + position * cols_own,)
    ).reshape(copies, -1)
    pb_line = jnp.sum(grad_attn.astype(f32), axis=0).reshape(copies, d_rows)
    tail_width = 4 * cols_own
    small_row = jnp.concatenate([qv_line, pb_line], axis=1)
    small_row = jnp.pad(small_row, ((0, 0), (0, tail_width - small_row.shape[1])))[:, None, :]
    small_row = jnp.pad(small_row, ((0, 0), (0, 15), (0, 0)))
    sums_three = scatter(
        jnp.concatenate(
            [
                jnp.concatenate([qkv_grad.reshape(copies, d_rows, 3 * cols_own), proj_grad], axis=2),
                small_row,
            ],
            axis=1,
        ).astype(bf16)
    )

    grad_hidden_a = reduce_group(
        mm("te,de->td", grad_projected, qkv_own).reshape(group, rows, width)
    )
    grad_scale_a = grad_hidden_a * normed_a[0]
    tokens_grad = grad_mid + norm_back(
        grad_hidden_a * (1.0 + scale_a[0]), normed_a[0], inv_std_a[0]
    )

    block_sums = jnp.concatenate(
        [
            jnp.sum(g, axis=0)
            for g in (
                grad_hidden_a,
                grad_scale_a,
                grad_gate_a,
                grad_hidden_b,
                grad_scale_b,
                grad_gate_b,
            )
        ]
        + [expert_total]
    )
    group_sums = gather_group(block_sums[None])[:, 0]
    grad_modulation = jnp.sum(
        jnp.where(block_hot[:, :, None], group_sums[:, None, :mod_width], 0.0), axis=0
    ).astype(bf16)
    counts_rel = group_sums[:, mod_width]
    expert_counts = in_order(counts_rel, position).astype(jnp.int32)
    mod_all = lax.all_to_all(
        jnp.broadcast_to(grad_modulation[None], (copies, slots, mod_width)),
        "dp",
        split_axis=0,
        concat_axis=0,
        tiled=True,
    ).reshape(copies * slots, mod_width)
    ada_grad = mm("sd,sm->dm", act_parts, mod_all)
    adabias_grad = jnp.sum(
        lax.dynamic_slice_in_dim(
            mod_all, place * ada_bias.shape[0], ada_bias.shape[0], axis=1
        ).astype(f32),
        axis=0,
    )
    cond_parts = mm("sm,dm->sd", mod_all, ada_weight).reshape(copies, slots, d_rows)
    grad_cond_act = (
        lax.all_to_all(cond_parts, "dp", split_axis=0, concat_axis=0, tiled=True)
        .transpose(1, 0, 2)
        .reshape(slots, width)
    )
    sigmoid_cond = jax.nn.sigmoid(cond_value)
    conditioning_grad = (grad_cond_act * sigmoid_cond * (1.0 + cond_value * (1.0 - sigmoid_cond)))[
        None
    ]

    down_rows = in_order(gather_group(sums_one[f_rows:]), position).reshape(f_rows, width)
    up_and_bias = in_order(gather_group(sums_two[chunks * d_rows :]), position)
    up_rows = (
        up_and_bias[:, :d_rows]
        .reshape(group, d_rows, copies, f_own)
        .transpose(1, 2, 0, 3)
        .reshape(d_rows, hidden_units)
    )
    upbias_rows = up_and_bias[:, d_rows, f_rows : f_rows + f_own].reshape(f_rows)
    line = sums_two[(chunks + 1) * d_rows].astype(f32)
    rupbias_row = line[:f_rows]
    rdownbias_row = line[f_rows + f_own : f_rows + f_own + d_rows]
    downbias_row = line[f_rows + f_own + d_rows : f_rows + f_own + 2 * d_rows]
    rup_rows = jnp.concatenate(
        [sums_two[c * d_rows : (c + 1) * d_rows] for c in range(chunks)], axis=1
    )
    last = in_order(gather_group(sums_three), position)
    qkv_rows = (
        last[:, :d_rows, : 3 * cols_own]
        .reshape(group, d_rows, 3, cols_own)
        .transpose(1, 2, 0, 3)
        .reshape(d_rows, 3 * width)
    )
    proj_rows = last[:, :d_rows, 3 * cols_own :].transpose(1, 0, 2).reshape(d_rows, width)
    qv_count = 2 * width // copies
    qvbias_rows = jnp.sum(last[:, d_rows, :qv_count].astype(f32), axis=0)
    projbias_rows = last[0, d_rows, qv_count : qv_count + d_rows]

    return (
        output,
        tokens_grad,
        conditioning_grad,
        qkv_rows.astype(f32),
        qvbias_rows,
        proj_rows.astype(f32),
        projbias_rows.astype(f32),
        ada_grad,
        adabias_grad,
        up_rows.astype(f32),
        upbias_rows.astype(f32),
        down_rows.astype(f32),
        downbias_row,
        rup_rows.astype(f32)[None],
        rupbias_row[None],
        sums_one[:f_rows].astype(f32)[None],
        rdownbias_row[None],
        expert_counts,
    )


def solution(mesh):
    in_specs = (
        P(("dp", "expert"), None),
        P("dp", None, None),
        P(("dp", "expert"), None),
        P(("dp", "expert"), None),
        P("dp"),
        P("dp", None),
        P(("dp", "expert"), None),
        P("dp", None),
        P("dp"),
        P("dp", None),
        P("dp"),
        P("dp", None),
        P("dp"),
        P("dp", None),
        P("dp"),
        P("dp", None),
        P("dp"),
        P("expert", "dp", None),
        P("expert", "dp"),
        P("expert", "dp", None),
        P("expert", "dp"),
    )
    out_specs = (
        P(("dp", "expert"), None),
        P(("dp", "expert"), None),
        P("dp", None, None),
        P("dp", None),
        P("dp"),
        P("dp", None),
        P("dp"),
        P("dp", None),
        P("dp"),
        P("dp", None),
        P("dp"),
        P("dp", None),
        P("dp"),
        P("expert", "dp", None),
        P("expert", "dp"),
        P("expert", "dp", None),
        P("expert", "dp"),
        P(),
    )
    return jax.shard_map(body, mesh=mesh, in_specs=in_specs, out_specs=out_specs, check_vma=False)
```

time: 2040 us -> 695 us (0.34)
  waiting for transfers between devices: 1550 us -> 371 us
  blocking collectives: 184 us -> 0 us
  matrix products: 178 us -> 92.7 us
  local copies, waits for them, and re-layouts: 31.1 us -> 82.7 us
  other arithmetic: 49.2 us -> 89.5 us
    reduce_scatter x9 -> x3, waiting for transfers between devices: 1060 us -> 188 us  [scatter(): return lax.psum_scatter(value, 'dp', scatter_dimension=0, tiled=False)]
    all_gather x9 -> x2, waiting for transfers between devices: 401 us -> 85.1 us  [the longest x1 85.1 us: body(): second_all = lax.all_gather(second_share, 'dp', axis=0)]
    dot_general x34 -> x31, matrix products: 178 us -> 90.8 us  [mm(): return jnp.einsum(spec, a, b, preferred_element_type=f32)]
    unnamed x2 -> x0, blocking collectives: 75.6 us -> none
    unnamed x23 -> x5, waiting for transfers between devices: 71.8 us -> 0.08 us
    ppermute x0 -> x22, waiting for transfers between devices: none -> 57 us  [swap(): return lax.ppermute(value, 'expert', [(i, i ^ mask) for i in range(size)])]
    psum x3 -> x0, blocking collectives: 56.5 us -> none  [the longest x1 39.4 us: body(): expert_counts = lax.psum(counts_local, ('dp', 'expert'))]
    all_gather x2 -> x0, blocking collectives: 52.2 us -> none  [the longest x1 26.3 us: gather_weights(): lax.all_gather(routed_upbias, 'dp', axis=1, tiled=True)]
  transfers between devices with their start and end apart: 25 -> 31, of which waited for: 18 -> 19; matrix products, arithmetic and copies ran while one was open for 11% -> 22% of each run, Pallas kernels for 0% -> 0%
where the time goes in v1:
time: 695 us; the launch traced here: 688 us
  waiting for transfers between devices  371 us (53%)
  matrix products  92.7 us (13%)
  other arithmetic  89.5 us (13%)
  local copies, waits for them, and re-layouts  82.7 us (12%)
  starting transfers between devices  35.1 us (5%)
  between operations  16.5 us (2%)
    reduce_scatter x3, waiting for transfers between devices, scatter(): return lax.psum_scatter(value, 'dp', scatter_dimension=0, tiled=False)  188 us
    dot_general x31, matrix products, mm(): return jnp.einsum(spec, a, b, preferred_element_type=f32)  90.8 us
    all_gather x1, waiting for transfers between devices, body(): second_all = lax.all_gather(second_share, 'dp', axis=0)  85.1 us
    ppermute x22, waiting for transfers between devices, swap(): return lax.ppermute(value, 'expert', [(i, i ^ mask) for i in range(size)])  57 us
    all_to_all x1, waiting for transfers between devices, body(): lax.all_to_all(mod_parts, 'dp', split_axis=0, concat_axis=0, tiled=True)  21.4 us
    unnamed x220, local copies, waits for them, and re-layouts  19.6 us
    ppermute x22, starting transfers between devices, swap(): return lax.ppermute(value, 'expert', [(i, i ^ mask) for i in range(size)])  16.5 us
    concatenate x1, other arithmetic, body(): jnp.concatenate([jnp.concatenate([heads_all[k, m ^ k] for k in range(grou...  14.1 us
  transfers between devices with their start and end apart: 31, of which 19 were waited for; matrix products, arithmetic and copies ran while one was open for 22% of the time, Pallas kernels for 0%

profile of v1, /device:TPU:0, one launch (start us, length us, event | category | flops | bytes accessed | tf_op | source)
XLA Modules:
  0.0 687.6 jit_solution(2319824139204393057)
XLA Ops:
  26.9 5.8 all-to-all-start
  39.7 12.9 %collective-permute-done = bf16[256,1536]{1,0:T(8,128)(2,1)S(1)} collective-permute-done((bf16[256,1536]{1,0:T(8,128)(2,1)S(1)}, bf16[256,1536]{1,0:T(8,128)(2,1)S(1)}, u32[]{:S(2)}, u32[]{:S(2)}) %collective-permute-start) | collective-permute-done | bytes 786464 | tf_op jit(solution)/shard_map/ppermute | solution.py:46
  56.9 5.7 all-to-all-start.1
  64.6 21.4 %all-to-all-done.1 = f32[8,4,4736]{2,1,0:T(4,128)} async-done(((f32[8,4,4736]{2,1,0:T(4,128)}), f32[8,4,4736]{2,1,0:T(4,128)}, u32[]{:S(2)}, u32[]{:S(2)}) %all-to-all-start.1) | async-done | bytes 606240 | tf_op jit(solution)/shard_map/all_to_all | solution.py:199
  125.4 5.5 collective-permute-done.4
  142.5 14.1 %maximum_maximum_fusion = bf16[1024,768]{0,1:T(8,128)(2,1)S(1)} fusion(bf16[256,192]{0,1:T(8,128)(2,1)S(1)} %get-tuple-element.80, bf16[256,192]{0,1:T(8,128)(2,1)S(1)} %get-tuple-element.116, bf16[256,192]{0,1:T(8,128)(2,1)S(1)} %get-tuple-element.81, bf16[256,192]{0,1:T(8,128)(2,1)S(1)} %get-tuple-element.112, bf16[256,192]{0,1:T(8,128)(2,1)S(1)} %get-tuple-element.82, ...), kind=kLoop, calls=%fused_computation.61 | loop fusion | flops 25165824 | bytes 3145728 | tf_op jit(solution)/shard_map/concatenate | solution.py:234
  165.3 85.1 %all-gather.7.cloned.1.call-done = bf16[7680,768]{1,0:T(8,128)(2,1)} async-done(((bf16[960,768]{1,0:T(8,128)(2,1)}), bf16[7680,768]{1,0:T(8,128)(2,1)}) %all-gather.7.cloned.1.call-update) | async-done | bytes 11796496 | tf_op jit(solution)/shard_map/all_gather | solution.py:138
  253.1 5.2 fusion.113
  261.0 6.8 fusion.135
  274.0 4.3 fusion.134
  286.3 8.3 %collective-permute-done.9 = bf16[256,768]{1,0:T(8,128)(2,1)S(1)} collective-permute-done((bf16[256,768]{1,0:T(8,128)(2,1)S(1)}, bf16[256,768]{1,0:T(8,128)(2,1)S(1)}, u32[]{:S(2)}, u32[]{:S(2)}) %collective-permute-start.9) | collective-permute-done | bytes 393248 | tf_op jit(solution)/shard_map/ppermute | solution.py:46
  299.9 8.9 %collective-permute-done.10 = bf16[256,768]{1,0:T(8,128)(2,1)S(1)} collective-permute-done((bf16[256,768]{1,0:T(8,128)(2,1)S(1)}, bf16[256,768]{1,0:T(8,128)(2,1)S(1)}, u32[]{:S(2)}, u32[]{:S(2)}) %collective-permute-start.10) | collective-permute-done | bytes 393248 | tf_op jit(solution)/shard_map/ppermute | solution.py:46
  315.0 6.8 fusion.31
  321.8 6.1 multiply_reduce_fusion
  328.9 5.6 multiply_convert_fusion
  334.6 5.0 fusion.30
  354.2 6.6 convolution_convert_fusion
  364.9 5.0 convolution_convert_fusion.1
  381.6 6.7 add_convert_fusion.3
  399.5 7.9 %collective-permute-done.7 = bf16[256,768]{1,0:T(8,128)(2,1)S(1)} collective-permute-done((bf16[256,768]{1,0:T(8,128)(2,1)}, bf16[256,768]{1,0:T(8,128)(2,1)S(1)}, u32[]{:S(2)}, u32[]{:S(2)}) %collective-permute-start.7) | collective-permute-done | bytes 393248 | tf_op jit(solution)/shard_map/ppermute | solution.py:46
  410.0 5.2 collective-permute-done.13
  434.8 13.2 %all-to-all-done.2 = bf16[8,4,4608]{2,1,0:T(4,128)(2,1)S(1)} async-done(((bf16[8,4,4608]{2,1,0:T(4,128)(2,1)}), bf16[8,4,4608]{2,1,0:T(4,128)(2,1)S(1)}, u32[]{:S(2)}, u32[]{:S(2)}) %all-to-all-start.2) | async-done | bytes 294944 | tf_op jit(solution)/shard_map/all_to_all | solution.py:404
  460.8 75.6 %reduce-scatter.8.cloned.1.call-done = bf16[1,480,768]{2,1,0:T(8,128)(2,1)} async-done(((bf16[8,480,768]{2,1,0:T(8,128)(2,1)}), bf16[1,480,768]{2,1,0:T(8,128)(2,1)}) %reduce-scatter.8.cloned.1.call-update) | async-done | bytes 737296 | tf_op jit(solution)/shard_map/reduce_scatter | solution.py:266
  543.0 112.5 %reduce-scatter.6.cloned.1.call-done = bf16[1,496,768]{2,1,0:T(8,128)(2,1)} async-done(((bf16[8,496,768]{2,1,0:T(8,128)(2,1)}), bf16[1,496,768]{2,1,0:T(8,128)(2,1)}) %reduce-scatter.6.cloned.1.call-update) | async-done | bytes 761872 | tf_op jit(solution)/shard_map/reduce_scatter | solution.py:266
  (494 shorter events, 231.0 us)
Async XLA Ops:
  7.2 91.8 %all-gather.5.cloned.1.call-start = ((), (), s32[]{:S(2)}) async-start(), calls=%async_computation.10 | async-start | bytes 2838528 | tf_op jit(solution)/shard_map/all_gather | solution.py:122
  16.3 234.1 %all-gather.7.cloned.1.call-start = ((), (), s32[]{:S(2)}) async-start(), calls=%async_computation.11 | async-start | bytes 13271040 | tf_op jit(solution)/shard_map/all_gather | solution.py:138
  23.3 12.9 %collective-permute-start.2 = (f32[4,256]{1,0:T(4,128)S(1)}, f32[4,256]{1,0:T(4,128)S(1)}, u32[]{:S(2)}, u32[]{:S(2)}) collective-permute-start(f32[4,256]{1,0:T(4,128)S(1)} %get-tuple-element.143), channel_id=1, source_target_pairs={{0,2},{1,3},{2,0},{3,1},{4,6},{5,7},{6,4},{7,5},{8,10},{9,11},{10,... | collective-permute-start | bytes 12296 | tf_op jit(solution)/shard_map/ppermute | solution.py:46
  26.9 12.4 %all-to-all-start = ((bf16[8,4,96]{2,1,0:T(4,128)(2,1)}), bf16[8,4,96]{2,1,0:T(4,128)(2,1)S(1)}, u32[]{:S(2)}, u32[]{:S(2)}) async-start(bf16[8,4,96]{2,1,0:T(4,128)(2,1)} %copy.186), calls=%async_computation | async-start | bytes 16384 | tf_op jit(solution)/shard_map/all_to_all | solution.py:183
  33.8 18.8 %collective-permute-start = (bf16[256,1536]{1,0:T(8,128)(2,1)S(1)}, bf16[256,1536]{1,0:T(8,128)(2,1)S(1)}, u32[]{:S(2)}, u32[]{:S(2)}) collective-permute-start(bf16[256,1536]{1,0:T(8,128)(2,1)S(1)} %constant_dynamic-update-slice_fusion), channel_id=1, source_target_pairs={{0,2},{1,3},{2,0},{3,1},{4,6},{5,7},{6,4},{7,5},{8,10},{9,11},{10,... | collective-permute-start | bytes 2359304 | tf_op jit(solution)/shard_map/ppermute | solution.py:46
  53.9 35.7 %collective-permute-start.1 = (bf16[2,256,1536]{2,1,0:T(8,128)(2,1)}, bf16[2,256,1536]{2,1,0:T(8,128)(2,1)}, u32[]{:S(2)}, u32[]{:S(2)}) collective-permute-start(bf16[2,256,1536]{2,1,0:T(8,128)(2,1)} %pad_maximum_fusion.3), channel_id=1, source_target_pairs={{0,1},{1,0},{2,3},{3,2},{4,5},{5,4},{6,7},{7,6},{8,9},{9,8},{10,11... | collective-permute-start | bytes 4718600 | tf_op jit(solution)/shard_map/ppermute | solution.py:46
  56.9 29.1 %all-to-all-start.1 = ((f32[8,4,4736]{2,1,0:T(4,128)}), f32[8,4,4736]{2,1,0:T(4,128)}, u32[]{:S(2)}, u32[]{:S(2)}) async-start(f32[8,4,4736]{2,1,0:T(4,128)} %reshape.586), calls=%async_computation.1 | async-start | bytes 1212416 | tf_op jit(solution)/shard_map/all_to_all | solution.py:199
  62.6 370.9 %reduce-scatter.4.cloned.1.call-start = ((), (), s32[]{:S(2)}) async-start(), calls=%async_computation.7 | async-start | bytes 1548288 | tf_op jit(solution)/shard_map/reduce_scatter | solution.py:266
  119.7 11.2 %collective-permute-start.4 = (bf16[4,256,192]{1,2,0:T(8,128)(2,1)}, bf16[4,256,192]{1,2,0:T(8,128)(2,1)}, u32[]{:S(2)}, u32[]{:S(2)}) collective-permute-start(bf16[4,256,192]{1,2,0:T(8,128)(2,1)} %copy.193), channel_id=1, source_target_pairs={{0,2},{1,3},{2,0},{3,1},{4,6},{5,7},{6,4},{7,5},{8,10},{9,11},{10,... | collective-permute-start | bytes 1179656 | tf_op jit(solution)/shard_map/ppermute | solution.py:46
  132.9 8.4 %collective-permute-start.5 = (bf16[2,4,256,192]{2,3,1,0:T(8,128)(2,1)}, bf16[2,4,256,192]{2,3,1,0:T(8,128)(2,1)}, u32[]{:S(2)}, u32[]{:S(2)}) collective-permute-start(bf16[2,4,256,192]{2,3,1,0:T(8,128)(2,1)} %pad_maximum_fusion.9), channel_id=1, source_target_pairs={{0,1},{1,0},{2,3},{3,2},{4,5},{5,4},{6,7},{7,6},{8,9},{9,8},{10,11... | collective-permute-start | bytes 2359304 | tf_op jit(solution)/shard_map/ppermute | solution.py:46
  283.4 11.2 %collective-permute-start.9 = (bf16[256,768]{1,0:T(8,128)(2,1)S(1)}, bf16[256,768]{1,0:T(8,128)(2,1)S(1)}, u32[]{:S(2)}, u32[]{:S(2)}) collective-permute-start(bf16[256,768]{1,0:T(8,128)(2,1)S(1)} %fusion.57), channel_id=1, source_target_pairs={{0,2},{1,3},{2,0},{3,1},{4,6},{5,7},{6,4},{7,5},{8,10},{9,11},{10,... | collective-permute-start | bytes 1179656 | tf_op jit(solution)/shard_map/ppermute | solution.py:46
  298.5 10.3 %collective-permute-start.10 = (bf16[256,768]{1,0:T(8,128)(2,1)S(1)}, bf16[256,768]{1,0:T(8,128)(2,1)S(1)}, u32[]{:S(2)}, u32[]{:S(2)}) collective-permute-start(bf16[256,768]{1,0:T(8,128)(2,1)S(1)} %get-tuple-element.35), channel_id=1, source_target_pairs={{0,2},{1,3},{2,0},{3,1},{4,6},{5,7},{6,4},{7,5},{8,10},{9,11},{10,... | collective-permute-start | bytes 1179656 | tf_op jit(solution)/shard_map/ppermute | solution.py:46
  351.1 185.2 %reduce-scatter.8.cloned.1.call-start = ((), (), s32[]{:S(2)}) async-start(), calls=%async_computation.9 | async-start | bytes 6635520 | tf_op jit(solution)/shard_map/reduce_scatter | solution.py:266
  363.8 291.6 %reduce-scatter.6.cloned.1.call-start = ((), (), s32[]{:S(2)}) async-start(), calls=%async_computation.8 | async-start | bytes 6856704 | tf_op jit(solution)/shard_map/reduce_scatter | solution.py:266
  389.5 4.5 collective-permute-start.6
  395.2 12.1 %collective-permute-start.7 = (bf16[256,768]{1,0:T(8,128)(2,1)}, bf16[256,768]{1,0:T(8,128)(2,1)S(1)}, u32[]{:S(2)}, u32[]{:S(2)}) collective-permute-start(bf16[256,768]{1,0:T(8,128)(2,1)} %fusion.56), channel_id=1, source_target_pairs={{0,2},{1,3},{2,0},{3,1},{4,6},{5,7},{6,4},{7,5},{8,10},{9,11},{10,... | collective-permute-start | bytes 1179656 | tf_op jit(solution)/shard_map/ppermute | solution.py:46
  398.7 16.5 %collective-permute-start.13 = (bf16[256,768]{1,0:T(8,128)(2,1)}, bf16[256,768]{1,0:T(8,128)(2,1)S(1)}, u32[]{:S(2)}, u32[]{:S(2)}) collective-permute-start(bf16[256,768]{1,0:T(8,128)(2,1)} %fusion.42), channel_id=1, source_target_pairs={{0,2},{1,3},{2,0},{3,1},{4,6},{5,7},{6,4},{7,5},{8,10},{9,11},{10,... | collective-permute-start | bytes 1179656 | tf_op jit(solution)/shard_map/ppermute | solution.py:46
  426.4 21.7 %all-to-all-start.2 = ((bf16[8,4,4608]{2,1,0:T(4,128)(2,1)}), bf16[8,4,4608]{2,1,0:T(4,128)(2,1)S(1)}, u32[]{:S(2)}, u32[]{:S(2)}) async-start(bf16[8,4,4608]{2,1,0:T(4,128)(2,1)} %broadcast_in_dim.97), calls=%async_computation.2 | async-start | bytes 589824 | tf_op jit(solution)/shard_map/all_to_all | solution.py:404
  433.5 19.1 %collective-permute-start.16 = (bf16[112,768]{1,0:T(8,128)(2,1)}, bf16[112,768]{1,0:T(8,128)(2,1)S(1)}, u32[]{:S(2)}, u32[]{:S(2)}) collective-permute-start(bf16[112,768]{1,0:T(8,128)(2,1)} %bitcast.376), channel_id=1, source_target_pairs={{0,2},{1,3},{2,0},{3,1},{4,6},{5,7},{6,4},{7,5},{8,10},{9,11},{10,... | collective-permute-start | bytes 516104 | tf_op jit(solution)/shard_map/ppermute | solution.py:46
  449.1 10.3 %all-to-all-start.3 = ((f32[8,4,96]{2,1,0:T(4,128)}), f32[8,4,96]{2,1,0:T(4,128)S(1)}, u32[]{:S(2)}, u32[]{:S(2)}) async-start(f32[8,4,96]{2,1,0:T(4,128)} %fusion.37), calls=%async_computation.3 | async-start | bytes 32768 | tf_op jit(solution)/shard_map/all_to_all | solution.py:420
  453.7 6.4 collective-permute-start.17
  537.3 5.5 collective-permute-start.20
  542.9 119.2 %collective-permute-start.21 = (bf16[2,96,768]{2,1,0:T(8,128)(2,1)S(1)}, bf16[2,96,768]{2,1,0:T(8,128)(2,1)S(1)}, u32[]{:S(2)}, u32[]{:S(2)}) collective-permute-start(bf16[2,96,768]{2,1,0:T(8,128)(2,1)S(1)} %pad_maximum_fusion.24), channel_id=1, source_target_pairs={{0,1},{1,0},{2,3},{3,2},{4,5},{5,4},{6,7},{7,6},{8,9},{9,8},{10,11... | collective-permute-start | bytes 884744 | tf_op jit(solution)/shard_map/ppermute | solution.py:46
  656.4 5.9 collective-permute-start.18
  (108 other events, 768.1 us)
Sparse Core Ops, SparseCore 0:
  16.4 62.6 all-gather.4
  81.4 168.9 all-gather.6
  351.3 62.8 reduce-scatter.3
  417.7 118.6 reduce-scatter.7
  539.9 115.4 reduce-scatter.5

commit v2 on v1

v2 whole, which is shorter than its diff:
```python
import jax
import jax.numpy as jnp
from jax import lax
from jax.experimental import pallas as pl
from jax.experimental.pallas import tpu as pltpu
from jax.sharding import PartitionSpec as P

HEADS = 12
HEAD_DIM = 64
CAP = 128

epsilon = 1e-06
gelu_root = 0.7978845608028654
gelu_cubic = 0.044715

bf16 = jnp.bfloat16
f32 = jnp.float32


def norm_parts(values):
    centered = values - jnp.mean(values, axis=-1, keepdims=True)
    inv_std = lax.rsqrt(jnp.mean(centered * centered, axis=-1, keepdims=True) + epsilon)
    return (centered * inv_std, inv_std)


def norm_back(grad_normed, normed, inv_std):
    mean_grad = jnp.mean(grad_normed, axis=-1, keepdims=True)
    mean_cross = jnp.mean(grad_normed * normed, axis=-1, keepdims=True)
    return inv_std * (grad_normed - mean_grad - normed * mean_cross)


def gelu_parts(values):
    square = values * values
    half = 0.5 + 0.5 * jnp.tanh(values * (gelu_root + gelu_root * gelu_cubic * square))
    activation = values * half
    slope = half + activation * (1.0 - half) * (
        2.0 * gelu_root + 6.0 * gelu_root * gelu_cubic * square
    )
    return (activation, slope)


def mm(spec, a, b):
    return jnp.einsum(spec, a, b, preferred_element_type=f32)


def swap(value, mask):
    size = lax.axis_size("expert")
    return lax.ppermute(value, "expert", [(i, i ^ mask) for i in range(size)])


def gather_group(value):
    across = swap(value, 2)
    beside = swap(jnp.stack([value, across]), 1)
    return jnp.stack([value, beside[0], across, beside[1]])


def reduce_group(send, keep):
    beside = swap(send, 1).astype(f32)
    own = keep[0] + beside[0]
    other = (keep[1] + beside[1]).astype(bf16)
    return own, swap(other, 2)


def dp_swap(value, mask):
    copies = lax.axis_size("dp")
    return lax.ppermute(value, "dp", [(i, i ^ mask) for i in range(copies)])


def pair_swap(value):
    return dp_swap(value, 2)


def side_groups(copies):
    return [[i for i in range(copies) if (i >> 1) % 2 == side] for side in range(2)]


def pair_places(p):
    first = ((p >> 1) << 2) | (p & 1)
    return first, first + 2


def spread(value):
    far = dp_swap(value, 4)
    return [value, dp_swap(value, 1), far, dp_swap(far, 1)]


def collect(send, keep, start, middle, end):
    got = dp_swap(tied(send, *start), 1)
    wide = tied(got, *middle).astype(f32)
    far = dp_swap((keep[1] + wide[1]).astype(bf16), 4)
    return keep[0] + wide[0] + tied(far, *end).astype(f32), got


def tied(value, *others):
    return lax.optimization_barrier((value, *others))[0]


def ring_place(at, copies):
    at = lax.rem(at + copies, copies)
    return jnp.where(at < copies // 2, 2 * at, 2 * (copies - 1 - at) + 1)


def ring_gather(share):
    copies = lax.axis_size("dp")
    if copies > 8:
        whole = lax.all_gather(share, "dp", axis=0)
        whole = whole.reshape((8, copies // 8 * share.shape[0]) + share.shape[1:])
        return [whole[k] for k in range(8)], jnp.arange(8, dtype=jnp.int32)
    half = copies // 2
    ring = [2 * i for i in range(half)] + [2 * i + 1 for i in reversed(range(half))]
    place = lax.axis_index("dp")
    position = jnp.where(lax.rem(place, 2) == 0, place // 2, copies - 1 - place // 2)

    def hop(value, way):
        return lax.ppermute(
            value, "dp", [(ring[i], ring[(i + way) % copies]) for i in range(copies)]
        )

    pieces, offsets = [share], [0]
    right = left = share
    for step in range(1, half + 1):
        right = hop(right, 1)
        pieces.append(right)
        offsets.append(-step)
        if step < half:
            left = hop(left, -1)
            pieces.append(left)
            offsets.append(step)
    return pieces, ring_place(position + jnp.array(offsets, jnp.int32), copies)


def dot(a, b, left=1, right=0):
    return lax.dot_general(
        a, b, (((left,), (right,)), ((), ())), preferred_element_type=f32
    )


def full(shape):
    return pl.BlockSpec(shape, lambda i: (0,) * len(shape), pipeline_mode=pl.Buffered(1))


SCALARS = pl.BlockSpec(memory_space=pltpu.SMEM)


def kernel_call(body, grid, in_specs, out_specs, out_shape, scratch, flops, operands):
    out_bytes = sum(int(o.size) * o.dtype.itemsize for o in out_shape)
    in_bytes = sum(int(o.size) * o.dtype.itemsize for o in operands)
    return pl.pallas_call(
        body,
        grid=(grid,),
        in_specs=in_specs,
        out_specs=out_specs,
        out_shape=out_shape,
        scratch_shapes=scratch,
        compiler_params=pltpu.CompilerParams(vmem_limit_bytes=56 * 2**20),
        cost_estimate=pl.CostEstimate(
            flops=int(flops), bytes_accessed=out_bytes + in_bytes, transcendentals=0
        ),
    )(*operands)


def shape(dims, dtype):
    return jax.ShapeDtypeStruct(dims, dtype)


def prepare(info, proj, qkv, biases, up, down, rup, rdown, keep, group):
    d_rows, width = proj.shape
    cols = width // group
    f_rows = down.shape[0]
    f_own = f_rows // group
    count = up.shape[1] // f_rows
    wide = 3 * cols

    def body(info, proj, qkv, *refs):
        biases, (up, down, rup, rdown, first, third, mine, theirs, d_mine, d_theirs) = (
            refs[: len(biases_in)],
            refs[len(biases_in) :],
        )
        third[d_rows + f_own :, :] = proj[...]
        lines = [
            jnp.concatenate([b[...].astype(f32), jnp.zeros((1, wide - b.shape[1]), f32)], axis=1)
            for b in biases[1:]
        ]
        for p in range(group):

            @pl.when(info[8] == p)
            def _():
                own = slice(p * f_own, (p + 1) * f_own)
                first[:d_rows, :] = jnp.concatenate(
                    [qkv[:, i * width + p * cols : i * width + (p + 1) * cols] for i in range(3)],
                    axis=1,
                )
                line = jnp.concatenate(
                    [biases[0][:, own].astype(f32), jnp.zeros((1, wide - f_own), f32)], axis=1
                )
                first[d_rows:, :] = jnp.concatenate(
                    [line] + lines + [jnp.zeros((15 - len(lines), wide), f32)], axis=0
                ).astype(bf16)
                third[:d_rows, :] = jnp.concatenate(
                    [
                        up[:, d * f_rows + p * f_own : d * f_rows + (p + 1) * f_own]
                        for d in range(count)
                    ],
                    axis=1,
                )
                third[d_rows : d_rows + f_own, :] = down[own, :]

        one, two = [], []
        for p in range(count // 2):
            at, to = (d * f_rows for d in pair_places(p))
            one += [(at, at + keep), (to, to + f_rows - keep)]
            two += [(to + f_rows - keep, to + f_rows), (at + keep, at + f_rows)]
        for side in range(2):

            @pl.when(info[9] == side)
            def _():
                own, other = (one, two) if side == 0 else (two, one)
                for ref, parts in ((mine, own), (theirs, other)):
                    at = 0
                    for low, high in parts:
                        ref[:, at : at + high - low] = rup[:, low:high]
                        at += high - low
                start = side * (f_rows - keep)
                d_mine[...] = rdown[start : start + keep, :]
                start = (1 - side) * keep
                d_theirs[...] = rdown[start : start + f_rows - keep, :]

    biases_in = biases
    operands = [proj, qkv, *biases, up, down, rup, rdown]
    outs = [
        shape((d_rows + 16, wide), bf16),
        shape((2 * d_rows + f_own, width), bf16),
        shape((d_rows, rup.shape[1] // 2), bf16),
        shape((d_rows, rup.shape[1] // 2), bf16),
        shape((keep, width), bf16),
        shape((f_rows - keep, width), bf16),
    ]
    return kernel_call(
        body,
        1,
        [SCALARS] + [full(o.shape) for o in operands],
        [full(o.shape) for o in outs],
        outs,
        [],
        0,
        [info, *operands],
    )


def middle_back(own, got, middle_rows, attn_out, cotangent, mods):
    rows, width = own.shape

    def body(own, got, mid, out, cot, mod, grad_mid, grad_attn, sums):
        grad = own[...] + got[...].astype(f32)
        normed, inv_std = norm_parts(mid[...])
        value = cot[...].astype(f32) + norm_back(
            grad * (1.0 + mod[0, 4:5, :]), normed, inv_std
        )
        grad_mid[...] = value
        grad_attn[...] = (mod[0, 2:3, :] * value).astype(bf16)
        sums[0:1, :] = jnp.sum(value * out[...], axis=0, keepdims=True)
        sums[1:2, :] = jnp.sum(grad, axis=0, keepdims=True)
        sums[2:3, :] = jnp.sum(grad * normed, axis=0, keepdims=True)
        sums[3:, :] = jnp.zeros((5, width), f32)

    operands = [own, got, middle_rows, attn_out, cotangent]
    outs = [shape((rows, width), f32), shape((rows, width), bf16), shape((8, width), f32)]
    return kernel_call(
        body,
        1,
        [full(o.shape) for o in operands] + [pl.BlockSpec((1, 8, width), lambda i: (0, 0, 0))],
        [full(o.shape) for o in outs],
        outs,
        [],
        0,
        [*operands, mods],
    )


def routed_rows(info, up_own, up_got, down_own, down_got, keep):
    d_rows, half = up_got.shape
    f_rows = down_own.shape[0]
    width = down_own.shape[1]
    pairs = half // f_rows

    def body(info, uo, ug, do, dg, up, down):
        for side in range(2):

            @pl.when(info[9] == side)
            def _():
                first, second = (0, 1) if side == 0 else (1, 0)
                values = (uo[:d_rows, :], ug[...].astype(f32))
                for p in range(pairs):
                    at, to = (d * f_rows for d in pair_places(p))
                    for whose, low, high, frm in (
                        (first, at, at + keep, 0),
                        (first, to, to + f_rows - keep, keep),
                        (second, to + f_rows - keep, to + f_rows, 0),
                        (second, at + keep, at + f_rows, keep),
                    ):
                        base = p * f_rows + frm
                        up[:, low:high] = values[whose][:, base : base + high - low]
                start = side * (f_rows - keep)
                down[start : start + keep, :] = do[:keep, :]
                start = (1 - side) * keep
                down[start : start + f_rows - keep, :] = dg[...].astype(f32)

    operands = [up_own, up_got, down_own, down_got]
    outs = [shape((d_rows, 2 * half), f32), shape((f_rows, width), f32)]
    return kernel_call(
        body,
        1,
        [SCALARS] + [full(o.shape) for o in operands],
        [full(o.shape) for o in outs],
        outs,
        [],
        0,
        [info, *operands],
    )


def group_rows_out(info, shared, last, d_rows, f_rows):
    group, _, width = shared.shape
    f_own = f_rows // group
    cols = width // group
    count = width // f_own

    def body(info, shared, last, up, down, qkv, proj):
        for a in range(group):
            part = shared[info[8] ^ a].astype(f32)
            for d in range(count):
                at = d * f_rows + a * f_own
                up[:, at : at + f_own] = part[:d_rows, d * f_own : (d + 1) * f_own]
            down[a * f_own : (a + 1) * f_own, :] = part[d_rows:, :]
            part = last[info[8] ^ a].astype(f32)
            for i in range(3):
                at = i * width + a * cols
                qkv[:, at : at + cols] = part[:, i * cols : (i + 1) * cols]
            proj[:, a * cols : (a + 1) * cols] = part[:, 3 * cols :]

    outs = [
        shape((d_rows, count * f_rows), f32),
        shape((f_rows, width), f32),
        shape((d_rows, 3 * width), f32),
        shape((d_rows, width), f32),
    ]
    return kernel_call(
        body,
        1,
        [SCALARS, full(shared.shape), full(last.shape)],
        [full(o.shape) for o in outs],
        outs,
        [],
        0,
        [info, shared, last],
    )


def front(info, tokens, mods, bias, pairs, pieces, rows_piece, cols_own, cut):
    blocks, rows, _ = tokens.shape
    width = 8 * rows_piece
    wide = 3 * cols_own

    def body(info, tok, mod, bias, pairs, *refs):
        parts = refs[:8]
        (hid, prj, qkv, table, gates, low_grad, slot, sums, lines, units, three, lists) = refs[8:]
        step = pl.program_id(0)

        @pl.when(step == 0)
        def _():
            for k in range(8):
                at = pl.multiple_of(info[k] * rows_piece, rows_piece)
                qkv[pl.ds(at, rows_piece), :] = parts[k][:rows_piece, :]
                if cut:
                    lists[info[k]] = parts[k][rows_piece:, :].astype(f32)
            three[...] = bias[...]
            if cut:
                three[:, :cols_own] = lists[info[8]][2:3, :cols_own]
                three[:, 2 * cols_own :] = lists[info[8] + 4][2:3, :cols_own]
                lines[...] = jnp.zeros_like(lines)
                for d in range(8):
                    at = slice(d * rows_piece, (d + 1) * rows_piece)
                    for i, row in enumerate((0, 3, 4, 5)):
                        lines[i : i + 1, at] = lists[d, row : row + 1, :rows_piece]
                size = units.shape[2]
                for side in range(2):

                    @pl.when(info[9] == side)
                    def _():
                        for p in range(units.shape[0]):
                            one, two = pair_places(p)
                            if side == 0:
                                units[p, :, :cut] = lists[one, 1:2, :cut]
                                units[p, :, cut:] = lists[two, 1:2, : size - cut]
                            else:
                                units[p, :, :cut] = lists[two, 1:2, size - cut : size]
                                units[p, :, cut:] = lists[one, 1:2, cut:size]

            sums[...] = jnp.zeros_like(sums)

        normed, _ = norm_parts(tok[0, :, :width].astype(f32))
        low = (normed * (1.0 + mod[0, 1:2, :]) + mod[0, 0:1, :]).astype(bf16)
        hid[...] = low
        prj[...] = (dot(low, qkv[...]) + three[...]).astype(bf16)

        me = info[8].astype(f32)
        one = (pairs[0, 0:1, :] == me).astype(f32)
        two = (pairs[0, 1:2, :] == me).astype(f32)
        hot = one + two
        gate = one * pairs[0, 2:3, :] + two * pairs[0, 3:4, :]
        across = lax.broadcasted_iota(jnp.int32, (rows, rows), 1)
        down = lax.broadcasted_iota(jnp.int32, (rows, rows), 0)
        earlier = (down < across).astype(f32).astype(bf16)
        rank = dot(jnp.broadcast_to(hot, (8, rows)).astype(bf16), earlier)[0:1, :]
        kept = hot * (rank < CAP).astype(f32)
        places = lax.broadcasted_iota(jnp.int32, (CAP, rows), 0).astype(f32)
        placed = jnp.where(rank == places, kept, 0.0)
        table[0] = placed.astype(bf16)
        gates[0] = jnp.sum(jnp.where(down == across, gate, 0.0), axis=1, keepdims=True)
        cot = tok[0, :, width:]
        grad = (mod[0, 5:6, :] * cot.astype(f32)).astype(bf16)
        low_grad[...] = grad
        gate_slot = jnp.sum(placed * gate, axis=1, keepdims=True)
        slot_grad = (gate_slot * (mod[0, 5:6, :] * dot(table[0], cot))).astype(bf16)
        slot[...] = slot_grad
        sums[0:1, :] += jnp.sum(slot_grad.astype(f32), axis=0, keepdims=True)
        sums[1:2, :] += jnp.sum(grad.astype(f32), axis=0, keepdims=True)
        sums[2:3, :] += jnp.broadcast_to(jnp.sum(kept, axis=1, keepdims=True), (1, width))

    return kernel_call(
        body,
        blocks,
        [
            SCALARS,
            pl.BlockSpec((1, rows, 2 * width), lambda i: (i, 0, 0)),
            pl.BlockSpec((1, 8, width), lambda i: (i, 0, 0)),
            full((1, wide)),
            pl.BlockSpec((1, 4, rows), lambda i: (i, 0, 0)),
        ]
        + [full(p.shape) for p in pieces],
        [
            pl.BlockSpec((rows, width), lambda i: (i, 0)),
            pl.BlockSpec((rows, wide), lambda i: (i, 0)),
            full((width, wide)),
            pl.BlockSpec((1, CAP, rows), lambda i: (i, 0, 0)),
            pl.BlockSpec((1, rows, 1), lambda i: (i, 0, 0)),
            pl.BlockSpec((rows, width), lambda i: (i, 0)),
            pl.BlockSpec((CAP, width), lambda i: (i, 0)),
            full((8, width)),
            full((8, width)),
            full((4, 1, width // 2)),
        ],
        [
            shape((blocks * rows, width), bf16),
            shape((blocks * rows, wide), bf16),
            shape((width, wide), bf16),
            shape((blocks, CAP, rows), bf16),
            shape((blocks, rows, 1), f32),
            shape((blocks * rows, width), bf16),
            shape((blocks * CAP, width), bf16),
            shape((8, width), f32),
            shape((8, width), f32),
            shape((4, 1, width // 2), f32),
        ],
        [pltpu.VMEM((1, wide), f32), pltpu.VMEM((8, 16, wide), f32)],
        2 * blocks * rows * width * wide,
        [info, tokens, mods, bias, pairs, *pieces],
    )


def to_rows(own, got, bias, table, gates, addend, tokens, line):
    blocks, cap, rows = table.shape
    width = own.shape[1]

    def body(own, got, bias, tab, gate, add, tok, line, send, keep, sums):
        slots = (own[...] + got[...].astype(f32) + bias[...]).astype(bf16)
        value = add[...] + gate[0] * dot(tab[0], slots, 0, 0)
        first = (pl.program_id(0) == 0).astype(f32)
        sums[0] = jnp.sum(
            tok[0].astype(f32) * (value + first * line[...]), axis=0, keepdims=True
        )
        for k in range(blocks):

            @pl.when(pl.program_id(0) == k)
            def _():
                if k % 2 == 1:
                    send[k // 2] = value.astype(bf16)
                else:
                    keep[k // 2] = value

    operands = [own, got, bias, table, gates, addend, tokens, line]
    return kernel_call(
        body,
        blocks,
        [
            pl.BlockSpec((cap, width), lambda i: (i, 0)),
            pl.BlockSpec((cap, width), lambda i: (i, 0)),
            full((1, width)),
            pl.BlockSpec((1, cap, rows), lambda i: (i, 0, 0)),
            pl.BlockSpec((1, rows, 1), lambda i: (i, 0, 0)),
            pl.BlockSpec((rows, width), lambda i: (i, 0)),
            pl.BlockSpec((1, rows, width), lambda i: (i, 0, 1)),
            full((1, width)),
        ],
        [
            full((2, rows, width)),
            full((2, rows, width)),
            pl.BlockSpec((1, 1, width), lambda i: (i, 0, 0)),
        ],
        [
            shape((2, rows, width), bf16),
            shape((2, rows, width), f32),
            shape((blocks, 1, width), f32),
        ],
        [],
        2 * blocks * rows * width * cap,
        operands,
    )


def score_parts(info, query, key, blocks, rows):
    own = info[10 + pl.program_id(0)]
    lanes = lax.broadcasted_iota(jnp.int32, (1, blocks * rows), 1) // rows
    seen = jnp.zeros((1, blocks * rows), jnp.int32)
    for j in range(blocks):
        seen = jnp.where((lanes == j) & (info[10 + j] == own), 1, seen)
    scores = dot(query, key, 1, 1) * (HEAD_DIM ** (-0.5))
    masked = jnp.where(seen == 1, scores, -1e30)
    exponent = jnp.exp(masked - jnp.max(masked, axis=-1, keepdims=True))
    return exponent / jnp.sum(exponent, axis=-1, keepdims=True)


def attention(info, projected, blocks, cols_own):
    total, wide = projected.shape
    rows = total // blocks

    def body(info, own, every, out):
        for h in range(cols_own // HEAD_DIM):
            q = slice(h * HEAD_DIM, (h + 1) * HEAD_DIM)
            k = slice(cols_own + h * HEAD_DIM, cols_own + (h + 1) * HEAD_DIM)
            v = slice(2 * cols_own + h * HEAD_DIM, 2 * cols_own + (h + 1) * HEAD_DIM)
            probs = score_parts(info, own[:, q], every[:, k], blocks, rows)
            out[:, q] = dot(probs.astype(bf16), every[:, v]).astype(bf16)

    return kernel_call(
        body,
        blocks,
        [SCALARS, pl.BlockSpec((rows, wide), lambda i: (i, 0)), full((total, wide))],
        [pl.BlockSpec((rows, cols_own), lambda i: (i, 0))],
        [shape((total, cols_own), bf16)],
        [],
        4 * total * total * cols_own,
        [info, projected, projected],
    )[0]


def attention_back(info, projected, grad_attn, proj_rel, blocks, cols_own):
    total, wide = projected.shape
    rows = total // blocks
    width = grad_attn.shape[1]
    scale = HEAD_DIM ** (-0.5)

    def body(info, own, every, grad, rel, out, sums_k, sums_v, sums_q):
        step = pl.program_id(0)

        @pl.when(step == 0)
        def _():
            sums_k[...] = jnp.zeros_like(sums_k)
            sums_v[...] = jnp.zeros_like(sums_v)

        back = dot(grad[...], rel[...], 1, 1).astype(bf16)
        for h in range(cols_own // HEAD_DIM):
            q = slice(h * HEAD_DIM, (h + 1) * HEAD_DIM)
            k = slice(cols_own + h * HEAD_DIM, cols_own + (h + 1) * HEAD_DIM)
            v = slice(2 * cols_own + h * HEAD_DIM, 2 * cols_own + (h + 1) * HEAD_DIM)
            probs = score_parts(info, own[:, q], every[:, k], blocks, rows)
            grad_probs = dot(back[:, q], every[:, v], 1, 1)
            inner = jnp.sum(probs * grad_probs, axis=-1, keepdims=True)
            scores = (probs * (grad_probs - inner)).astype(bf16)
            at = pl.multiple_of(step * rows, rows)
            sums_q[pl.ds(at, rows), q] = dot(scores, every[:, k]) * scale
            sums_k[:, q] += dot(scores, own[:, q], 0, 0)
            sums_v[:, q] += dot(probs.astype(bf16), back[:, q], 0, 0)

        @pl.when(step == blocks - 1)
        def _():
            out[:, :cols_own] = sums_q[...].astype(bf16)
            out[:, cols_own : 2 * cols_own] = (sums_k[...] * scale).astype(bf16)
            out[:, 2 * cols_own :] = sums_v[...].astype(bf16)

    return kernel_call(
        body,
        blocks,
        [
            SCALARS,
            pl.BlockSpec((rows, wide), lambda i: (i, 0)),
            full((total, wide)),
            pl.BlockSpec((rows, width), lambda i: (i, 0)),
            full((cols_own, width)),
        ],
        [full((total, wide))],
        [shape((total, wide), bf16)],
        [pltpu.VMEM((total, cols_own), f32)] * 3,
        10 * total * total * cols_own + 2 * total * width * cols_own,
        [info, projected, projected, grad_attn, proj_rel],
    )[0]


def middle(info, tokens, mods, heads, pieces, proj_bias, table, rows_piece):
    blocks, rows, _ = tokens.shape
    width = 8 * rows_piece
    cols = width // blocks
    cap = table.shape[1]

    def body(info, tok, mod, h0, h1, h2, h3, bias, tab, *refs):
        parts, (hid, att, buf, out0, mid0, own, rel) = refs[:4], refs[4:]

        @pl.when(pl.program_id(0) == 0)
        def _():
            for k in range(8):
                place = info[18 + k]
                at = ((place >> 1) ^ info[8]) * cols + (place & 1) * rows_piece
                at = pl.multiple_of(at, rows_piece)
                rel[pl.ds(at, rows_piece), :] = parts[k // 2][k % 2, -rows_piece:, :]
            own[...] = rel[:cols, :]

        attended = jnp.concatenate([h0[...], h1[...], h2[...], h3[...]], axis=1)
        att[...] = attended
        out = dot(attended, rel[...]) + bias[...]
        mid = tok[0].astype(f32) + mod[0, 2:3, :] * out
        normed, _ = norm_parts(mid)
        low = (normed * (1.0 + mod[0, 4:5, :]) + mod[0, 3:4, :]).astype(bf16)
        hid[...] = low
        buf[...] = dot(tab[0], low).astype(bf16)

        @pl.when(pl.program_id(0) == 0)
        def _():
            out0[...] = out
            mid0[...] = mid

    return kernel_call(
        body,
        blocks,
        [
            SCALARS,
            pl.BlockSpec((1, rows, width), lambda i: (i, 0, 0)),
            pl.BlockSpec((1, 8, width), lambda i: (i, 0, 0)),
            pl.BlockSpec((rows, cols), lambda i: (i, 0)),
            pl.BlockSpec((rows, cols), lambda i: (i ^ 1, 0)),
            pl.BlockSpec((rows, cols), lambda i: (i ^ 2, 0)),
            pl.BlockSpec((rows, cols), lambda i: (i ^ 3, 0)),
            full((1, width)),
            pl.BlockSpec((1, cap, rows), lambda i: (i, 0, 0)),
        ]
        + [full(p.shape) for p in pieces],
        [
            pl.BlockSpec((rows, width), lambda i: (i, 0)),
            pl.BlockSpec((rows, width), lambda i: (i, 0)),
            pl.BlockSpec((cap, width), lambda i: (i, 0)),
            full((rows, width)),
            full((rows, width)),
            full((cols, width)),
        ],
        [
            shape((blocks * rows, width), bf16),
            shape((blocks * rows, width), bf16),
            shape((blocks * cap, width), bf16),
            shape((rows, width), f32),
            shape((rows, width), f32),
            shape((cols, width), bf16),
        ],
        [pltpu.VMEM((width, width), bf16)],
        2 * blocks * rows * width * (width + cap),
        [info, tokens, mods, *heads, proj_bias, table, *pieces],
    )


def shared_expert(info, hidden, grad, bias, pieces, rows_piece, blocks, paired):
    total, width = hidden.shape
    rows = total // blocks
    pairs = 4
    sums_mine = (pairs, 2 * rows_piece, width) if paired else (2, width, width)
    sums_theirs = (pairs, 2 * rows_piece, width) if paired else (1, 8, width)

    def body(info, hid, gcl, bias, *refs):
        parts, (out, back, mine, theirs, line, up, down, up_sum, down_sum, wide) = refs[:4], refs[4:]
        step = pl.program_id(0)

        @pl.when(step == 0)
        def _():
            for k in range(8):
                at = pl.multiple_of(info[18 + k] * rows_piece, rows_piece)
                up[pl.ds(at, rows_piece), :] = parts[k // 2][k % 2, :rows_piece, :]
                down[pl.ds(at, rows_piece), :] = parts[k // 2][k % 2, rows_piece : 2 * rows_piece, :]
            up_sum[...] = jnp.zeros_like(up_sum)
            down_sum[...] = jnp.zeros_like(down_sum)
            wide[...] = jnp.zeros_like(wide)

        act, slope = gelu_parts(dot(hid[...], up[...]) + bias[...])
        low = act.astype(bf16)
        out[...] = dot(low, down[...])
        down_sum[...] += dot(low, gcl[...], 0, 0)
        grad_pre = dot(gcl[...], down[...], 1, 1) * slope
        grad_low = grad_pre.astype(bf16)
        wide[...] += jnp.sum(grad_low.astype(f32), axis=0, keepdims=True)
        up_sum[...] += dot(hid[...], grad_low, 0, 0)
        back[...] = dot(grad_low, up[...], 1, 1)

        @pl.when(step == blocks - 1)
        def _():
            line[...] = wide[...]
            if not paired:
                mine[0], mine[1] = up_sum[...], down_sum[...]
            for p in range(pairs if paired else 0):
                at = pl.multiple_of(info[18 + 2 * p] * rows_piece, rows_piece)
                far = pl.multiple_of(info[19 + 2 * p] * rows_piece, rows_piece)
                mine[p, :rows_piece, :] = up_sum[pl.ds(at, rows_piece), :]
                mine[p, rows_piece:, :] = down_sum[pl.ds(at, rows_piece), :]
                theirs[p, :rows_piece, :] = up_sum[pl.ds(far, rows_piece), :].astype(bf16)
                theirs[p, rows_piece:, :] = down_sum[pl.ds(far, rows_piece), :].astype(bf16)

    return kernel_call(
        body,
        blocks,
        [
            SCALARS,
            pl.BlockSpec((rows, width), lambda i: (i, 0)),
            pl.BlockSpec((rows, width), lambda i: (i, 0)),
            full((1, width)),
        ]
        + [full(p.shape) for p in pieces],
        [
            pl.BlockSpec((rows, width), lambda i: (i, 0)),
            pl.BlockSpec((rows, width), lambda i: (i, 0)),
            full(sums_mine),
            full(sums_theirs),
            full((1, width)),
        ],
        [
            shape((total, width), f32),
            shape((total, width), f32),
            shape(sums_mine, f32),
            shape(sums_theirs, bf16),
            shape((1, width), f32),
        ],
        [
            pltpu.VMEM((width, width), bf16),
            pltpu.VMEM((width, width), bf16),
            pltpu.VMEM((width, width), f32),
            pltpu.VMEM((width, width), f32),
            pltpu.VMEM((1, width), f32),
        ],
        12 * total * width * width,
        [info, hidden, grad, bias, *pieces],
    )


def routed_expert(info, buffers, slots, ups, downs, bias):
    pairs, _, units = bias.shape
    count, width = buffers[0].shape
    piece = width // (2 * pairs)
    every = pairs * units

    def body(info, b0, b1, s0, s1, *refs):
        ups, downs, bias = refs[:4], refs[4:8], refs[8]
        (ds, dk, us, uk, g0, g1, e0, e1, line, up, down, grad, gsum, esum, bs, ss) = refs[9:]
        step = pl.program_id(0)

        @pl.when(step == 0)
        def _():
            for r in range(pairs):
                for j in range(2):
                    at = pl.multiple_of(info[18 + 2 * r + j] * piece, piece)
                    up[pl.ds(at, piece), :] = ups[r][j]
                at = pl.multiple_of(info[14 + r] * units, units)
                down[pl.ds(at, units), :] = downs[r][...]
            bs[:count, :], bs[count:, :] = b0[...], b1[...]
            ss[:count, :], ss[count:, :] = s0[...], s1[...]
            gsum[...] = jnp.zeros_like(gsum)
            esum[...] = jnp.zeros_like(esum)

        block = info[14 + step]
        at = pl.multiple_of(block * units, 128)
        w_up = up[:, pl.ds(at, units)]
        w_down = down[pl.ds(at, units), :]
        bias_now = bias[pl.ds(block, 1)][0]
        act, slope = gelu_parts(dot(bs[...], w_up) + bias_now)
        low = act.astype(bf16)
        esum[...] += dot(low, w_down)
        rdown = dot(low, ss[...], 0, 0)
        grad_low = (dot(ss[...], w_down, 1, 1) * slope).astype(bf16)
        total = jnp.sum(grad_low.astype(f32), axis=0, keepdims=True)
        grad[...] = dot(bs[...], grad_low, 0, 0)
        gsum[...] += dot(grad_low, w_up, 1, 1)
        line[pl.ds(block, 1)] = total[None]
        for r in range(pairs):
            for j in range(2):
                row = pl.multiple_of(info[18 + 2 * r + j] * piece, piece)
                value = grad[pl.ds(row, piece), :]
                if r % 2 == 1:
                    us[r // 2, j * piece : (j + 1) * piece, pl.ds(at, units)] = value.astype(bf16)
                else:
                    uk[r // 2, j * piece : (j + 1) * piece, pl.ds(at, units)] = value

            @pl.when(step == r)
            def _():
                if r % 2 == 1:
                    ds[r // 2] = rdown.astype(bf16)
                else:
                    dk[r // 2] = rdown

        @pl.when(step == pairs - 1)
        def _():
            g0[...] = gsum[:count, :]
            g1[...] = gsum[count:, :].astype(bf16)
            e0[...] = esum[:count, :]
            e1[...] = esum[count:, :].astype(bf16)

    outs = [
        shape((2, units, width), bf16),
        shape((2, units, width), f32),
        shape((2, 2 * piece, every), bf16),
        shape((2, 2 * piece, every), f32),
        shape((count, width), f32),
        shape((count, width), bf16),
        shape((count, width), f32),
        shape((count, width), bf16),
        shape((pairs, 1, units), f32),
    ]
    operands = [*buffers, *slots, *ups, *downs, bias]
    return kernel_call(
        body,
        pairs,
        [SCALARS] + [full(o.shape) for o in operands],
        [full(o.shape) for o in outs],
        outs,
        [
            pltpu.VMEM((width, every), bf16),
            pltpu.VMEM((every, width), bf16),
            pltpu.VMEM((width, units), f32),
            pltpu.VMEM((2 * count, width), f32),
            pltpu.VMEM((2 * count, width), f32),
            pltpu.VMEM((2 * count, width), bf16),
            pltpu.VMEM((2 * count, width), bf16),
        ],
        24 * count * width * every,
        [info, *operands],
    )


def tail_grads(info, tokens, hidden, grads, attended, grad_attn, qkv):
    total, width = hidden.shape
    wide = grads.shape[1]
    blocks, rows, _ = tokens.shape
    cols = width // blocks
    piece = width // 8

    def body(info, tok, hid, gr, att, ga, qkv, out, send, keep, sums, lines, proj):
        out_qkv = dot(hid[...], gr[...], 0, 0).astype(bf16)
        for m in range(blocks):
            these = slice(m * rows, (m + 1) * rows)
            grad = dot(gr[these, :], qkv[...], 1, 1)
            if m % 2 == 1:
                send[m // 2] = grad.astype(bf16)
            else:
                keep[m // 2] = grad
            normed, _ = norm_parts(tok[m].astype(f32))
            sums[m : m + 1, :] = jnp.sum(grad, axis=0, keepdims=True)
            sums[blocks + m : blocks + m + 1, :] = jnp.sum(grad * normed, axis=0, keepdims=True)
        lines[:, :wide] = jnp.sum(gr[...].astype(f32), axis=0, keepdims=True)
        lines[:, wide:] = jnp.sum(ga[...].astype(f32), axis=0, keepdims=True)
        own = ga[:, :cols]
        for k in range(1, blocks):
            own = jnp.where(info[8] == k, ga[:, k * cols : (k + 1) * cols], own)
        proj[...] = dot(att[...], own, 0, 0)
        for d in range(8):
            out[d, :, :wide] = out_qkv[d * piece : (d + 1) * piece, :]
            at = ((d // 2) ^ info[8]) * cols + (d % 2) * piece
            at = pl.multiple_of(at, piece)
            out[d, :, wide:] = proj[pl.ds(at, piece), :].astype(bf16)

    return kernel_call(
        body,
        1,
        [SCALARS, pl.BlockSpec((blocks, rows, width), lambda i: (0, 0, 0))]
        + [full((total, width)), full((total, wide)), full((total, width))]
        + [full((total, width)), full((width, wide))],
        [
            full((8, piece, width)),
            full((2, rows, width)),
            full((2, rows, width)),
            full((2 * blocks, width)),
            full((1, wide + width)),
        ],
        [
            shape((8, piece, width), bf16),
            shape((2, rows, width), bf16),
            shape((2, rows, width), f32),
            shape((2 * blocks, width), f32),
            shape((1, wide + width), f32),
        ],
        [pltpu.VMEM((width, cols), f32)],
        2 * total * width * (2 * wide + cols),
        [info, tokens, hidden, grads, attended, grad_attn, qkv],
    )


def in_order(relative, position):
    return jnp.stack(
        [
            lax.dynamic_index_in_dim(relative, position ^ a, 0, keepdims=False)
            for a in range(relative.shape[0])
        ]
    )


def body(
    tokens,
    conditioning,
    routes,
    gate_weights,
    image_counts,
    image_lengths,
    cotangent,
    qkv_weight,
    qv_bias,
    proj_weight,
    proj_bias,
    ada_weight,
    ada_bias,
    up_weight,
    up_bias,
    down_weight,
    down_bias,
    routed_up,
    routed_upbias,
    routed_down,
    routed_downbias,
):
    group = lax.axis_size("expert")
    copies = lax.axis_size("dp")
    position = lax.axis_index("expert")
    place = lax.axis_index("dp")
    rows, width = tokens.shape
    group_rows = group * rows
    heads_own = HEADS // group
    cols_own = heads_own * HEAD_DIM
    d_rows = qkv_weight.shape[0]
    f_rows = down_weight.shape[0]
    f_own = f_rows // group
    hidden_units = f_rows * copies
    quarter = hidden_units // group
    side = lax.rem(place // 2, 2)
    first_side = side == 0
    pairs_count = copies // 2
    keep = f_rows * 2 // 3
    send = f_rows - keep
    half_units = hidden_units // 2

    def my_units(value):
        one, two = [], []
        for p in range(pairs_count):
            at, to = (d * f_rows for d in pair_places(p))
            one += [value[..., at : at + keep], value[..., to : to + send]]
            two += [value[..., to + send : to + f_rows], value[..., at + keep : at + f_rows]]
        one, two = jnp.concatenate(one, axis=-1), jnp.concatenate(two, axis=-1)
        return jnp.where(first_side, one, two), jnp.where(first_side, two, one)

    def from_units(mine, theirs):
        one = jnp.where(first_side, mine, theirs)
        two = jnp.where(first_side, theirs, mine)
        out = [None] * copies
        for p in range(pairs_count):
            at = f_rows * p
            first, second = pair_places(p)
            out[first] = [one[..., at : at + keep], two[..., at + keep : at + f_rows]]
            out[second] = [one[..., at + keep : at + f_rows], two[..., at : at + keep]]
        out = sum(out, [])
        return jnp.concatenate(out, axis=-1)

    bias_list = [up_bias, routed_upbias[0], qv_bias, proj_bias, down_bias, routed_downbias[0]]
    if copies == 8:
        first_share, third_share, rup_mine, rup_theirs, rdown_mine, rdown_theirs = prepare(
            jnp.stack([position] * 9 + [side]).astype(jnp.int32),
            proj_weight,
            qkv_weight,
            [b[None] for b in bias_list],
            up_weight,
            down_weight,
            routed_up[0],
            routed_down[0],
            keep,
            group,
        )
    else:
        qkv_share = lax.dynamic_index_in_dim(
            qkv_weight.reshape(d_rows, 3, group, cols_own), position, 2, keepdims=False
        ).reshape(d_rows, 3 * cols_own)
        first_share = qkv_share
        up_share = lax.dynamic_index_in_dim(
            up_weight.reshape(d_rows, copies, group, f_own), position, 2, keepdims=False
        ).reshape(d_rows, quarter)
        down_share = lax.dynamic_slice_in_dim(down_weight, position * f_own, f_own, axis=0)
        third_share = jnp.concatenate([up_share, down_share, proj_weight], axis=0)
        rup_mine, rup_theirs = my_units(routed_up[0])
        rdown_mine = lax.dynamic_slice_in_dim(routed_down[0], side * send, keep, axis=0)
        rdown_theirs = lax.dynamic_slice_in_dim(routed_down[0], (1 - side) * keep, send, axis=0)
    rup_got = pair_swap(rup_theirs)
    rdown_got = pair_swap(rdown_theirs)
    first, order = ring_gather(first_share)
    bias_three = jnp.zeros((1, 3 * cols_own), f32)
    if copies > 8:
        upb, rupb, qvb, projb, downb, rdownb = (
            lax.all_gather(b, "dp", axis=0, tiled=True).astype(f32) for b in bias_list
        )
        upb_own = lax.dynamic_index_in_dim(
            upb.reshape(copies, group, f_own), position, 1, keepdims=False
        ).reshape(quarter)
        bias_lines = jnp.stack([upb_own, projb, downb, rdownb])
        rupb_own = my_units(rupb)[0].reshape(4, 1, half_units // 4)
        bias_three = jnp.concatenate(
            [
                lax.dynamic_slice_in_dim(qvb, position * cols_own, cols_own),
                jnp.zeros((cols_own,), f32),
                lax.dynamic_slice_in_dim(qvb, width + position * cols_own, cols_own),
            ]
        )[None]

    pair_steps = jnp.arange(4, dtype=jnp.int32)
    if copies == 8:
        third = spread(tied(jnp.stack([third_share, pair_swap(third_share)]), *first[3:5]))
        downs = spread(tied(jnp.concatenate([rdown_mine, rdown_got]), third[2]))
        ups = spread(tied(jnp.stack([rup_mine, rup_got]), downs[2]))
        pair_now = (place >> 2) * 2 + (place & 1)
        unit_blocks = pair_now ^ pair_steps
        masks = jnp.array([0, 2, 1, 3, 4, 6, 5, 7], jnp.int32)
        row_blocks = place ^ masks
    else:
        groups = side_groups(copies)
        whole = lax.all_gather(third_share, "dp", axis=0)
        third = jnp.concatenate(
            [
                whole[:, :d_rows].reshape(8, -1, width),
                whole[:, d_rows : d_rows + f_own].reshape(8, -1, width),
                whole[:, d_rows + f_own :].reshape(8, -1, width),
            ],
            axis=1,
        ).reshape(4, 2, -1, width)
        sided = jnp.where(
            first_side, jnp.stack([rup_mine, rup_got]), jnp.stack([rup_got, rup_mine])
        )
        ups = lax.all_gather(sided, "dp", axis=0, axis_index_groups=groups)
        ups = ups.reshape(pairs_count // 2, 2, 2, d_rows, half_units).transpose(0, 2, 1, 3, 4)
        ups = ups.reshape(4, 2, width // 8, half_units)
        downs = lax.all_gather(
            jnp.concatenate([rdown_mine, rdown_got]), "dp", axis=0, axis_index_groups=groups
        ).reshape(4, half_units // 4, width)
        third, ups, downs = ([v[r] for r in range(4)] for v in (third, ups, downs))
        unit_blocks = pair_steps
        row_blocks = jnp.arange(8, dtype=jnp.int32)

    def by_side(whole):
        out = whole.reshape(pairs_count // 2, 2, 2, d_rows, -1).transpose(1, 0, 2, 3, 4)
        return out.reshape(2, 4, width // 8, -1)

    both = gather_group(jnp.concatenate([tokens, cotangent], axis=1))
    pairs = gather_group(jnp.concatenate([routes.astype(f32).T, gate_weights.T], axis=0))

    lengths = image_lengths[0]
    image_total = image_counts[0]
    slots = lengths.shape[0]
    slot_ids = jnp.arange(slots, dtype=jnp.int32)
    starts = jnp.sum(
        jnp.where(slot_ids[None, :] < slot_ids[:, None], lengths[None, :], 0), axis=1
    )
    live = (slot_ids >= 1) & (slot_ids < image_total)
    block_ids = position ^ jnp.arange(group, dtype=jnp.int32)
    segment = jnp.sum(
        (live[None, :] & (starts[None, :] <= (block_ids * rows)[:, None])).astype(jnp.int32),
        axis=1,
    )
    block_hot = segment[:, None] == slot_ids[None, :]

    info = jnp.concatenate(
        [
            order,
            jnp.stack([position, side]),
            segment,
            unit_blocks,
            row_blocks,
            jnp.zeros((6,), jnp.int32),
        ]
    ).astype(jnp.int32)

    cond_value = conditioning[0].astype(f32)
    cond_act = jax.nn.silu(cond_value).astype(bf16)
    act_parts = lax.all_to_all(
        cond_act.reshape(slots, copies, d_rows).transpose(1, 0, 2),
        "dp",
        split_axis=0,
        concat_axis=0,
        tiled=True,
    ).reshape(copies * slots, d_rows)
    mod_width = ada_weight.shape[1]
    mod_own = mod_width // group
    bias_line = lax.dynamic_update_slice(
        jnp.zeros((mod_width,), f32), ada_bias.astype(f32), (place * ada_bias.shape[0],)
    )
    ada_own = lax.dynamic_slice_in_dim(ada_weight, position * mod_own, mod_own, axis=1)
    bias_own = lax.dynamic_slice_in_dim(bias_line, position * mod_own, mod_own)
    mod_parts = (mm("sd,dm->sm", tied(act_parts, *first[1:3]), ada_own) + bias_own[None]).reshape(
        copies, slots, mod_own
    )
    mod_got = lax.all_to_all(mod_parts, "dp", split_axis=0, concat_axis=0, tiled=True)
    mod_sum = jnp.sum(tied(mod_got, *first[3:5]), axis=0)
    mod_across = tied(swap(mod_sum, 2), *first[5:7])
    mod_beside = swap(jnp.stack([mod_sum, mod_across]), 1)
    mod_group = jnp.stack([mod_sum, mod_beside[0], mod_across, mod_beside[1]])
    modulation = in_order(mod_group, position).transpose(1, 0, 2).reshape(slots, mod_width)
    per_block = jnp.sum(
        jnp.where(block_hot[:, :, None], modulation[None, :, :], 0.0), axis=1
    )
    mods = jnp.pad(per_block.reshape(group, 6, width), ((0, 0), (0, 2), (0, 0)))
    shift_a, scale_a, gate_a, shift_b, scale_b, gate_b = (mods[0, i : i + 1] for i in range(6))

    (
        hidden_a,
        projected,
        qkv_own,
        table,
        gates,
        grad_comb_low,
        slot_own,
        sums_f,
        lines_got,
        units_got,
    ) = front(
        info,
        both,
        mods,
        bias_three,
        pairs,
        first,
        width // 8,
        cols_own,
        keep if copies == 8 else 0,
    )
    if copies == 8:
        bias_lines, rupb_own = lines_got, units_got
    upb_line, projb_line, downb_line, rdownb_line = (bias_lines[i : i + 1] for i in range(4))
    slot_got = pair_swap(slot_own)
    heads_0 = attention(info, tied(projected, third[1], third[2]), group, cols_own)
    heads_2 = swap(heads_0, 2)
    heads_1 = swap(heads_0, 1)
    heads_3 = swap(heads_2, 1)
    hidden_b, attended, buffer_own, attn_out, residual_mid, proj_own = middle(
        info,
        both,
        mods,
        (heads_0, heads_1, heads_2, heads_3),
        third,
        projb_line,
        tied(table, downs[1], downs[2]),
        width // 8,
    )
    buffer_got = pair_swap(buffer_own)

    shared_parts, shared_back, shared_mine, shared_theirs, upbias_line = shared_expert(
        info, tied(hidden_b, ups[1]), grad_comb_low, upb_line, third, width // 8, group, copies == 8
    )
    if copies != 8:
        sided = jnp.concatenate([by_side(shared_mine[0]), by_side(shared_mine[1])], axis=2)
        shared_mine, shared_theirs = (
            lax.dynamic_index_in_dim(sided, which, 0, keepdims=False) for which in (side, 1 - side)
        )
        shared_theirs = shared_theirs.astype(bf16)
    shared_sums = shared_mine + pair_swap(shared_theirs).astype(f32)
    (
        down_send,
        down_keep,
        up_send,
        up_keep,
        back_own,
        back_theirs,
        out_own,
        out_theirs,
        units_sum,
    ) = routed_expert(
        info,
        (tied(buffer_own, shared_theirs), buffer_got),
        (slot_own, slot_got),
        ups,
        downs,
        rupb_own,
    )
    units_sum = units_sum.reshape(pairs_count, f_rows)
    blank = jnp.zeros((pairs_count, f_rows), f32)
    units_one = jnp.where(first_side, units_sum, blank)
    units_two = jnp.where(first_side, blank, units_sum)
    units_by_place = jnp.stack(
        [
            jnp.concatenate([units_one[:, :keep], units_two[:, keep:]], axis=1),
            jnp.concatenate([units_one[:, keep:], units_two[:, :keep]], axis=1),
        ]
    )
    units_by_place = units_by_place.reshape(2, pairs_count // 2, 2, f_rows).transpose(1, 0, 2, 3)
    expert_line = jnp.concatenate(
        [
            units_by_place.reshape(copies, f_rows),
            upbias_line.reshape(copies, f_own),
            sums_f[0].reshape(copies, d_rows),
            sums_f[1].reshape(copies, d_rows),
        ],
        axis=1,
    )
    zero_line = jnp.zeros((1, width), f32)
    rows_send, rows_keep, _ = to_rows(
        back_own,
        pair_swap(back_theirs),
        zero_line,
        table,
        jnp.ones((group, rows, 1), f32),
        shared_back,
        both,
        zero_line,
    )
    back_near, back_got = reduce_group(rows_send, rows_keep)
    grad_mid, grad_attn_own, sums_b = middle_back(
        back_near, back_got, residual_mid, attn_out, cotangent, mods
    )
    attn_2 = swap(grad_attn_own, 2)
    grad_attn = jnp.concatenate(
        [grad_attn_own, swap(grad_attn_own, 1), attn_2, swap(attn_2, 1)]
    )

    grad_projected = attention_back(info, projected, grad_attn, proj_own, group, cols_own)
    last_parts, back_send, back_keep, sums_a, lines = tail_grads(
        info, both, hidden_a, grad_projected, attended, grad_attn, qkv_own
    )
    last_sums = jnp.sum(
        lax.all_to_all(
            last_parts.reshape(copies, d_rows, width), "dp", split_axis=0, concat_axis=0, tiled=True
        ).astype(f32),
        axis=0,
    )
    if copies == 8:
        end = (last_parts,)
        rdown_sums, down_got = collect(down_send, down_keep, (), (grad_attn_own,), end)
        rup_sums, up_got = collect(up_send, up_keep, (down_got,), (grad_projected,), end)
        shared_rows, _ = collect(
            jnp.stack([shared_sums[1], shared_sums[3]]).astype(bf16),
            (shared_sums[0], shared_sums[2]),
            (up_got,),
            (grad_projected,),
            end,
        )
    else:

        def scatter(value, each):
            return lax.psum_scatter(
                value.reshape(pairs_count, each, -1).astype(bf16),
                "dp",
                scatter_dimension=0,
                axis_index_groups=side_groups(copies),
                tiled=False,
            )

        def whole_of(send, keep):
            send = send.astype(f32)
            return jnp.stack([keep[0], send[0], keep[1], send[1]])

        shared_rows = jnp.concatenate(
            [scatter(shared_sums[:, : width // 8], d_rows), scatter(shared_sums[:, width // 8 :], f_own)]
        )
        rdown_sums = scatter(whole_of(down_send, down_keep), f_rows)
        sided = by_side(whole_of(up_send, up_keep))
        rup_sums = jnp.concatenate(
            [
                scatter(lax.dynamic_index_in_dim(sided, which, 0, keepdims=False), d_rows)
                for which in (side, 1 - side)
            ]
        )

    lines = lines[0]
    qv_line = lax.dynamic_update_slice(
        jnp.zeros((2 * width,), f32), lines[:cols_own], (position * cols_own,)
    )
    qv_line = lax.dynamic_update_slice(
        qv_line, lines[2 * cols_own : 3 * cols_own], (width + position * cols_own,)
    ).reshape(copies, -1)
    pb_line = lines[3 * cols_own :].reshape(copies, d_rows)
    count_own = sums_f[2, 0]
    count_high = jnp.floor(count_own / 128.0)
    count_line = jnp.broadcast_to(
        jnp.stack([count_high, count_own - 128.0 * count_high])[None], (copies, 2)
    )
    line = jnp.concatenate([expert_line, qv_line, pb_line, count_line], axis=1)
    line_width = -(-line.shape[1] // (slots * 128)) * 128
    line = jnp.pad(line, ((0, 0), (0, slots * line_width - line.shape[1]))).reshape(
        copies, slots, line_width
    )

    rows_send, rows_keep, sums_out = to_rows(
        tied(out_own, last_parts),
        pair_swap(tied(out_theirs, grad_attn_own)),
        rdownb_line,
        table,
        gates,
        shared_parts,
        both,
        downb_line,
    )
    combined_near, combined_got = reduce_group(rows_send, rows_keep)
    combined = combined_near + combined_got.astype(f32) + downb_line
    output = (residual_mid + gate_b * combined).astype(bf16)

    block_of = block_hot.astype(f32)
    sums_all = jnp.concatenate(
        [
            sums_a[:group],
            sums_a[group:],
            jnp.pad(sums_b[:3].reshape(1, 3 * width), ((0, group - 1), (0, 0))),
            sums_out.reshape(group, width),
        ],
        axis=1,
    )
    slot_sums = jnp.sum(block_of[:, :, None] * sums_all[:, None, :], axis=0)
    slot_sums = slot_sums + swap(slot_sums, 1)
    slot_sums = slot_sums + swap(slot_sums, 2)
    grad_modulation = slot_sums.astype(bf16)
    mod_got = lax.all_to_all(
        jnp.concatenate(
            [
                jnp.broadcast_to(grad_modulation[None], (copies, slots, mod_width)),
                line.astype(bf16),
            ],
            axis=2,
        ),
        "dp",
        split_axis=0,
        concat_axis=0,
        tiled=True,
    )
    mod_all = mod_got[:, :, :mod_width].reshape(copies * slots, mod_width)
    line_sums = jnp.sum(mod_got[:, :, mod_width:].astype(f32), axis=0).reshape(-1)
    ada_grad = mm("sd,sm->dm", act_parts, mod_all)
    adabias_grad = jnp.sum(
        lax.dynamic_slice_in_dim(
            mod_all, place * ada_bias.shape[0], ada_bias.shape[0], axis=1
        ).astype(f32),
        axis=0,
    )
    cond_parts = mm("sm,dm->sd", mod_all, ada_weight).reshape(copies, slots, d_rows)
    grad_cond_act = (
        lax.all_to_all(cond_parts, "dp", split_axis=0, concat_axis=0, tiled=True)
        .transpose(1, 0, 2)
        .reshape(slots, width)
    )
    sigmoid_cond = jax.nn.sigmoid(cond_value)
    conditioning_grad = (grad_cond_act * sigmoid_cond * (1.0 + cond_value * (1.0 - sigmoid_cond)))[
        None
    ]

    near_a, got_a = reduce_group(back_send, back_keep)
    grad_hidden_a = near_a + got_a.astype(f32)
    normed_a, inv_std_a = norm_parts(tokens.astype(f32))
    tokens_grad = grad_mid + norm_back(grad_hidden_a * (1.0 + scale_a), normed_a, inv_std_a)

    rup_got = pair_swap(rup_sums[d_rows:].astype(bf16))
    rdown_got = pair_swap(rdown_sums[keep:].astype(bf16))
    shared_all = gather_group(shared_rows.astype(bf16))
    last_all = gather_group(last_sums.astype(bf16))
    if copies == 8:
        rup_rows, rdown_rows = routed_rows(info, rup_sums, rup_got, rdown_sums, rdown_got, keep)
        up_rows, down_rows, qkv_rows, proj_rows = group_rows_out(
            info, shared_all, last_all, d_rows, f_rows
        )
    else:
        rup_rows = from_units(rup_sums[:d_rows].astype(f32), rup_got.astype(f32))
        kept, back = rdown_sums[:keep].astype(f32), rdown_got.astype(f32)
        rdown_rows = jnp.where(
            first_side, jnp.concatenate([kept, back]), jnp.concatenate([back, kept])
        )
        shared_all, last_all = (
            in_order(v, position).astype(f32) for v in (shared_all, last_all)
        )
        up_rows = (
            shared_all[:, :d_rows]
            .reshape(group, d_rows, copies, f_own)
            .transpose(1, 2, 0, 3)
            .reshape(d_rows, hidden_units)
        )
        down_rows = shared_all[:, d_rows:].reshape(f_rows, width)
        qkv_rows = (
            last_all[:, :, : 3 * cols_own]
            .reshape(group, d_rows, 3, cols_own)
            .transpose(1, 2, 0, 3)
            .reshape(d_rows, 3 * width)
        )
        proj_rows = last_all[:, :, 3 * cols_own :].transpose(1, 0, 2).reshape(d_rows, width)
    cuts = [f_rows, f_own, d_rows, d_rows, 2 * width // copies, d_rows, 2]
    at = [sum(cuts[:i]) for i in range(len(cuts))]
    rupbias_row, upbias_sum, rdownbias_row, downbias_row, qvbias_sum, projbias_row, counts = (
        line_sums[o : o + n] for o, n in zip(at, cuts)
    )
    small = in_order(
        gather_group(jnp.concatenate([upbias_sum, qvbias_sum, counts])[None]), position
    )[:, 0]
    upbias_rows = small[:, :f_own].reshape(f_rows)
    qvbias_rows = jnp.sum(small[:, f_own:-2], axis=0)
    expert_counts = (128.0 * small[:, -2] + small[:, -1]).astype(jnp.int32)

    return (
        output,
        tokens_grad,
        conditioning_grad,
        qkv_rows,
        qvbias_rows,
        proj_rows,
        projbias_row,
        ada_grad,
        adabias_grad,
        up_rows,
        upbias_rows,
        down_rows,
        downbias_row,
        rup_rows[None],
        rupbias_row[None],
        rdown_rows[None],
        rdownbias_row[None],
        expert_counts,
    )


def solution(mesh):
    in_specs = (
        P(("dp", "expert"), None),
        P("dp", None, None),
        P(("dp", "expert"), None),
        P(("dp", "expert"), None),
        P("dp"),
        P("dp", None),
        P(("dp", "expert"), None),
        P("dp", None),
        P("dp"),
        P("dp", None),
        P("dp"),
        P("dp", None),
        P("dp"),
        P("dp", None),
        P("dp"),
        P("dp", None),
        P("dp"),
        P("expert", "dp", None),
        P("expert", "dp"),
        P("expert", "dp", None),
        P("expert", "dp"),
    )
    out_specs = (
        P(("dp", "expert"), None),
        P(("dp", "expert"), None),
        P("dp", None, None),
        P("dp", None),
        P("dp"),
        P("dp", None),
        P("dp"),
        P("dp", None),
        P("dp"),
        P("dp", None),
        P("dp"),
        P("dp", None),
        P("dp"),
        P("expert", "dp", None),
        P("expert", "dp"),
        P("expert", "dp", None),
        P("expert", "dp"),
        P(),
    )
    return jax.shard_map(body, mesh=mesh, in_specs=in_specs, out_specs=out_specs, check_vma=False)
```

time: 695 us -> 436 us (0.63)
  waiting for transfers between devices: 371 us -> 150 us
  Pallas kernels: 0 us -> 126 us
  matrix products: 92.7 us -> 2.2 us
  local copies, waits for them, and re-layouts: 82.7 us -> 28 us
  other arithmetic: 89.5 us -> 40.8 us
  starting transfers between devices: 35.1 us -> 80.6 us
  between operations: 16.5 us -> 4 us
    reduce_scatter x3 -> x0, waiting for transfers between devices: 188 us -> none  [scatter(): return lax.psum_scatter(value, 'dp', scatter_dimension=0, tiled=False)]
    pallas_call x0 -> x13, Pallas kernels: none -> 126 us  [kernel_call(): pl.pallas_call(body, grid=(grid,), in_specs=in_specs, out_specs=out_specs...]
    ppermute x0 -> x32, waiting for transfers between devices: none -> 115 us  [the longest x25 115 us: dp_swap(): return lax.ppermute(value, 'dp', [(i, i ^ mask) for i in range(copies)])]
    dot_general x31 -> x3, matrix products: 90.8 us -> 2.2 us  [mm(): return jnp.einsum(spec, a, b, preferred_element_type=f32)]
    all_gather x2 -> x0, waiting for transfers between devices: 85.1 us -> none  [the longest x1 85.1 us: body(): second_all = lax.all_gather(second_share, 'dp', axis=0)]
    ppermute x0 -> x32, starting transfers between devices: none -> 47.7 us  [the longest x25 38.7 us: dp_swap(): return lax.ppermute(value, 'dp', [(i, i ^ mask) for i in range(copies)])]
    ppermute x22 -> x26, waiting for transfers between devices: 57 us -> 21.3 us  [swap(): return lax.ppermute(value, 'expert', [(i, i ^ mask) for i in range(size)])]
    concatenate x5 -> x6, other arithmetic: 21.3 us -> 1.01 us  [the longest x1 0.86 us: body(): jnp.concatenate([jnp.broadcast_to(grad_modulation[None], (copies, slots,...]
  transfers between devices with their start and end apart: 31 -> 63, of which waited for: 19 -> 23; matrix products, arithmetic and copies ran while one was open for 22% -> 13% of each run, Pallas kernels for 0% -> 20%
where the time goes in v2:
time: 436 us; the launch traced here: 432 us
  waiting for transfers between devices  150 us (34%)
  Pallas kernels  126 us (29%)
  starting transfers between devices  80.6 us (18%)
  other arithmetic  40.8 us (9%)
  local copies, waits for them, and re-layouts  28 us (6%)
    pallas_call x13, Pallas kernels, kernel_call(): pl.pallas_call(body, grid=(grid,), in_specs=in_specs, out_specs=out_specs...  126 us
    ppermute x25, waiting for transfers between devices, dp_swap(): return lax.ppermute(value, 'dp', [(i, i ^ mask) for i in range(copies)])  115 us
    ppermute x25, starting transfers between devices, dp_swap(): return lax.ppermute(value, 'dp', [(i, i ^ mask) for i in range(copies)])  38.7 us
    ppermute x26, waiting for transfers between devices, swap(): return lax.ppermute(value, 'expert', [(i, i ^ mask) for i in range(size)])  21.3 us
    ppermute x26, starting transfers between devices, swap(): return lax.ppermute(value, 'expert', [(i, i ^ mask) for i in range(size)])  12.7 us
    unnamed x132, local copies, waits for them, and re-layouts  9.65 us
    ppermute x7, starting transfers between devices, hop(): lax.ppermute(value, 'dp', [(ring[i], ring[(i + way) % copies]) for i in r...  8.95 us
  transfers between devices with their start and end apart: 63, of which 23 were waited for; matrix products, arithmetic and copies ran while one was open for 13% of the time, Pallas kernels for 20%

profile of v2, /device:TPU:0, one launch (start us, length us, event | category | flops | bytes accessed | tf_op | source)
XLA Modules:
  0.0 431.8 jit_solution(9033188388376238481)
XLA Ops:
  13.2 5.8 %all-to-all-start = ((bf16[8,4,96]{2,1,0:T(4,128)(2,1)}), bf16[8,4,96]{2,1,0:T(4,128)(2,1)S(1)}, u32[]{:S(2)}, u32[]{:S(2)}) async-start(bf16[8,4,96]{2,1,0:T(4,128)(2,1)} %copy.78), calls=%async_computation | async-start | bytes 16384 | tf_op jit(solution)/shard_map/all_to_all | solution.py:1097
  34.7 5.6 %all-to-all-done.1 = f32[8,4,1152]{2,1,0:T(4,128)S(1)} async-done(((f32[8,4,1152]{2,1,0:T(4,128)}), f32[8,4,1152]{2,1,0:T(4,128)S(1)}, u32[]{:S(2)}, u32[]{:S(2)}) %all-to-all-start.1) | async-done | bytes 147488 | tf_op jit(solution)/shard_map/all_to_all | solution.py:1114
  46.3 6.1 %collective-permute-done.13 = bf16[288,768]{1,0:T(8,128)(2,1)S(1)} collective-permute-done((bf16[288,768]{1,0:T(8,128)(2,1)}, bf16[288,768]{1,0:T(8,128)(2,1)S(1)}, u32[]{:S(2)}, u32[]{:S(2)}) %collective-permute-start.13) | collective-permute-done | bytes 442400 | tf_op jit(solution)/shard_map/ppermute | solution.py:66
  61.6 7.3 %shard_map.359 = (bf16[1024,768]{1,0:T(8,128)(2,1)}, bf16[1024,576]{1,0:T(8,128)(2,1)}, bf16[768,576]{1,0:T(8,128)(2,1)}, bf16[4,128,256]{2,1,0:T(8,128)(2,1)}, ...) custom-call(s32[32]{0:T(128)} %concatenate.38.info, ...), custom_call_target="tpu_custom_call" | custom-call | flops 905969664 | bytes 10613120 | tf_op jit(solution)/shard_map/pallas_call | solution.py:148
  69.0 20.5 %collective-permute-done.15.refs_2_ = bf16[2,288,768]{2,1,0:T(8,128)(2,1)} collective-permute-done((bf16[2,288,768]{2,1,0:T(8,128)(2,1)S(1)}, bf16[2,288,768]{2,1,0:T(8,128)(2,1)}, u32[]{:S(2)}, u32[]{:S(2)}) %collective-permute-start.15) | collective-permute-done | bytes 884768 | tf_op jit(solution)/shard_map/ppermute | solution.py:66
  89.4 10.7 %shard_map.360.h0 = bf16[1024,192]{1,0:T(8,128)(2,1)} custom-call(s32[32]{0:T(128)} %concatenate.38.info, bf16[1024,576]{1,0:T(8,128)(2,1)} %get-tuple-element.100.own.every, bf16[1024,576]{1,0:T(8,128)(2,1)} %get-tuple-element.100.own.every), custom_call_target="tpu_custom_call" | custom-call | flops 805306368 | bytes 2752640 | tf_op jit(solution)/shard_map/pallas_call | solution.py:148
  108.1 11.7 %collective-permute-done.23 = bf16[96,1536]{1,0:T(8,128)(2,1)S(1)} collective-permute-done((bf16[96,1536]{1,0:T(8,128)(2,1)S(1)}, bf16[96,1536]{1,0:T(8,128)(2,1)S(1)}, u32[]{:S(2)}, u32[]{:S(2)}) %collective-permute-start.23) | collective-permute-done | bytes 294944 | tf_op jit(solution)/shard_map/ppermute | solution.py:66
  120.3 8.8 %collective-permute-done.21.refs_6_ = bf16[384,768]{1,0:T(8,128)(2,1)S(1)} collective-permute-done((bf16[384,768]{1,0:T(8,128)(2,1)S(1)}, bf16[384,768]{1,0:T(8,128)(2,1)S(1)}, u32[]{:S(2)}, u32[]{:S(2)}) %collective-permute-start.21) | collective-permute-done | bytes 589856 | tf_op jit(solution)/shard_map/ppermute | solution.py:66
  136.5 4.8 %collective-permute-start.26 = (bf16[512,768]{1,0:T(8,128)(2,1)}, bf16[512,768]{1,0:T(8,128)(2,1)S(1)}, u32[]{:S(2)}, u32[]{:S(2)}) collective-permute-start(bf16[512,768]{1,0:T(8,128)(2,1)} %get-tuple-element.117.s0), channel_id=1, source_target_pairs={{0,8},{4,12},{8,0},{12,4},{16,24},{20,28},{24,16},{28,20},{1,9},{5... | collective-permute-start | bytes 2359304 | tf_op jit(solution)/shard_map/ppermute | solution.py:66
  141.3 9.2 %shard_map.361 = (bf16[1024,768]{1,0:T(8,128)(2,1)}, bf16[1024,768]{1,0:T(8,128)(2,1)}, bf16[512,768]{1,0:T(8,128)(2,1)}, f32[256,768]{1,0:T(8,128)}, f32[256,768]{1,0:T(8,128)}, /*index=5*/bf16[192,768]{1,0:T(8,128)(2,1)}) custom-call(s32[32]{0:T(128)} %concatenate.38.info, bf16[4,256,1536]{2,1,0:T(8,128)(2,1)} %pad_maximum_fusion.tok, ...), custom_call_target="tpu_custom_call" | custom-call | flops 1409286144 | bytes 14421120 | tf_op jit(solution)/shard_map/pallas_call | solution.py:148
  158.2 14.5 %shard_map.362 = (f32[1024,768]{1,0:T(8,128)}, f32[1024,768]{1,0:T(8,128)}, f32[4,192,768]{2,1,0:T(8,128)}, bf16[4,192,768]{2,1,0:T(8,128)(2,1)}, f32[1,768]{1,0:T(1,128)}) custom-call(s32[32]{0:T(128)} %concatenate.38.info, bf16[1024,768]{1,0:T(8,128)(2,1)} %get-tuple-element.113.hid, bf16[1024,768]{1,0:T(8,128)(2,1)} %get-tuple-element.114.gcl, ...), custom_call_target="tpu_custom_call" | custom-call | flops 7247757312 | bytes 16521344 | tf_op jit(solution)/shard_map/pallas_call | solution.py:148
  174.4 9.4 %collective-permute-done.25.b1 = bf16[512,768]{1,0:T(8,128)(2,1)S(1)} collective-permute-done((bf16[512,768]{1,0:T(8,128)(2,1)}, bf16[512,768]{1,0:T(8,128)(2,1)S(1)}, u32[]{:S(2)}, u32[]{:S(2)}) %collective-permute-start.25) | collective-permute-done | bytes 786464 | tf_op jit(solution)/shard_map/ppermute | solution.py:66
  184.6 30.6 %shard_map.363 = (bf16[2,384,768]{2,1,0:T(8,128)(2,1)}, f32[2,384,768]{2,1,0:T(8,128)}, bf16[2,192,1536]{2,1,0:T(8,128)(2,1)}, f32[2,192,1536]{2,1,0:T(8,128)}, ...) custom-call(s32[32]{0:T(128)} %concatenate.38.info, ...), custom_call_target="tpu_custom_call" | custom-call | flops 14495514624 | bytes 19673216 | tf_op jit(solution)/shard_map/pallas_call | solution.py:148
  221.9 14.0 %collective-permute-done.30.got = bf16[512,768]{1,0:T(8,128)(2,1)S(1)} collective-permute-done((bf16[512,768]{1,0:T(8,128)(2,1)}, bf16[512,768]{1,0:T(8,128)(2,1)S(1)}, u32[]{:S(2)}, u32[]{:S(2)}) %collective-permute-start.30) | collective-permute-done | bytes 786464 | tf_op jit(solution)/shard_map/ppermute | solution.py:66
  237.4 6.3 %shard_map.364 = (bf16[2,256,768]{2,1,0:T(8,128)(2,1)}, f32[2,256,768]{2,1,0:T(8,128)}, f32[4,1,768]{2,1,0:T(1,128)}) custom-call(f32[512,768]{1,0:T(8,128)} %get-tuple-element.121.own, bf16[512,768]{1,0:T(8,128)(2,1)} %copy-done.24, f32[1,768]{1,0:T(1,128)} %broadcast_in_dim.122.bias.line, bf16[4,128,256]{2,1,0:T(8,128)(2,1)} %get-tuple-element.106.tab, ...), custom_call_target="tpu_custom_call" | custom-call | flops 201326592 | bytes 11294720 | tf_op jit(solution)/shard_map/pallas_call | solution.py:148
  249.3 5.5 %collective-permute-done.43 = bf16[4,192,768]{2,1,0:T(8,128)(2,1)} collective-permute-done((bf16[4,192,768]{2,1,0:T(8,128)(2,1)}, bf16[4,192,768]{2,1,0:T(8,128)(2,1)}, u32[]{:S(2)}, u32[]{:S(2)}) %collective-permute-start.43) | collective-permute-done | bytes 1179680 | tf_op jit(solution)/shard_map/ppermute | solution.py:66
  266.9 7.8 %collective-permute-done.34 = bf16[256,768]{1,0:T(8,128)(2,1)S(1)} collective-permute-done((bf16[256,768]{1,0:T(8,128)(2,1)}, bf16[256,768]{1,0:T(8,128)(2,1)S(1)}, u32[]{:S(2)}, u32[]{:S(2)}) %collective-permute-start.34) | collective-permute-done | bytes 393248 | tf_op jit(solution)/shard_map/ppermute | solution.py:48
  279.1 18.3 %shard_map.366.gr = bf16[1024,576]{1,0:T(8,128)(2,1)} custom-call(s32[32]{0:T(128)} %concatenate.38.info, bf16[1024,576]{1,0:T(8,128)(2,1)} %get-tuple-element.100.own.every, bf16[1024,576]{1,0:T(8,128)(2,1)} %get-tuple-element.100.own.every, bf16[1024,768]{1,0:T(8,128)(2,1)} %copy-done.10, bf16[192,768]{1,0:T(8,128)(2,1)} %get-tuple-element.128.rel), custom_call_target="tpu_custom_call" | custom-call | flops 2315255808 | bytes 5406848 | tf_op jit(solution)/shard_map/pallas_call | solution.py:148
  297.4 9.0 %shard_map.367 = (bf16[8,96,768]{2,1,0:T(8,128)(2,1)}, bf16[2,256,768]{2,1,0:T(8,128)(2,1)}, f32[2,256,768]{2,1,0:T(8,128)}, f32[8,768]{1,0:T(8,128)}, f32[1,1344]{1,0:T(1,128)}) custom-call(s32[32]{0:T(128)} %concatenate.38.info, bf16[4,256,1536]{2,1,0:T(8,128)(2,1)} %pad_maximum_fusion.tok, bf16[1024,768]{1,0:T(8,128)(2,1)} %get-tuple-element.120.hid, ...), custom_call_target="tpu_custom_call" | custom-call | flops 2113929216 | bytes 13497728 | tf_op jit(solution)/shard_map/pallas_call | solution.py:148
  308.5 6.1 %shard_map.368 = (bf16[2,256,768]{2,1,0:T(8,128)(2,1)}, f32[2,256,768]{2,1,0:T(8,128)}, f32[4,1,768]{2,1,0:T(1,128)}) custom-call(f32[512,768]{1,0:T(8,128)} %get-tuple-element.132.own, bf16[512,768]{1,0:T(8,128)(2,1)} %copy-done.23, f32[1,768]{1,0:T(1,128)} %get-tuple-element.197.bias, bf16[4,128,256]{2,1,0:T(8,128)(2,1)} %get-tuple-element.106.tab, ...), custom_call_target="tpu_custom_call" | custom-call | flops 201326592 | bytes 11294720 | tf_op jit(solution)/shard_map/pallas_call | solution.py:148
  334.9 30.9 %collective-permute-done.47 = bf16[192,768]{1,0:T(8,128)(2,1)S(1)} collective-permute-done((bf16[192,768]{1,0:T(8,128)(2,1)S(1)}, bf16[192,768]{1,0:T(8,128)(2,1)S(1)}, u32[]{:S(2)}, u32[]{:S(2)}) %collective-permute-start.47) | collective-permute-done | bytes 294944 | tf_op jit(solution)/shard_map/ppermute | solution.py:66
  384.5 4.0 all-to-all-start.4
  406.4 4.3 collective-permute-done.38
  411.7 5.8 %all-to-all-done.4 = bf16[8,96,768]{2,1,0:T(8,128)(2,1)S(1)} async-done(((bf16[8,96,768]{2,1,0:T(8,128)(2,1)}), bf16[8,96,768]{2,1,0:T(8,128)(2,1)S(1)}, u32[]{:S(2)}, u32[]{:S(2)}) %all-to-all-start.4) | async-done | bytes 1179680 | tf_op jit(solution)/shard_map/all_to_all | solution.py:1241
  (396 shorter events, 171.0 us)
Async XLA Ops:
  19.6 82.0 %collective-permute-start.19 = (bf16[128,768]{1,0:T(8,128)(2,1)}, bf16[128,768]{1,0:T(8,128)(2,1)S(1)}, u32[]{:S(2)}, u32[]{:S(2)}) collective-permute-start(bf16[128,768]{1,0:T(8,128)(2,1)} %get-tuple-element.104), channel_id=1, source_target_pairs={{0,8},{4,12},{8,0},{12,4},{16,24},{20,28},{24,16},{28,20},{1,9},{5... | collective-permute-start | bytes 589832 | tf_op jit(solution)/shard_map/ppermute | solution.py:66
  52.5 37.0 %collective-permute-start.15 = (bf16[2,288,768]{2,1,0:T(8,128)(2,1)S(1)}, bf16[2,288,768]{2,1,0:T(8,128)(2,1)}, u32[]{:S(2)}, u32[]{:S(2)}) collective-permute-start(bf16[2,288,768]{2,1,0:T(8,128)(2,1)S(1)} %pad_maximum_fusion.3.refs_0_), channel_id=1, source_target_pairs={{0,16},{4,20},{8,24},{12,28},{16,0},{20,4},{24,8},{28,12},{1,17},{... | collective-permute-start | bytes 2654216 | tf_op jit(solution)/shard_map/ppermute | solution.py:66
  52.8 36.7 %collective-permute-start.14 = (bf16[2,288,768]{2,1,0:T(8,128)(2,1)S(1)}, bf16[2,288,768]{2,1,0:T(8,128)(2,1)}, u32[]{:S(2)}, u32[]{:S(2)}) collective-permute-start(bf16[2,288,768]{2,1,0:T(8,128)(2,1)S(1)} %pad_maximum_fusion.3.refs_0_), channel_id=1, source_target_pairs={{0,4},{4,0},{8,12},{12,8},{16,20},{20,16},{24,28},{28,24},{1,5},{5... | collective-permute-start | bytes 2654216 | tf_op jit(solution)/shard_map/ppermute | solution.py:66
  101.7 27.4 %collective-permute-start.21 = (bf16[384,768]{1,0:T(8,128)(2,1)S(1)}, bf16[384,768]{1,0:T(8,128)(2,1)S(1)}, u32[]{:S(2)}, u32[]{:S(2)}) collective-permute-start(bf16[384,768]{1,0:T(8,128)(2,1)S(1)} %pad_maximum_fusion.4.refs_4_), channel_id=1, source_target_pairs={{0,16},{4,20},{8,24},{12,28},{16,0},{20,4},{24,8},{28,12},{1,17},{... | collective-permute-start | bytes 1769480 | tf_op jit(solution)/shard_map/ppermute | solution.py:66
  101.8 27.3 %collective-permute-start.20 = (bf16[384,768]{1,0:T(8,128)(2,1)S(1)}, bf16[384,768]{1,0:T(8,128)(2,1)S(1)}, u32[]{:S(2)}, u32[]{:S(2)}) collective-permute-start(bf16[384,768]{1,0:T(8,128)(2,1)S(1)} %pad_maximum_fusion.4.refs_4_), channel_id=1, source_target_pairs={{0,4},{4,0},{8,12},{12,8},{16,20},{20,16},{24,28},{28,24},{1,5},{5... | collective-permute-start | bytes 1769480 | tf_op jit(solution)/shard_map/ppermute | solution.py:66
  104.7 31.8 %collective-permute-start.22 = (bf16[2,288,768]{2,1,0:T(8,128)(2,1)}, bf16[2,288,768]{2,1,0:T(8,128)(2,1)S(1)}, u32[]{:S(2)}, u32[]{:S(2)}) collective-permute-start(bf16[2,288,768]{2,1,0:T(8,128)(2,1)} %collective-permute-done.15.refs_2_), channel_id=1, source_target_pairs={{0,4},{4,0},{8,12},{12,8},{16,20},{20,16},{24,28},{28,24},{1,5},{5... | collective-permute-start | bytes 2654216 | tf_op jit(solution)/shard_map/ppermute | solution.py:66
  129.1 27.5 %collective-permute-start.27 = (bf16[2,96,1536]{2,1,0:T(8,128)(2,1)S(1)}, bf16[2,96,1536]{2,1,0:T(8,128)(2,1)}, u32[]{:S(2)}, u32[]{:S(2)}) collective-permute-start(bf16[2,96,1536]{2,1,0:T(8,128)(2,1)S(1)} %pad_maximum_fusion.5.refs_0_), channel_id=1, source_target_pairs={{0,16},{4,20},{8,24},{12,28},{16,0},{20,4},{24,8},{28,12},{1,17},{... | collective-permute-start | bytes 1769480 | tf_op jit(solution)/shard_map/ppermute | solution.py:66
  130.7 27.5 %collective-permute-start.24 = (bf16[2,96,1536]{2,1,0:T(8,128)(2,1)S(1)}, bf16[2,96,1536]{2,1,0:T(8,128)(2,1)}, u32[]{:S(2)}, u32[]{:S(2)}) collective-permute-start(bf16[2,96,1536]{2,1,0:T(8,128)(2,1)S(1)} %pad_maximum_fusion.5.refs_0_), channel_id=1, source_target_pairs={{0,4},{4,0},{8,12},{12,8},{16,20},{20,16},{24,28},{28,24},{1,5},{5... | collective-permute-start | bytes 1769480 | tf_op jit(solution)/shard_map/ppermute | solution.py:66
  136.5 37.9 %collective-permute-start.26 = (bf16[512,768]{1,0:T(8,128)(2,1)}, bf16[512,768]{1,0:T(8,128)(2,1)S(1)}, u32[]{:S(2)}, u32[]{:S(2)}) collective-permute-start(bf16[512,768]{1,0:T(8,128)(2,1)} %get-tuple-element.117.s0), channel_id=1, source_target_pairs={{0,8},{4,12},{8,0},{12,4},{16,24},{20,28},{24,16},{28,20},{1,9},{5... | collective-permute-start | bytes 2359304 | tf_op jit(solution)/shard_map/ppermute | solution.py:66
  150.5 33.3 %collective-permute-start.25 = (bf16[512,768]{1,0:T(8,128)(2,1)}, bf16[512,768]{1,0:T(8,128)(2,1)S(1)}, u32[]{:S(2)}, u32[]{:S(2)}) collective-permute-start(bf16[512,768]{1,0:T(8,128)(2,1)} %get-tuple-element.116.b0), channel_id=1, source_target_pairs={{0,8},{4,12},{8,0},{12,4},{16,24},{20,28},{24,16},{28,20},{1,9},{5... | collective-permute-start | bytes 2359304 | tf_op jit(solution)/shard_map/ppermute | solution.py:66
  215.5 28.7 %collective-permute-start.44 = (bf16[2,384,768]{2,1,0:T(8,128)(2,1)}, bf16[2,384,768]{2,1,0:T(8,128)(2,1)}, u32[]{:S(2)}, u32[]{:S(2)}) collective-permute-start(bf16[2,384,768]{2,1,0:T(8,128)(2,1)} %get-tuple-element.151), channel_id=1, source_target_pairs={{0,4},{4,0},{8,12},{12,8},{16,20},{20,16},{24,28},{28,24},{1,5},{5... | collective-permute-start | bytes 3538952 | tf_op jit(solution)/shard_map/ppermute | solution.py:66
  219.7 35.1 %collective-permute-start.43 = (bf16[4,192,768]{2,1,0:T(8,128)(2,1)}, bf16[4,192,768]{2,1,0:T(8,128)(2,1)}, u32[]{:S(2)}, u32[]{:S(2)}) collective-permute-start(bf16[4,192,768]{2,1,0:T(8,128)(2,1)} %get-tuple-element.115), channel_id=1, source_target_pairs={{0,8},{4,12},{8,0},{12,4},{16,24},{20,28},{24,16},{28,20},{1,9},{5... | collective-permute-start | bytes 3538952 | tf_op jit(solution)/shard_map/ppermute | solution.py:66
  244.2 31.9 %collective-permute-start.45 = (bf16[2,192,1536]{2,1,0:T(8,128)(2,1)}, bf16[2,192,1536]{2,1,0:T(8,128)(2,1)S(1)}, u32[]{:S(2)}, u32[]{:S(2)}) collective-permute-start(bf16[2,192,1536]{2,1,0:T(8,128)(2,1)} %get-tuple-element.152), channel_id=1, source_target_pairs={{0,4},{4,0},{8,12},{12,8},{16,20},{20,16},{24,28},{28,24},{1,5},{5... | collective-permute-start | bytes 3538952 | tf_op jit(solution)/shard_map/ppermute | solution.py:66
  265.2 42.4 %collective-permute-start.36 = (bf16[512,768]{1,0:T(8,128)(2,1)}, bf16[512,768]{1,0:T(8,128)(2,1)S(1)}, u32[]{:S(2)}, u32[]{:S(2)}) collective-permute-start(bf16[512,768]{1,0:T(8,128)(2,1)} %get-tuple-element.134), channel_id=1, source_target_pairs={{0,8},{4,12},{8,0},{12,4},{16,24},{20,28},{24,16},{28,20},{1,9},{5... | collective-permute-start | bytes 2359304 | tf_op jit(solution)/shard_map/ppermute | solution.py:66
  275.7 44.1 %collective-permute-start.56 = (bf16[384,768]{1,0:T(8,128)(2,1)}, bf16[384,768]{1,0:T(8,128)(2,1)}, u32[]{:S(2)}, u32[]{:S(2)}) collective-permute-start(bf16[384,768]{1,0:T(8,128)(2,1)} %fusion.31), channel_id=1, source_target_pairs={{0,16},{4,20},{8,24},{12,28},{16,0},{20,4},{24,8},{28,12},{1,17},{... | collective-permute-start | bytes 1769480 | tf_op jit(solution)/shard_map/ppermute | solution.py:66
  276.1 50.8 %collective-permute-start.46 = (bf16[2,192,768]{2,1,0:T(8,128)(2,1)S(1)}, bf16[2,192,768]{2,1,0:T(8,128)(2,1)S(1)}, u32[]{:S(2)}, u32[]{:S(2)}) collective-permute-start(bf16[2,192,768]{2,1,0:T(8,128)(2,1)S(1)} %pad_maximum_fusion.6), channel_id=1, source_target_pairs={{0,4},{4,0},{8,12},{12,8},{16,20},{20,16},{24,28},{28,24},{1,5},{5... | collective-permute-start | bytes 1769480 | tf_op jit(solution)/shard_map/ppermute | solution.py:66
  315.5 78.4 %collective-permute-start.37 = (bf16[2,256,768]{2,1,0:T(8,128)(2,1)}, bf16[2,256,768]{2,1,0:T(8,128)(2,1)}, u32[]{:S(2)}, u32[]{:S(2)}) collective-permute-start(bf16[2,256,768]{2,1,0:T(8,128)(2,1)} %get-tuple-element.138), channel_id=1, source_target_pairs={{0,1},{1,0},{2,3},{3,2},{4,5},{5,4},{6,7},{7,6},{8,9},{9,8},{10,11... | collective-permute-start | bytes 2359304 | tf_op jit(solution)/shard_map/ppermute | solution.py:48
  316.0 73.9 %collective-permute-start.39 = (bf16[2,256,768]{2,1,0:T(8,128)(2,1)}, bf16[2,256,768]{2,1,0:T(8,128)(2,1)}, u32[]{:S(2)}, u32[]{:S(2)}) collective-permute-start(bf16[2,256,768]{2,1,0:T(8,128)(2,1)} %get-tuple-element.141), channel_id=1, source_target_pairs={{0,1},{1,0},{2,3},{3,2},{4,5},{5,4},{6,7},{7,6},{8,9},{9,8},{10,11... | collective-permute-start | bytes 2359304 | tf_op jit(solution)/shard_map/ppermute | solution.py:48
  319.8 47.8 %collective-permute-start.54 = (bf16[192,1536]{1,0:T(8,128)(2,1)}, bf16[192,1536]{1,0:T(8,128)(2,1)}, u32[]{:S(2)}, u32[]{:S(2)}) collective-permute-start(bf16[192,1536]{1,0:T(8,128)(2,1)} %fusion.30), channel_id=1, source_target_pairs={{0,16},{4,20},{8,24},{12,28},{16,0},{20,4},{24,8},{28,12},{1,17},{... | collective-permute-start | bytes 1769480 | tf_op jit(solution)/shard_map/ppermute | solution.py:66
  326.8 70.6 %collective-permute-start.57 = (bf16[128,768]{1,0:T(8,128)(2,1)}, bf16[128,768]{1,0:T(8,128)(2,1)}, u32[]{:S(2)}, u32[]{:S(2)}) collective-permute-start(bf16[128,768]{1,0:T(8,128)(2,1)} %slice.476), channel_id=1, source_target_pairs={{0,8},{4,12},{8,0},{12,4},{16,24},{20,28},{24,16},{28,20},{1,9},{5... | collective-permute-start | bytes 589832 | tf_op jit(solution)/shard_map/ppermute | solution.py:66
  328.1 37.7 %collective-permute-start.47 = (bf16[192,768]{1,0:T(8,128)(2,1)S(1)}, bf16[192,768]{1,0:T(8,128)(2,1)S(1)}, u32[]{:S(2)}, u32[]{:S(2)}) collective-permute-start(bf16[192,768]{1,0:T(8,128)(2,1)S(1)} %fusion.39), channel_id=1, source_target_pairs={{0,16},{4,20},{8,24},{12,28},{16,0},{20,4},{24,8},{28,12},{1,17},{... | collective-permute-start | bytes 884744 | tf_op jit(solution)/shard_map/ppermute | solution.py:66
  331.5 39.0 %all-to-all-start.2 = ((bf16[8,4,4864]{2,1,0:T(4,128)(2,1)}), bf16[8,4,4864]{2,1,0:T(4,128)(2,1)S(1)}, u32[]{:S(2)}, u32[]{:S(2)}) async-start(bf16[8,4,4864]{2,1,0:T(4,128)(2,1)} %pad_maximum_fusion.9), calls=%async_computation.2 | async-start | bytes 622592 | tf_op jit(solution)/shard_map/all_to_all | solution.py:1331
  384.5 32.9 %all-to-all-start.4 = ((bf16[8,96,768]{2,1,0:T(8,128)(2,1)}), bf16[8,96,768]{2,1,0:T(8,128)(2,1)S(1)}, u32[]{:S(2)}, u32[]{:S(2)}) async-start(bf16[8,96,768]{2,1,0:T(8,128)(2,1)} %get-tuple-element.131), calls=%async_computation.4 | async-start | bytes 2359296 | tf_op jit(solution)/shard_map/all_to_all | solution.py:1241
  393.9 29.9 %collective-permute-start.49 = (bf16[2,192,768]{2,1,0:T(8,128)(2,1)}, bf16[2,192,768]{2,1,0:T(8,128)(2,1)}, u32[]{:S(2)}, u32[]{:S(2)}) collective-permute-start(bf16[2,192,768]{2,1,0:T(8,128)(2,1)} %pad_maximum_fusion.7), channel_id=1, source_target_pairs={{0,1},{1,0},{2,3},{3,2},{4,5},{5,4},{6,7},{7,6},{8,9},{9,8},{10,11... | collective-permute-start | bytes 1769480 | tf_op jit(solution)/shard_map/ppermute | solution.py:48
  (99 other events, 1086.5 us)

commit v3 on v2

--- a/solution.py
+++ b/solution.py
@@ -79,9 +79,9 @@
     return first, first + 2
 
 
-def spread(value):
+def spread(value, *before):
     far = dp_swap(value, 4)
-    return [value, dp_swap(value, 1), far, dp_swap(far, 1)]
+    return [value, dp_swap(tied(value, *before), 1), far, dp_swap(far, 1)]
 
 
 def collect(send, keep, start, middle, end):
@@ -170,9 +170,10 @@
     f_own = f_rows // group
     count = up.shape[1] // f_rows
     wide = 3 * cols
+    chunks = rup.shape[1] // 2 // width
 
     def body(info, proj, qkv, *refs):
-        biases, (up, down, rup, rdown, first, third, mine, theirs, d_mine, d_theirs) = (
+        biases, (up, down, rup, rdown, first, third, mine, theirs) = (
             refs[: len(biases_in)],
             refs[len(biases_in) :],
         )
@@ -216,24 +217,21 @@
             def _():
                 own, other = (one, two) if side == 0 else (two, one)
                 for ref, parts in ((mine, own), (theirs, other)):
-                    at = 0
-                    for low, high in parts:
-                        ref[:, at : at + high - low] = rup[:, low:high]
-                        at += high - low
+                    line = jnp.concatenate([rup[:, low:high] for low, high in parts], axis=1)
+                    for c in range(line.shape[1] // width):
+                        ref[c * d_rows : (c + 1) * d_rows, :] = line[:, c * width : (c + 1) * width]
                 start = side * (f_rows - keep)
-                d_mine[...] = rdown[start : start + keep, :]
+                mine[chunks * d_rows :, :] = rdown[start : start + keep, :]
                 start = (1 - side) * keep
-                d_theirs[...] = rdown[start : start + f_rows - keep, :]
+                theirs[chunks * d_rows :, :] = rdown[start : start + f_rows - keep, :]
 
     biases_in = biases
     operands = [proj, qkv, *biases, up, down, rup, rdown]
     outs = [
         shape((d_rows + 16, wide), bf16),
         shape((2 * d_rows + f_own, width), bf16),
-        shape((d_rows, rup.shape[1] // 2), bf16),
-        shape((d_rows, rup.shape[1] // 2), bf16),
-        shape((keep, width), bf16),
-        shape((f_rows - keep, width), bf16),
+        shape((chunks * d_rows + keep, width), bf16),
+        shape((chunks * d_rows + f_rows - keep, width), bf16),
     ]
     return kernel_call(
         body,
@@ -356,12 +354,12 @@
     )
 
 
-def front(info, tokens, mods, bias, pairs, pieces, rows_piece, cols_own, cut):
-    blocks, rows, _ = tokens.shape
+def front(info, tokens, mods, bias, pieces, rows_piece, cols_own, cut):
+    blocks, rows = tokens.shape[0], tokens.shape[1] - 16
     width = 8 * rows_piece
     wide = 3 * cols_own
 
-    def body(info, tok, mod, bias, pairs, *refs):
+    def body(info, tok, more, mod, bias, *refs):
         parts = refs[:8]
         (hid, prj, qkv, table, gates, low_grad, slot, sums, lines, units, three, lists) = refs[8:]
         step = pl.program_id(0)
@@ -404,10 +402,13 @@
         prj[...] = (dot(low, qkv[...]) + three[...]).astype(bf16)
 
         me = info[8].astype(f32)
-        one = (pairs[0, 0:1, :] == me).astype(f32)
-        two = (pairs[0, 1:2, :] == me).astype(f32)
+        pairs = more[0].astype(f32)
+        one = (pairs[0:1, :] == me).astype(f32)
+        two = (pairs[1:2, :] == me).astype(f32)
         hot = one + two
-        gate = one * pairs[0, 2:3, :] + two * pairs[0, 3:4, :]
+        gate = one * (pairs[2:3, :] + pairs[4:5, :] + pairs[6:7, :]) + two * (
+            pairs[3:4, :] + pairs[5:6, :] + pairs[7:8, :]
+        )
         across = lax.broadcasted_iota(jnp.int32, (rows, rows), 1)
         down = lax.broadcasted_iota(jnp.int32, (rows, rows), 0)
         earlier = (down < across).astype(f32).astype(bf16)
@@ -433,9 +434,9 @@
         [
             SCALARS,
             pl.BlockSpec((1, rows, 2 * width), lambda i: (i, 0, 0)),
+            pl.BlockSpec((1, 16, rows), lambda i: (i, rows // 16, 0)),
             pl.BlockSpec((1, 8, width), lambda i: (i, 0, 0)),
             full((1, wide)),
-            pl.BlockSpec((1, 4, rows), lambda i: (i, 0, 0)),
         ]
         + [full(p.shape) for p in pieces],
         [
@@ -464,7 +465,7 @@
         ],
         [pltpu.VMEM((1, wide), f32), pltpu.VMEM((8, 16, wide), f32)],
         2 * blocks * rows * width * wide,
-        [info, tokens, mods, bias, pairs, *pieces],
+        [info, tokens, tokens, mods, bias, *pieces],
     )
 
 
@@ -607,13 +608,13 @@
 
 
 def middle(info, tokens, mods, heads, pieces, proj_bias, table, rows_piece):
-    blocks, rows, _ = tokens.shape
+    blocks, rows = tokens.shape[0], tokens.shape[1] - 16
     width = 8 * rows_piece
     cols = width // blocks
     cap = table.shape[1]
 
     def body(info, tok, mod, h0, h1, h2, h3, bias, tab, *refs):
-        parts, (hid, att, buf, out0, mid0, own, rel) = refs[:4], refs[4:]
+        parts, (hid, att, buf, out0, mid0, own, rel) = refs[:8], refs[8:]
 
         @pl.when(pl.program_id(0) == 0)
         def _():
@@ -621,7 +622,7 @@
                 place = info[18 + k]
                 at = ((place >> 1) ^ info[8]) * cols + (place & 1) * rows_piece
                 at = pl.multiple_of(at, rows_piece)
-                rel[pl.ds(at, rows_piece), :] = parts[k // 2][k % 2, -rows_piece:, :]
+                rel[pl.ds(at, rows_piece), :] = parts[k][2 * rows_piece :, :]
             own[...] = rel[:cols, :]
 
         attended = jnp.concatenate([h0[...], h1[...], h2[...], h3[...]], axis=1)
@@ -683,15 +684,15 @@
     sums_theirs = (pairs, 2 * rows_piece, width) if paired else (1, 8, width)
 
     def body(info, hid, gcl, bias, *refs):
-        parts, (out, back, mine, theirs, line, up, down, up_sum, down_sum, wide) = refs[:4], refs[4:]
+        parts, (out, back, mine, theirs, line, up, down, up_sum, down_sum, wide) = refs[:8], refs[8:]
         step = pl.program_id(0)
 
         @pl.when(step == 0)
         def _():
             for k in range(8):
                 at = pl.multiple_of(info[18 + k] * rows_piece, rows_piece)
-                up[pl.ds(at, rows_piece), :] = parts[k // 2][k % 2, :rows_piece, :]
-                down[pl.ds(at, rows_piece), :] = parts[k // 2][k % 2, rows_piece : 2 * rows_piece, :]
+                up[pl.ds(at, rows_piece), :] = parts[k][:rows_piece, :]
+                down[pl.ds(at, rows_piece), :] = parts[k][rows_piece : 2 * rows_piece, :]
             up_sum[...] = jnp.zeros_like(up_sum)
             down_sum[...] = jnp.zeros_like(down_sum)
             wide[...] = jnp.zeros_like(wide)
@@ -755,15 +756,17 @@
     )
 
 
-def routed_expert(info, buffers, slots, ups, downs, bias):
+def routed_rows_grads(info, buffers, slots, own, other, bias):
     pairs, _, units = bias.shape
     count, width = buffers[0].shape
     piece = width // (2 * pairs)
     every = pairs * units
+    chunks = every // width
+    cut = own[0].shape[0] - chunks * piece
 
     def body(info, b0, b1, s0, s1, *refs):
-        ups, downs, bias = refs[:4], refs[4:8], refs[8]
-        (ds, dk, us, uk, g0, g1, e0, e1, line, up, down, grad, gsum, esum, bs, ss) = refs[9:]
+        packs, bias = (refs[:4], refs[4:8]), refs[8]
+        (g0, g1, e0, e1, line, act_low, grad_low, bs, ss, up, down, gsum, esum) = refs[9:]
         step = pl.program_id(0)
 
         @pl.when(step == 0)
@@ -771,32 +774,86 @@
             for r in range(pairs):
                 for j in range(2):
                     at = pl.multiple_of(info[18 + 2 * r + j] * piece, piece)
-                    up[pl.ds(at, piece), :] = ups[r][j]
-                at = pl.multiple_of(info[14 + r] * units, units)
-                down[pl.ds(at, units), :] = downs[r][...]
+                    for c in range(chunks):
+                        up[pl.ds(at, piece), c * width : (c + 1) * width] = packs[j][r][
+                            c * piece : (c + 1) * piece, :
+                        ]
+                    at = info[14 + r] * units + j * cut
+                    at = pl.multiple_of(at, 128)
+                    size = units - cut if j else cut
+                    down[pl.ds(at, size), :] = packs[j][r][chunks * piece :, :]
             bs[:count, :], bs[count:, :] = b0[...], b1[...]
             ss[:count, :], ss[count:, :] = s0[...], s1[...]
             gsum[...] = jnp.zeros_like(gsum)
             esum[...] = jnp.zeros_like(esum)
 
+        at = pl.multiple_of(step * units, 128)
+        w_up = up[:, pl.ds(at, units)]
+        w_down = down[pl.ds(at, units), :]
+        act, slope = gelu_parts(dot(bs[...], w_up) + bias[step])
+        low = act.astype(bf16)
+        act_low[...] = low
+        esum[...] += dot(low, w_down)
+        grad = (dot(ss[...], w_down, 1, 1) * slope).astype(bf16)
+        grad_low[...] = grad
+        line[0] = jnp.sum(grad.astype(f32), axis=0, keepdims=True)
+        gsum[...] += dot(grad, w_up, 1, 1)
+
+        @pl.when(step == pairs - 1)
+        def _():
+            g0[...] = gsum[:count, :]
+            g1[...] = gsum[count:, :].astype(bf16)
+            e0[...] = esum[:count, :]
+            e1[...] = esum[count:, :].astype(bf16)
+
+    outs = [
+        shape((count, width), f32),
+        shape((count, width), bf16),
+        shape((count, width), f32),
+        shape((count, width), bf16),
+        shape((pairs, 1, units), f32),
+        shape((2 * count, every), bf16),
+        shape((2 * count, every), bf16),
+        shape((2 * count, width), bf16),
+        shape((2 * count, width), bf16),
+    ]
+    operands = [*buffers, *slots, *own, *other, bias]
+    by_step = pl.BlockSpec((2 * count, units), lambda i: (0, i))
+    return kernel_call(
+        body,
+        pairs,
+        [SCALARS] + [full(o.shape) for o in operands],
+        [full(o.shape) for o in outs[:4]]
+        + [pl.BlockSpec((1, 1, units), lambda i: (i, 0, 0)), by_step, by_step]
+        + [full(o.shape) for o in outs[7:]],
+        outs,
+        [
+            pltpu.VMEM((width, every), bf16),
+            pltpu.VMEM((every, width), bf16),
+            pltpu.VMEM((2 * count, width), f32),
+            pltpu.VMEM((2 * count, width), f32),
+        ],
+        16 * count * width * every,
+        [info, *operands],
+    )
+
+
+def routed_weight_grads(info, act_low, grad_low, rows, slots, pairs):
+    total, width = rows.shape
+    every = act_low.shape[1]
+    units = every // pairs
+    piece = width // (2 * pairs)
+
+    def body(info, act, grad, bs, ss, ds, dk, us, uk, values):
+        step = pl.program_id(0)
         block = info[14 + step]
         at = pl.multiple_of(block * units, 128)
-        w_up = up[:, pl.ds(at, units)]
-        w_down = down[pl.ds(at, units), :]
-        bias_now = bias[pl.ds(block, 1)][0]
-        act, slope = gelu_parts(dot(bs[...], w_up) + bias_now)
-        low = act.astype(bf16)
-        esum[...] += dot(low, w_down)
-        rdown = dot(low, ss[...], 0, 0)
-        grad_low = (dot(ss[...], w_down, 1, 1) * slope).astype(bf16)
-        total = jnp.sum(grad_low.astype(f32), axis=0, keepdims=True)
-        grad[...] = dot(bs[...], grad_low, 0, 0)
-        gsum[...] += dot(grad_low, w_up, 1, 1)
-        line[pl.ds(block, 1)] = total[None]
+        rdown = dot(act[:, pl.ds(at, units)], ss[...], 0, 0)
+        values[...] = dot(bs[...], grad[:, pl.ds(at, units)], 0, 0)
         for r in range(pairs):
             for j in range(2):
                 row = pl.multiple_of(info[18 + 2 * r + j] * piece, piece)
-                value = grad[pl.ds(row, piece), :]
+                value = values[pl.ds(row, piece), :]
                 if r % 2 == 1:
                     us[r // 2, j * piece : (j + 1) * piece, pl.ds(at, units)] = value.astype(bf16)
                 else:
@@ -809,41 +866,21 @@
                 else:
                     dk[r // 2] = rdown
 
-        @pl.when(step == pairs - 1)
-        def _():
-            g0[...] = gsum[:count, :]
-            g1[...] = gsum[count:, :].astype(bf16)
-            e0[...] = esum[:count, :]
-            e1[...] = esum[count:, :].astype(bf16)
-
     outs = [
         shape((2, units, width), bf16),
         shape((2, units, width), f32),
         shape((2, 2 * piece, every), bf16),
         shape((2, 2 * piece, every), f32),
-        shape((count, width), f32),
-        shape((count, width), bf16),
-        shape((count, width), f32),
-        shape((count, width), bf16),
-        shape((pairs, 1, units), f32),
     ]
-    operands = [*buffers, *slots, *ups, *downs, bias]
+    operands = [act_low, grad_low, rows, slots]
     return kernel_call(
         body,
         pairs,
         [SCALARS] + [full(o.shape) for o in operands],
         [full(o.shape) for o in outs],
         outs,
-        [
-            pltpu.VMEM((width, every), bf16),
-            pltpu.VMEM((every, width), bf16),
-            pltpu.VMEM((width, units), f32),
-            pltpu.VMEM((2 * count, width), f32),
-            pltpu.VMEM((2 * count, width), f32),
-            pltpu.VMEM((2 * count, width), bf16),
-            pltpu.VMEM((2 * count, width), bf16),
-        ],
-        24 * count * width * every,
+        [pltpu.VMEM((width, units), f32)],
+        4 * total * width * every,
         [info, *operands],
     )
 
@@ -851,12 +888,12 @@
 def tail_grads(info, tokens, hidden, grads, attended, grad_attn, qkv):
     total, width = hidden.shape
     wide = grads.shape[1]
-    blocks, rows, _ = tokens.shape
+    blocks, rows = tokens.shape[0], tokens.shape[1] - 16
     cols = width // blocks
     piece = width // 8
 
-    def body(info, tok, hid, gr, att, ga, qkv, out, send, keep, sums, lines, proj):
-        out_qkv = dot(hid[...], gr[...], 0, 0).astype(bf16)
+    def body(info, tok, hid, gr, att, ga, qkv, away, stay, send, keep, sums, lines, proj, wq):
+        wq[...] = dot(hid[...], gr[...], 0, 0)
         for m in range(blocks):
             these = slice(m * rows, (m + 1) * rows)
             grad = dot(gr[these, :], qkv[...], 1, 1)
@@ -873,11 +910,19 @@
         for k in range(1, blocks):
             own = jnp.where(info[8] == k, ga[:, k * cols : (k + 1) * cols], own)
         proj[...] = dot(att[...], own, 0, 0)
-        for d in range(8):
-            out[d, :, :wide] = out_qkv[d * piece : (d + 1) * piece, :]
-            at = ((d // 2) ^ info[8]) * cols + (d % 2) * piece
-            at = pl.multiple_of(at, piece)
-            out[d, :, wide:] = proj[pl.ds(at, piece), :].astype(bf16)
+        for k in range(8):
+            place = info[18 + k]
+            at = pl.multiple_of(place * piece, piece)
+            value = wq[pl.ds(at, piece), :]
+            at = pl.multiple_of(((place >> 1) ^ info[8]) * cols + (place & 1) * piece, piece)
+            other = proj[pl.ds(at, piece), :]
+            i = k % 2 + 2 * (k // 4)
+            if k // 2 % 2 == 1:
+                away[i, :, :wide] = value.astype(bf16)
+                away[i, :, wide:] = other.astype(bf16)
+            else:
+                stay[i, :, :wide] = value
+                stay[i, :, wide:] = other
 
     return kernel_call(
         body,
@@ -886,20 +931,22 @@
         + [full((total, width)), full((total, wide)), full((total, width))]
         + [full((total, width)), full((width, wide))],
         [
-            full((8, piece, width)),
+            full((4, piece, width)),
+            full((4, piece, width)),
             full((2, rows, width)),
             full((2, rows, width)),
             full((2 * blocks, width)),
             full((1, wide + width)),
         ],
         [
-            shape((8, piece, width), bf16),
+            shape((4, piece, width), bf16),
+            shape((4, piece, width), f32),
             shape((2, rows, width), bf16),
             shape((2, rows, width), f32),
             shape((2 * blocks, width), f32),
             shape((1, wide + width), f32),
         ],
-        [pltpu.VMEM((width, cols), f32)],
+        [pltpu.VMEM((width, cols), f32), pltpu.VMEM((width, wide), f32)],
         2 * total * width * (2 * wide + cols),
         [info, tokens, hidden, grads, attended, grad_attn, qkv],
     )
@@ -980,7 +1027,7 @@
 
     bias_list = [up_bias, routed_upbias[0], qv_bias, proj_bias, down_bias, routed_downbias[0]]
     if copies == 8:
-        first_share, third_share, rup_mine, rup_theirs, rdown_mine, rdown_theirs = prepare(
+        first_share, third_share, routed_mine, routed_theirs = prepare(
             jnp.stack([position] * 9 + [side]).astype(jnp.int32),
             proj_weight,
             qkv_weight,
@@ -1005,8 +1052,8 @@
         rup_mine, rup_theirs = my_units(routed_up[0])
         rdown_mine = lax.dynamic_slice_in_dim(routed_down[0], side * send, keep, axis=0)
         rdown_theirs = lax.dynamic_slice_in_dim(routed_down[0], (1 - side) * keep, send, axis=0)
-    rup_got = pair_swap(rup_theirs)
-    rdown_got = pair_swap(rdown_theirs)
+        rup_got = pair_swap(rup_theirs)
+        rdown_got = pair_swap(rdown_theirs)
     first, order = ring_gather(first_share)
     bias_three = jnp.zeros((1, 3 * cols_own), f32)
     if copies > 8:
@@ -1028,9 +1075,13 @@
 
     pair_steps = jnp.arange(4, dtype=jnp.int32)
     if copies == 8:
-        third = spread(tied(jnp.stack([third_share, pair_swap(third_share)]), *first[3:5]))
-        downs = spread(tied(jnp.concatenate([rdown_mine, rdown_got]), third[2]))
-        ups = spread(tied(jnp.stack([rup_mine, rup_got]), downs[2]))
+        third_swap, routed_swap = pair_swap(third_share), pair_swap(routed_theirs)
+        third_own = spread(third_share, *first[5:7])
+        third_got = spread(third_swap, *first[5:7])
+        routed_own = spread(tied(routed_mine, third_got[2]), *first[5:7])
+        routed_got = spread(tied(routed_swap, third_got[2]), *first[5:7])
+        third = [v for pair in zip(third_own, third_got) for v in pair]
+        dues = [(*first[1:3], third_swap), (*first[3:5], third_own[2]), (*first[5:7], routed_swap), (third_got[2],), (third_own[3],), (), (routed_own[2],), (routed_own[3], routed_got[1])]
         pair_now = (place >> 2) * 2 + (place & 1)
         unit_blocks = pair_now ^ pair_steps
         masks = jnp.array([0, 2, 1, 3, 4, 6, 5, 7], jnp.int32)
@@ -1055,7 +1106,20 @@
         downs = lax.all_gather(
             jnp.concatenate([rdown_mine, rdown_got]), "dp", axis=0, axis_index_groups=groups
         ).reshape(4, half_units // 4, width)
-        third, ups, downs = ([v[r] for r in range(4)] for v in (third, ups, downs))
+        third = [third[r, j] for r in range(4) for j in range(2)]
+        cut = keep * half_units // (4 * f_rows)
+
+        def packs(j, low, high):
+            return [
+                jnp.concatenate(
+                    [ups[r, j, :, c : c + width] for c in range(0, half_units, width)]
+                    + [downs[r, low:high]]
+                )
+                for r in range(4)
+            ]
+
+        routed_own, routed_got = packs(0, 0, cut), packs(1, cut, half_units // 4)
+        dues = [()] * 8
         unit_blocks = pair_steps
         row_blocks = jnp.arange(8, dtype=jnp.int32)
 
@@ -1063,8 +1127,16 @@
         out = whole.reshape(pairs_count // 2, 2, 2, d_rows, -1).transpose(1, 0, 2, 3, 4)
         return out.reshape(2, 4, width // 8, -1)
 
-    both = gather_group(jnp.concatenate([tokens, cotangent], axis=1))
-    pairs = gather_group(jnp.concatenate([routes.astype(f32).T, gate_weights.T], axis=0))
+    gates_left, gate_parts = gate_weights.T, []
+    for _ in range(3):
+        part = lax.reduce_precision(gates_left, 8, 7)
+        gate_parts.append(part.astype(bf16))
+        gates_left = gates_left - part
+    under = jnp.concatenate([routes.T.astype(bf16), *gate_parts], axis=0)
+    under = jnp.pad(under, ((0, 8), (0, 2 * width - rows)))
+    both = gather_group(
+        jnp.concatenate([jnp.concatenate([tokens, cotangent], axis=1), under], axis=0)
+    )
 
     lengths = image_lengths[0]
     image_total = image_counts[0]
@@ -1108,12 +1180,12 @@
     )
     ada_own = lax.dynamic_slice_in_dim(ada_weight, position * mod_own, mod_own, axis=1)
     bias_own = lax.dynamic_slice_in_dim(bias_line, position * mod_own, mod_own)
-    mod_parts = (mm("sd,dm->sm", tied(act_parts, *first[1:3]), ada_own) + bias_own[None]).reshape(
+    mod_parts = (mm("sd,dm->sm", tied(act_parts, *dues[0]), ada_own) + bias_own[None]).reshape(
         copies, slots, mod_own
     )
     mod_got = lax.all_to_all(mod_parts, "dp", split_axis=0, concat_axis=0, tiled=True)
-    mod_sum = jnp.sum(tied(mod_got, *first[3:5]), axis=0)
-    mod_across = tied(swap(mod_sum, 2), *first[5:7])
+    mod_sum = jnp.sum(tied(mod_got, *dues[1]), axis=0)
+    mod_across = tied(swap(mod_sum, 2), *dues[2])
     mod_beside = swap(jnp.stack([mod_sum, mod_across]), 1)
     mod_group = jnp.stack([mod_sum, mod_beside[0], mod_across, mod_beside[1]])
     modulation = in_order(mod_group, position).transpose(1, 0, 2).reshape(slots, mod_width)
@@ -1137,9 +1209,8 @@
     ) = front(
         info,
         both,
-        mods,
+        tied(mods, *dues[3]),
         bias_three,
-        pairs,
         first,
         width // 8,
         cols_own,
@@ -1149,7 +1220,8 @@
         bias_lines, rupb_own = lines_got, units_got
     upb_line, projb_line, downb_line, rdownb_line = (bias_lines[i : i + 1] for i in range(4))
     slot_got = pair_swap(slot_own)
-    heads_0 = attention(info, tied(projected, third[1], third[2]), group, cols_own)
+    heads_0 = attention(info, tied(projected, *dues[4]), group, cols_own)
+    heads_0 = tied(heads_0, *dues[5])
     heads_2 = swap(heads_0, 2)
     heads_1 = swap(heads_0, 1)
     heads_3 = swap(heads_2, 1)
@@ -1160,13 +1232,13 @@
         (heads_0, heads_1, heads_2, heads_3),
         third,
         projb_line,
-        tied(table, downs[1], downs[2]),
+        tied(table, slot_got, *dues[6]),
         width // 8,
     )
     buffer_got = pair_swap(buffer_own)
 
     shared_parts, shared_back, shared_mine, shared_theirs, upbias_line = shared_expert(
-        info, tied(hidden_b, ups[1]), grad_comb_low, upb_line, third, width // 8, group, copies == 8
+        info, tied(hidden_b, *dues[7]), grad_comb_low, upb_line, third, width // 8, group, copies == 8
     )
     if copies != 8:
         sided = jnp.concatenate([by_side(shared_mine[0]), by_side(shared_mine[1])], axis=2)
@@ -1174,25 +1246,39 @@
             lax.dynamic_index_in_dim(sided, which, 0, keepdims=False) for which in (side, 1 - side)
         )
         shared_theirs = shared_theirs.astype(bf16)
-    shared_sums = shared_mine + pair_swap(shared_theirs).astype(f32)
+    shared_back_got = pair_swap(shared_theirs)
     (
-        down_send,
-        down_keep,
-        up_send,
-        up_keep,
         back_own,
         back_theirs,
         out_own,
         out_theirs,
         units_sum,
-    ) = routed_expert(
+        act_low,
+        grad_low,
+        both_rows,
+        both_slots,
+    ) = routed_rows_grads(
         info,
         (tied(buffer_own, shared_theirs), buffer_got),
         (slot_own, slot_got),
-        ups,
-        downs,
+        routed_own,
+        routed_got,
         rupb_own,
     )
+    shared_sums = shared_mine + shared_back_got.astype(f32)
+    shared_send = jnp.stack([shared_sums[1], shared_sums[3]]).astype(bf16)
+    down_send, down_keep, up_send, up_keep = routed_weight_grads(
+        info, tied(act_low, shared_send), grad_low, both_rows, both_slots, 4
+    )
+    if copies == 8:
+        shared_first = dp_swap(shared_send, 1)
+        shared_near = shared_sums[0] + shared_first[0].astype(f32)
+        shared_far = dp_swap((shared_sums[2] + shared_first[1].astype(f32)).astype(bf16), 4)
+        down_first = dp_swap(down_send, 1)
+        due_rows = (down_send, shared_first)
+        due_back = (down_first, shared_far)
+    else:
+        due_rows, due_back = (down_send,), ()
     units_sum = units_sum.reshape(pairs_count, f_rows)
     blank = jnp.zeros((pairs_count, f_rows), f32)
     units_one = jnp.where(first_side, units_sum, blank)
@@ -1215,7 +1301,7 @@
     )
     zero_line = jnp.zeros((1, width), f32)
     rows_send, rows_keep, _ = to_rows(
-        back_own,
+        tied(back_own, *due_rows),
         pair_swap(back_theirs),
         zero_line,
         table,
@@ -1226,7 +1312,7 @@
     )
     back_near, back_got = reduce_group(rows_send, rows_keep)
     grad_mid, grad_attn_own, sums_b = middle_back(
-        back_near, back_got, residual_mid, attn_out, cotangent, mods
+        tied(back_near, *due_back), back_got, residual_mid, attn_out, cotangent, mods
     )
     attn_2 = swap(grad_attn_own, 2)
     grad_attn = jnp.concatenate(
@@ -1234,26 +1320,23 @@
     )
 
     grad_projected = attention_back(info, projected, grad_attn, proj_own, group, cols_own)
-    last_parts, back_send, back_keep, sums_a, lines = tail_grads(
-        info, both, hidden_a, grad_projected, attended, grad_attn, qkv_own
-    )
-    last_sums = jnp.sum(
-        lax.all_to_all(
-            last_parts.reshape(copies, d_rows, width), "dp", split_axis=0, concat_axis=0, tiled=True
-        ).astype(f32),
-        axis=0,
-    )
+    out_got = pair_swap(out_theirs)
+    due_tail = (out_got,)
     if copies == 8:
-        end = (last_parts,)
-        rdown_sums, down_got = collect(down_send, down_keep, (), (grad_attn_own,), end)
-        rup_sums, up_got = collect(up_send, up_keep, (down_got,), (grad_projected,), end)
-        shared_rows, _ = collect(
-            jnp.stack([shared_sums[1], shared_sums[3]]).astype(bf16),
-            (shared_sums[0], shared_sums[2]),
-            (up_got,),
-            (grad_projected,),
-            end,
-        )
+        down_far = dp_swap((down_keep[1] + down_first[1].astype(f32)).astype(bf16), 4)
+        up_first = dp_swap(tied(up_send, down_first), 1)
+        due_tail = (out_got, down_far, up_first)
+    away, stay, back_send, back_keep, sums_a, lines = tail_grads(
+        info, both, tied(hidden_a, *due_tail), grad_projected, attended, grad_attn, qkv_own
+    )
+
+    if copies == 8:
+        up_far = dp_swap((up_keep[1] + up_first[1].astype(f32)).astype(bf16), 4)
+        shared_rows = shared_near + shared_far.astype(f32)
+        rdown_sums = down_keep[0] + down_first[0].astype(f32) + down_far.astype(f32)
+        rup_sums = up_keep[0] + up_first[0].astype(f32) + up_far.astype(f32)
+        last_first = stay + dp_swap(away, 1).astype(f32)
+        last_second = last_first[:2] + dp_swap(last_first[2:].astype(bf16), 4).astype(f32)
     else:
 
         def scatter(value, each):
@@ -1280,6 +1363,19 @@
                 for which in (side, 1 - side)
             ]
         )
+        last_parts = jnp.stack(
+            [(away if k // 2 % 2 else stay)[k % 2 + 2 * (k // 4)].astype(bf16) for k in range(8)]
+        )
+        last_sums = jnp.sum(
+            lax.all_to_all(
+                last_parts.reshape(copies, d_rows, width),
+                "dp",
+                split_axis=0,
+                concat_axis=0,
+                tiled=True,
+            ).astype(f32),
+            axis=0,
+        )
 
     lines = lines[0]
     qv_line = lax.dynamic_update_slice(
@@ -1301,8 +1397,8 @@
     )
 
     rows_send, rows_keep, sums_out = to_rows(
-        tied(out_own, last_parts),
-        pair_swap(tied(out_theirs, grad_attn_own)),
+        tied(out_own, away),
+        out_got,
         rdownb_line,
         table,
         gates,
@@ -1311,8 +1407,7 @@
         downb_line,
     )
     combined_near, combined_got = reduce_group(rows_send, rows_keep)
-    combined = combined_near + combined_got.astype(f32) + downb_line
-    output = (residual_mid + gate_b * combined).astype(bf16)
+    near_a, got_a = reduce_group(back_send, back_keep)
 
     block_of = block_hot.astype(f32)
     sums_all = jnp.concatenate(
@@ -1351,6 +1446,18 @@
         axis=0,
     )
     cond_parts = mm("sm,dm->sd", mod_all, ada_weight).reshape(copies, slots, d_rows)
+    after = cond_parts
+    got_a, combined_got = tied(got_a, after), tied(combined_got, after)
+    combined = combined_near + combined_got.astype(f32) + downb_line
+    output = (residual_mid + gate_b * combined).astype(bf16)
+    grad_hidden_a = near_a + got_a.astype(f32)
+    normed_a, inv_std_a = norm_parts(tokens.astype(f32))
+    tokens_grad = grad_mid + norm_back(grad_hidden_a * (1.0 + scale_a), normed_a, inv_std_a)
+    if copies == 8:
+        last_second = tied(last_second, after)
+        last_third = dp_swap(last_second[1].astype(bf16), 2)
+        last_sums = last_second[0] + last_third.astype(f32)
+        rup_sums = tied(rup_sums, after)
     grad_cond_act = (
         lax.all_to_all(cond_parts, "dp", split_axis=0, concat_axis=0, tiled=True)
         .transpose(1, 0, 2)
@@ -1360,11 +1467,6 @@
     conditioning_grad = (grad_cond_act * sigmoid_cond * (1.0 + cond_value * (1.0 - sigmoid_cond)))[
         None
     ]
-
-    near_a, got_a = reduce_group(back_send, back_keep)
-    grad_hidden_a = near_a + got_a.astype(f32)
-    normed_a, inv_std_a = norm_parts(tokens.astype(f32))
-    tokens_grad = grad_mid + norm_back(grad_hidden_a * (1.0 + scale_a), normed_a, inv_std_a)
 
     rup_got = pair_swap(rup_sums[d_rows:].astype(bf16))
     rdown_got = pair_swap(rdown_sums[keep:].astype(bf16))

time: 436 us -> 403 us (0.924)
  waiting for transfers between devices: 150 us -> 114 us
  Pallas kernels: 126 us -> 134 us
    ppermute x25 -> x30, waiting for transfers between devices: 115 us -> 63.9 us  [dp_swap(): return lax.ppermute(value, 'dp', [(i, i ^ mask) for i in range(copies)])]
    all_to_all x1, waiting for transfers between devices: 0.01 us -> 10.2 us  [body(): lax.all_to_all(jnp.concatenate([jnp.broadcast_to(grad_modulation[None], (...]
    pallas_call x13 -> x14, Pallas kernels: 126 us -> 134 us  [kernel_call(): pl.pallas_call(body, grid=(grid,), in_specs=in_specs, out_specs=out_specs...]
    all_to_all x1, waiting for transfers between devices: 2.08 us -> 9.63 us  [body(): lax.all_to_all(cond_act.reshape(slots, copies, d_rows).transpose(1, 0, 2)...]
    all_to_all x1 -> x0, waiting for transfers between devices: 5.79 us -> none  [body(): lax.all_to_all(last_parts.reshape(copies, d_rows, width), 'dp', split_axi...]
    all_to_all x1, waiting for transfers between devices: 5.63 us -> 0.01 us  [body(): lax.all_to_all(mod_parts, 'dp', split_axis=0, concat_axis=0, tiled=True)]
    ppermute x7, waiting for transfers between devices: 0.02 us -> 5.14 us  [hop(): lax.ppermute(value, 'dp', [(ring[i], ring[(i + way) % copies]) for i in r...]
    unnamed x132 -> x113, local copies, waits for them, and re-layouts: 9.65 us -> 5.78 us
  transfers between devices with their start and end apart: 63 -> 65, of which waited for: 23 -> 22; matrix products, arithmetic and copies ran while one was open for 13% -> 15% of each run, Pallas kernels for 20% -> 32%
where the time goes in v3:
time: 403 us; the launch traced here: 398 us
  Pallas kernels  134 us (33%)
  waiting for transfers between devices  114 us (28%)
  starting transfers between devices  77.2 us (19%)
  other arithmetic  40.4 us (10%)
  local copies, waits for them, and re-layouts  26.4 us (7%)
  between operations  4.05 us (1%)
    pallas_call x14, Pallas kernels, kernel_call(): pl.pallas_call(body, grid=(grid,), in_specs=in_specs, out_specs=out_specs...  134 us
    ppermute x30, waiting for transfers between devices, dp_swap(): return lax.ppermute(value, 'dp', [(i, i ^ mask) for i in range(copies)])  63.9 us
    ppermute x30, starting transfers between devices, dp_swap(): return lax.ppermute(value, 'dp', [(i, i ^ mask) for i in range(copies)])  38.8 us
    ppermute x24, waiting for transfers between devices, swap(): return lax.ppermute(value, 'expert', [(i, i ^ mask) for i in range(size)])  24.6 us
    ppermute x24, starting transfers between devices, swap(): return lax.ppermute(value, 'expert', [(i, i ^ mask) for i in range(size)])  15.3 us
    all_to_all x1, waiting for transfers between devices, body(): lax.all_to_all(jnp.concatenate([jnp.broadcast_to(grad_modulation[None], (...  10.2 us
    all_to_all x1, waiting for transfers between devices, body(): lax.all_to_all(cond_act.reshape(slots, copies, d_rows).transpose(1, 0, 2)...  9.63 us
    ppermute x7, starting transfers between devices, hop(): lax.ppermute(value, 'dp', [(ring[i], ring[(i + way) % copies]) for i in r...  9.11 us
  transfers between devices with their start and end apart: 65, of which 22 were waited for; matrix products, arithmetic and copies ran while one was open for 15% of the time, Pallas kernels for 32%

profile of v3, /device:TPU:0, one launch (start us, length us, event | category | flops | bytes accessed | tf_op | source)
XLA Modules:
  0.0 397.9 jit_solution(12714538532218597375)
XLA Ops:
  28.7 9.6 %all-to-all-done = bf16[8,4,96]{2,1,0:T(4,128)(2,1)S(1)} async-done(((bf16[8,4,96]{2,1,0:T(4,128)(2,1)}), bf16[8,4,96]{2,1,0:T(4,128)(2,1)S(1)}, u32[]{:S(2)}, u32[]{:S(2)}) %all-to-all-start) | async-done | bytes 6176 | tf_op jit(solution)/shard_map/all_to_all | solution.py:1169
  46.1 5.1 %collective-permute-done.6.refs_4_ = bf16[112,576]{1,0:T(8,128)(2,1)} collective-permute-done((bf16[112,576]{1,0:T(8,128)(2,1)}, bf16[112,576]{1,0:T(8,128)(2,1)}, u32[]{:S(2)}, u32[]{:S(2)}) %collective-permute-start.6) | collective-permute-done | bytes 129056 | tf_op jit(solution)/shard_map/ppermute | solution.py:115
  68.0 16.7 %collective-permute-done.13.refs_5_ = bf16[288,768]{1,0:T(8,128)(2,1)} collective-permute-done((bf16[288,768]{1,0:T(8,128)(2,1)}, bf16[288,768]{1,0:T(8,128)(2,1)}, u32[]{:S(2)}, u32[]{:S(2)}) %collective-permute-start.13) | collective-permute-done | bytes 442400 | tf_op jit(solution)/shard_map/ppermute | solution.py:66
  88.8 7.4 %shard_map.359 = (bf16[1024,768]{1,0:T(8,128)(2,1)}, bf16[1024,576]{1,0:T(8,128)(2,1)}, bf16[768,576]{1,0:T(8,128)(2,1)}, bf16[4,128,256]{2,1,0:T(8,128)(2,1)}, ...) custom-call(s32[32]{0:T(128)} %concatenate.38.info, ...), custom_call_target="tpu_custom_call" | custom-call | flops 905969664 | bytes 14135680 | tf_op jit(solution)/shard_map/pallas_call | solution.py:148
  96.2 4.9 %collective-permute-start.19 = (bf16[512,768]{1,0:T(8,128)(2,1)}, bf16[512,768]{1,0:T(8,128)(2,1)S(1)}, u32[]{:S(2)}, u32[]{:S(2)}) collective-permute-start(bf16[512,768]{1,0:T(8,128)(2,1)} %get-tuple-element.111.s0), channel_id=1, source_target_pairs={{0,8},{4,12},{8,0},{12,4},{16,24},{20,28},{24,16},{28,20},{1,9},{5... | collective-permute-start | bytes 2359304 | tf_op jit(solution)/shard_map/ppermute | solution.py:66
  103.1 10.6 %shard_map.360.h0 = bf16[1024,192]{1,0:T(8,128)(2,1)} custom-call(s32[32]{0:T(128)} %concatenate.38.info, bf16[1024,576]{1,0:T(8,128)(2,1)} %get-tuple-element.108.own.every, bf16[1024,576]{1,0:T(8,128)(2,1)} %get-tuple-element.108.own.every), custom_call_target="tpu_custom_call" | custom-call | flops 805306368 | bytes 2752640 | tf_op jit(solution)/shard_map/pallas_call | solution.py:148
  119.3 4.1 %collective-permute-done.23.refs_7_ = bf16[288,768]{1,0:T(8,128)(2,1)S(1)} collective-permute-done((bf16[288,768]{1,0:T(8,128)(2,1)}, bf16[288,768]{1,0:T(8,128)(2,1)S(1)}, u32[]{:S(2)}, u32[]{:S(2)}) %collective-permute-start.23) | collective-permute-done | bytes 442400 | tf_op jit(solution)/shard_map/ppermute | solution.py:66
  126.0 15.5 %collective-permute-done.19.s1 = bf16[512,768]{1,0:T(8,128)(2,1)S(1)} collective-permute-done((bf16[512,768]{1,0:T(8,128)(2,1)}, bf16[512,768]{1,0:T(8,128)(2,1)S(1)}, u32[]{:S(2)}, u32[]{:S(2)}) %collective-permute-start.19) | collective-permute-done | bytes 786464 | tf_op jit(solution)/shard_map/ppermute | solution.py:66
  145.7 9.1 %shard_map.361 = (bf16[1024,768]{1,0:T(8,128)(2,1)}, bf16[1024,768]{1,0:T(8,128)(2,1)}, bf16[512,768]{1,0:T(8,128)(2,1)}, f32[256,768]{1,0:T(8,128)}, f32[256,768]{1,0:T(8,128)}, /*index=5*/bf16[192,768]{1,0:T(8,128)(2,1)}) custom-call(s32[32]{0:T(128)} %concatenate.38.info, bf16[4,272,1536]{2,1,0:T(8,128)(2,1)} %pad_maximum_fusion.tok.more, ...), custom_call_target="tpu_custom_call" | custom-call | flops 1409286144 | bytes 14617728 | tf_op jit(solution)/shard_map/pallas_call | solution.py:148
  154.9 14.8 %shard_map.362 = (f32[1024,768]{1,0:T(8,128)}, f32[1024,768]{1,0:T(8,128)}, f32[4,192,768]{2,1,0:T(8,128)}, bf16[4,192,768]{2,1,0:T(8,128)(2,1)}, f32[1,768]{1,0:T(1,128)}) custom-call(s32[32]{0:T(128)} %concatenate.38.info, bf16[1024,768]{1,0:T(8,128)(2,1)} %get-tuple-element.122.hid, bf16[1024,768]{1,0:T(8,128)(2,1)} %get-tuple-element.123.gcl, ...), custom_call_target="tpu_custom_call" | custom-call | flops 7247757312 | bytes 16521344 | tf_op jit(solution)/shard_map/pallas_call | solution.py:148
  176.4 24.1 %shard_map.363 = (f32[512,768]{1,0:T(8,128)}, bf16[512,768]{1,0:T(8,128)(2,1)}, f32[512,768]{1,0:T(8,128)}, bf16[512,768]{1,0:T(8,128)(2,1)}, f32[4,1,384]{2,1,0...) custom-call(s32[32]{0:T(128)} %concatenate.38.info, ...), custom_call_target="tpu_custom_call" | custom-call | flops 9663676416 | bytes 22032512 | tf_op jit(solution)/shard_map/pallas_call | solution.py:148
  204.5 13.9 %shard_map.364 = (bf16[2,384,768]{2,1,0:T(8,128)(2,1)}, f32[2,384,768]{2,1,0:T(8,128)}, bf16[2,192,1536]{2,1,0:T(8,128)(2,1)}, f32[2,192,1536]{2,1,0:T(8,128)}) custom-call(s32[32]{0:T(128)} %concatenate.38.info, bf16[1024,1536]{1,0:T(8,128)(2,1)} %get-tuple-element.133.act, bf16[1024,1536]{1,0:T(8,128)(2,1)} %get-tuple-element.134.grad, ...), custom_call_target="tpu_custom_call" | custom-call | flops 4831838208 | bytes 16515200 | tf_op jit(solution)/shard_map/pallas_call | solution.py:148
  226.5 6.3 %shard_map.365 = (bf16[2,256,768]{2,1,0:T(8,128)(2,1)}, f32[2,256,768]{2,1,0:T(8,128)}, f32[4,1,768]{2,1,0:T(1,128)}) custom-call(f32[512,768]{1,0:T(8,128)} %get-tuple-element.143.own, bf16[512,768]{1,0:T(8,128)(2,1)} %collective-permute-done.36.got, f32[1,768]{1,0:T(1,128)} %broadcast_in_dim.122.bias.line, bf16[4,128,256]{2,1,0:T(8,128)(2,1)} %get-tuple-element.114.tab, ...), custom_call_target="tpu_custom_call" | custom-call | flops 201326592 | bytes 11491328 | tf_op jit(solution)/shard_map/pallas_call | solution.py:148
  239.2 5.2 %collective-permute-done.32 = bf16[2,384,768]{2,1,0:T(8,128)(2,1)S(1)} collective-permute-done((bf16[2,384,768]{2,1,0:T(8,128)(2,1)}, bf16[2,384,768]{2,1,0:T(8,128)(2,1)S(1)}, u32[]{:S(2)}, u32[]{:S(2)}) %collective-permute-start.32) | collective-permute-done | bytes 1179680 | tf_op jit(solution)/shard_map/ppermute | solution.py:66
  254.2 4.7 %collective-permute-done.39.got = bf16[256,768]{1,0:T(8,128)(2,1)S(1)} collective-permute-done((bf16[256,768]{1,0:T(8,128)(2,1)}, bf16[256,768]{1,0:T(8,128)(2,1)S(1)}, u32[]{:S(2)}, u32[]{:S(2)}) %collective-permute-start.39) | collective-permute-done | bytes 393248 | tf_op jit(solution)/shard_map/ppermute | solution.py:48
  259.6 3.7 shard_map.366
  263.3 9.5 %collective-permute-done.33 = bf16[384,768]{1,0:T(8,128)(2,1)} collective-permute-done((bf16[384,768]{1,0:T(8,128)(2,1)}, bf16[384,768]{1,0:T(8,128)(2,1)}, u32[]{:S(2)}, u32[]{:S(2)}) %collective-permute-start.33) | collective-permute-done | bytes 589856 | tf_op jit(solution)/shard_map/ppermute | solution.py:66
  284.6 18.3 %shard_map.367.gr = bf16[1024,576]{1,0:T(8,128)(2,1)} custom-call(s32[32]{0:T(128)} %concatenate.38.info, bf16[1024,576]{1,0:T(8,128)(2,1)} %get-tuple-element.108.own.every, bf16[1024,576]{1,0:T(8,128)(2,1)} %get-tuple-element.108.own.every, bf16[1024,768]{1,0:T(8,128)(2,1)} %copy-done.7, bf16[192,768]{1,0:T(8,128)(2,1)} %get-tuple-element.151.rel), custom_call_target="tpu_custom_call" | custom-call | flops 2315255808 | bytes 5406848 | tf_op jit(solution)/shard_map/pallas_call | solution.py:148
  302.9 9.4 %shard_map.368 = (bf16[4,96,768]{2,1,0:T(8,128)(2,1)}, f32[4,96,768]{2,1,0:T(8,128)}, bf16[2,256,768]{2,1,0:T(8,128)(2,1)}, f32[2,256,768]{2,1,0:T(8,128)}, f32[8,768]{1,0:T(8,128)}, /*index=5*/f32[1,1344]{1,0:T(1,128)}) custom-call(s32[32]{0:T(128)} %concatenate.38.info, bf16[4,272,1536]{2,1,0:T(8,128)(2,1)} %pad_maximum_fusion.tok.more, ...), custom_call_target="tpu_custom_call" | custom-call | flops 2113929216 | bytes 14284160 | tf_op jit(solution)/shard_map/pallas_call | solution.py:148
  313.1 6.1 %shard_map.369 = (bf16[2,256,768]{2,1,0:T(8,128)(2,1)}, f32[2,256,768]{2,1,0:T(8,128)}, f32[4,1,768]{2,1,0:T(1,128)}) custom-call(f32[512,768]{1,0:T(8,128)} %get-tuple-element.155.own, bf16[512,768]{1,0:T(8,128)(2,1)} %collective-permute-done.30.got, f32[1,768]{1,0:T(1,128)} %get-tuple-element.211.bias, bf16[4,128,256]{2,1,0:T(8,128)(2,1)} %get-tuple-element.114.tab, ...), custom_call_target="tpu_custom_call" | custom-call | flops 201326592 | bytes 11491328 | tf_op jit(solution)/shard_map/pallas_call | solution.py:148
  326.8 3.7 all-to-all-start.2
  337.9 10.2 %all-to-all-done.2 = bf16[8,4,4864]{2,1,0:T(4,128)(2,1)S(1)} async-done(((bf16[8,4,4864]{2,1,0:T(4,128)(2,1)}), bf16[8,4,4864]{2,1,0:T(4,128)(2,1)S(1)}, u32[]{:S(2)}, u32[]{:S(2)}) %all-to-all-start.2) | async-done | bytes 311328 | tf_op jit(solution)/shard_map/all_to_all | solution.py:1426
  378.2 4.0 collective-permute-done.54
  382.7 7.2 %collective-permute-done.44 = bf16[256,768]{1,0:T(8,128)(2,1)} collective-permute-done((bf16[256,768]{1,0:T(8,128)(2,1)}, bf16[256,768]{1,0:T(8,128)(2,1)}, u32[]{:S(2)}, u32[]{:S(2)}) %collective-permute-start.44) | collective-permute-done | bytes 393248 | tf_op jit(solution)/shard_map/ppermute | solution.py:48
  (378 shorter events, 169.6 us)
Async XLA Ops:
  10.3 28.0 %collective-permute-start.3 = (bf16[112,576]{1,0:T(8,128)(2,1)}, bf16[112,576]{1,0:T(8,128)(2,1)}, u32[]{:S(2)}, u32[]{:S(2)}) collective-permute-start(bf16[112,576]{1,0:T(8,128)(2,1)} %get-tuple-element.100.refs_0_), channel_id=1, source_target_pairs={{0,4},{8,0},{16,8},{24,16},{28,24},{20,28},{12,20},{4,12},{1,5},{9... | collective-permute-start | bytes 387080 | tf_op jit(solution)/shard_map/ppermute | solution.py:115
  10.3 28.0 %collective-permute-start.4 = (bf16[288,768]{1,0:T(8,128)(2,1)}, bf16[288,768]{1,0:T(8,128)(2,1)}, u32[]{:S(2)}, u32[]{:S(2)}) collective-permute-start(bf16[288,768]{1,0:T(8,128)(2,1)} %get-tuple-element.115.refs_0_), channel_id=1, source_target_pairs={{0,8},{4,12},{8,0},{12,4},{16,24},{20,28},{24,16},{28,20},{1,9},{5... | collective-permute-start | bytes 1327112 | tf_op jit(solution)/shard_map/ppermute | solution.py:66
  12.4 40.9 %collective-permute-start.7 = (bf16[288,768]{1,0:T(8,128)(2,1)}, bf16[288,768]{1,0:T(8,128)(2,1)S(1)}, u32[]{:S(2)}, u32[]{:S(2)}) collective-permute-start(bf16[288,768]{1,0:T(8,128)(2,1)} %get-tuple-element.115.refs_0_), channel_id=1, source_target_pairs={{0,16},{4,20},{8,24},{12,28},{16,0},{20,4},{24,8},{28,12},{1,17},{... | collective-permute-start | bytes 1327112 | tf_op jit(solution)/shard_map/ppermute | solution.py:66
  20.1 35.5 %collective-permute-start = (bf16[272,1536]{1,0:T(8,128)(2,1)}, bf16[272,1536]{1,0:T(8,128)(2,1)S(1)}, u32[]{:S(2)}, u32[]{:S(2)}) collective-permute-start(bf16[272,1536]{1,0:T(8,128)(2,1)} %get-tuple-element.198), channel_id=1, source_target_pairs={{0,2},{1,3},{2,0},{3,1},{4,6},{5,7},{6,4},{7,5},{8,10},{9,11},{10,... | collective-permute-start | bytes 2506760 | tf_op jit(solution)/shard_map/ppermute | solution.py:48
  26.7 30.3 %collective-permute-start.11 = (bf16[320,768]{1,0:T(8,128)(2,1)}, bf16[320,768]{1,0:T(8,128)(2,1)}, u32[]{:S(2)}, u32[]{:S(2)}) collective-permute-start(bf16[320,768]{1,0:T(8,128)(2,1)} %get-tuple-element.104), channel_id=1, source_target_pairs={{0,8},{4,12},{8,0},{12,4},{16,24},{20,28},{24,16},{28,20},{1,9},{5... | collective-permute-start | bytes 1474568 | tf_op jit(solution)/shard_map/ppermute | solution.py:66
  56.9 27.7 %collective-permute-start.1 = (bf16[2,272,1536]{2,1,0:T(8,128)(2,1)}, bf16[2,272,1536]{2,1,0:T(8,128)(2,1)}, u32[]{:S(2)}, u32[]{:S(2)}) collective-permute-start(bf16[2,272,1536]{2,1,0:T(8,128)(2,1)} %pad_maximum_fusion.1), channel_id=1, source_target_pairs={{0,1},{1,0},{2,3},{3,2},{4,5},{5,4},{6,7},{7,6},{8,9},{9,8},{10,11... | collective-permute-start | bytes 5013512 | tf_op jit(solution)/shard_map/ppermute | solution.py:48
  59.6 54.1 %collective-permute-start.21 = (bf16[288,768]{1,0:T(8,128)(2,1)S(1)}, bf16[288,768]{1,0:T(8,128)(2,1)}, u32[]{:S(2)}, u32[]{:S(2)}) collective-permute-start(bf16[288,768]{1,0:T(8,128)(2,1)S(1)} %copy-done.22), channel_id=1, source_target_pairs={{0,4},{4,0},{8,12},{12,8},{16,20},{20,16},{24,28},{28,24},{1,5},{5... | collective-permute-start | bytes 1327112 | tf_op jit(solution)/shard_map/ppermute | solution.py:66
  59.9 28.3 %collective-permute-start.14 = (bf16[112,576]{1,0:T(8,128)(2,1)}, bf16[112,576]{1,0:T(8,128)(2,1)}, u32[]{:S(2)}, u32[]{:S(2)}) collective-permute-start(bf16[112,576]{1,0:T(8,128)(2,1)} %collective-permute-done.9.refs_5_), channel_id=1, source_target_pairs={{0,8},{8,16},{16,24},{24,28},{28,20},{20,12},{12,4},{4,0},{1,9},{9... | collective-permute-start | bytes 387080 | tf_op jit(solution)/shard_map/ppermute | solution.py:115
  64.4 36.7 %collective-permute-start.15 = (bf16[288,768]{1,0:T(8,128)(2,1)}, bf16[288,768]{1,0:T(8,128)(2,1)}, u32[]{:S(2)}, u32[]{:S(2)}) collective-permute-start(bf16[288,768]{1,0:T(8,128)(2,1)} %copy-done.23), channel_id=1, source_target_pairs={{0,4},{4,0},{8,12},{12,8},{16,20},{20,16},{24,28},{28,24},{1,5},{5... | collective-permute-start | bytes 1327112 | tf_op jit(solution)/shard_map/ppermute | solution.py:66
  84.7 32.8 %collective-permute-start.20 = (bf16[448,768]{1,0:T(8,128)(2,1)}, bf16[448,768]{1,0:T(8,128)(2,1)S(1)}, u32[]{:S(2)}, u32[]{:S(2)}) collective-permute-start(bf16[448,768]{1,0:T(8,128)(2,1)} %get-tuple-element.126.refs_0_), channel_id=1, source_target_pairs={{0,16},{4,20},{8,24},{12,28},{16,0},{20,4},{24,8},{28,12},{1,17},{... | collective-permute-start | bytes 2064392 | tf_op jit(solution)/shard_map/ppermute | solution.py:66
  96.2 45.3 %collective-permute-start.19 = (bf16[512,768]{1,0:T(8,128)(2,1)}, bf16[512,768]{1,0:T(8,128)(2,1)S(1)}, u32[]{:S(2)}, u32[]{:S(2)}) collective-permute-start(bf16[512,768]{1,0:T(8,128)(2,1)} %get-tuple-element.111.s0), channel_id=1, source_target_pairs={{0,8},{4,12},{8,0},{12,4},{16,24},{20,28},{24,16},{28,20},{1,9},{5... | collective-permute-start | bytes 2359304 | tf_op jit(solution)/shard_map/ppermute | solution.py:66
  115.2 27.0 %collective-permute-start.28 = (bf16[320,768]{1,0:T(8,128)(2,1)}, bf16[320,768]{1,0:T(8,128)(2,1)}, u32[]{:S(2)}, u32[]{:S(2)}) collective-permute-start(bf16[320,768]{1,0:T(8,128)(2,1)} %collective-permute-done.11.refs_4_), channel_id=1, source_target_pairs={{0,16},{4,20},{8,24},{12,28},{16,0},{20,4},{24,8},{28,12},{1,17},{... | collective-permute-start | bytes 1474568 | tf_op jit(solution)/shard_map/ppermute | solution.py:66
  117.5 37.4 %collective-permute-start.24 = (bf16[448,768]{1,0:T(8,128)(2,1)S(1)}, bf16[448,768]{1,0:T(8,128)(2,1)S(1)}, u32[]{:S(2)}, u32[]{:S(2)}) collective-permute-start(bf16[448,768]{1,0:T(8,128)(2,1)S(1)} %collective-permute-done.20.refs_2_), channel_id=1, source_target_pairs={{0,4},{4,0},{8,12},{12,8},{16,20},{20,16},{24,28},{28,24},{1,5},{5... | collective-permute-start | bytes 2064392 | tf_op jit(solution)/shard_map/ppermute | solution.py:66
  123.4 31.5 %collective-permute-start.25 = (bf16[320,768]{1,0:T(8,128)(2,1)}, bf16[320,768]{1,0:T(8,128)(2,1)S(1)}, u32[]{:S(2)}, u32[]{:S(2)}) collective-permute-start(bf16[320,768]{1,0:T(8,128)(2,1)} %collective-permute-done.11.refs_4_), channel_id=1, source_target_pairs={{0,4},{4,0},{8,12},{12,8},{16,20},{20,16},{24,28},{28,24},{1,5},{5... | collective-permute-start | bytes 1474568 | tf_op jit(solution)/shard_map/ppermute | solution.py:66
  142.2 29.7 %collective-permute-start.27 = (bf16[448,768]{1,0:T(8,128)(2,1)}, bf16[448,768]{1,0:T(8,128)(2,1)}, u32[]{:S(2)}, u32[]{:S(2)}) collective-permute-start(bf16[448,768]{1,0:T(8,128)(2,1)} %get-tuple-element.126.refs_0_), channel_id=1, source_target_pairs={{0,4},{4,0},{8,12},{12,8},{16,20},{20,16},{24,28},{28,24},{1,5},{5... | collective-permute-start | bytes 2064392 | tf_op jit(solution)/shard_map/ppermute | solution.py:66
  144.8 27.5 %collective-permute-start.29 = (bf16[320,768]{1,0:T(8,128)(2,1)}, bf16[320,768]{1,0:T(8,128)(2,1)}, u32[]{:S(2)}, u32[]{:S(2)}) collective-permute-start(bf16[320,768]{1,0:T(8,128)(2,1)} %collective-permute-done.28.refs_6_), channel_id=1, source_target_pairs={{0,4},{4,0},{8,12},{12,8},{16,20},{20,16},{24,28},{28,24},{1,5},{5... | collective-permute-start | bytes 1474568 | tf_op jit(solution)/shard_map/ppermute | solution.py:66
  169.8 30.7 %collective-permute-start.31 = (bf16[4,192,768]{2,1,0:T(8,128)(2,1)}, bf16[4,192,768]{2,1,0:T(8,128)(2,1)S(1)}, u32[]{:S(2)}, u32[]{:S(2)}) collective-permute-start(bf16[4,192,768]{2,1,0:T(8,128)(2,1)} %get-tuple-element.124), channel_id=1, source_target_pairs={{0,8},{4,12},{8,0},{12,4},{16,24},{20,28},{24,16},{28,20},{1,9},{5... | collective-permute-start | bytes 3538952 | tf_op jit(solution)/shard_map/ppermute | solution.py:66
  233.2 50.2 %collective-permute-start.30 = (bf16[512,768]{1,0:T(8,128)(2,1)}, bf16[512,768]{1,0:T(8,128)(2,1)}, u32[]{:S(2)}, u32[]{:S(2)}) collective-permute-start(bf16[512,768]{1,0:T(8,128)(2,1)} %get-tuple-element.130), channel_id=1, source_target_pairs={{0,8},{4,12},{8,0},{12,4},{16,24},{20,28},{24,16},{28,20},{1,9},{5... | collective-permute-start | bytes 2359304 | tf_op jit(solution)/shard_map/ppermute | solution.py:66
  253.2 28.7 %collective-permute-start.34 = (bf16[2,192,1536]{2,1,0:T(8,128)(2,1)}, bf16[2,192,1536]{2,1,0:T(8,128)(2,1)S(1)}, u32[]{:S(2)}, u32[]{:S(2)}) collective-permute-start(bf16[2,192,1536]{2,1,0:T(8,128)(2,1)} %get-tuple-element.140), channel_id=1, source_target_pairs={{0,4},{4,0},{8,12},{12,8},{16,20},{20,16},{24,28},{28,24},{1,5},{5... | collective-permute-start | bytes 3538952 | tf_op jit(solution)/shard_map/ppermute | solution.py:66
  276.4 98.5 %collective-permute-start.60 = (bf16[128,768]{1,0:T(8,128)(2,1)}, bf16[128,768]{1,0:T(8,128)(2,1)}, u32[]{:S(2)}, u32[]{:S(2)}) collective-permute-start(bf16[128,768]{1,0:T(8,128)(2,1)} %slice.476), channel_id=1, source_target_pairs={{0,8},{4,12},{8,0},{12,4},{16,24},{20,28},{24,16},{28,20},{1,9},{5... | collective-permute-start | bytes 589832 | tf_op jit(solution)/shard_map/ppermute | solution.py:66
  282.0 48.5 %collective-permute-start.58 = (bf16[192,1536]{1,0:T(8,128)(2,1)S(1)}, bf16[192,1536]{1,0:T(8,128)(2,1)S(1)}, u32[]{:S(2)}, u32[]{:S(2)}) collective-permute-start(bf16[192,1536]{1,0:T(8,128)(2,1)S(1)} %fusion.25), channel_id=1, source_target_pairs={{0,16},{4,20},{8,24},{12,28},{16,0},{20,4},{24,8},{28,12},{1,17},{... | collective-permute-start | bytes 1769480 | tf_op jit(solution)/shard_map/ppermute | solution.py:66
  323.3 40.2 %collective-permute-start.47 = (bf16[2,256,768]{2,1,0:T(8,128)(2,1)}, bf16[2,256,768]{2,1,0:T(8,128)(2,1)}, u32[]{:S(2)}, u32[]{:S(2)}) collective-permute-start(bf16[2,256,768]{2,1,0:T(8,128)(2,1)} %get-tuple-element.170), channel_id=1, source_target_pairs={{0,1},{1,0},{2,3},{3,2},{4,5},{5,4},{6,7},{7,6},{8,9},{9,8},{10,11... | collective-permute-start | bytes 2359304 | tf_op jit(solution)/shard_map/ppermute | solution.py:48
  325.8 41.9 %collective-permute-start.43 = (bf16[2,256,768]{2,1,0:T(8,128)(2,1)}, bf16[2,256,768]{2,1,0:T(8,128)(2,1)}, u32[]{:S(2)}, u32[]{:S(2)}) collective-permute-start(bf16[2,256,768]{2,1,0:T(8,128)(2,1)} %get-tuple-element.159), channel_id=1, source_target_pairs={{0,1},{1,0},{2,3},{3,2},{4,5},{5,4},{6,7},{7,6},{8,9},{9,8},{10,11... | collective-permute-start | bytes 2359304 | tf_op jit(solution)/shard_map/ppermute | solution.py:48
  334.9 29.9 %collective-permute-start.52 = (bf16[2,96,768]{2,1,0:T(8,128)(2,1)S(1)}, bf16[2,96,768]{2,1,0:T(8,128)(2,1)}, u32[]{:S(2)}, u32[]{:S(2)}) collective-permute-start(bf16[2,96,768]{2,1,0:T(8,128)(2,1)S(1)} %slice.475), channel_id=1, source_target_pairs={{0,16},{4,20},{8,24},{12,28},{16,0},{20,4},{24,8},{28,12},{1,17},{... | collective-permute-start | bytes 884744 | tf_op jit(solution)/shard_map/ppermute | solution.py:66
  (92 other events, 1102.9 us)

commit v4 on v3

--- a/solution.py
+++ b/solution.py
@@ -48,16 +48,20 @@
     return lax.ppermute(value, "expert", [(i, i ^ mask) for i in range(size)])
 
 
+def exchange_group(value):
+    across = swap(value, 2)
+    return value, across, swap(jnp.stack([value, across]), 1)
+
+
 def gather_group(value):
-    across = swap(value, 2)
-    beside = swap(jnp.stack([value, across]), 1)
+    value, across, beside = exchange_group(value)
     return jnp.stack([value, beside[0], across, beside[1]])
 
 
 def reduce_group(send, keep):
-    beside = swap(send, 1).astype(f32)
-    own = keep[0] + beside[0]
-    other = (keep[1] + beside[1]).astype(bf16)
+    beside = swap(send, 1)
+    own = keep[0] + beside[0].astype(f32)
+    other = (keep[1] + beside[1].astype(f32)).astype(bf16)
     return own, swap(other, 2)
 
 
@@ -179,7 +183,9 @@
         )
         third[d_rows + f_own :, :] = proj[...]
         lines = [
-            jnp.concatenate([b[...].astype(f32), jnp.zeros((1, wide - b.shape[1]), f32)], axis=1)
+            jnp.concatenate(
+                [b[...].astype(f32).reshape(1, -1), jnp.zeros((1, wide - b.shape[0]), f32)], axis=1
+            )
             for b in biases[1:]
         ]
         for p in range(group):
@@ -192,7 +198,11 @@
                     axis=1,
                 )
                 line = jnp.concatenate(
-                    [biases[0][:, own].astype(f32), jnp.zeros((1, wide - f_own), f32)], axis=1
+                    [
+                        biases[0][...].astype(f32).reshape(1, -1)[:, own],
+                        jnp.zeros((1, wide - f_own), f32),
+                    ],
+                    axis=1,
                 )
                 first[d_rows:, :] = jnp.concatenate(
                     [line] + lines + [jnp.zeros((15 - len(lines), wide), f32)], axis=0
@@ -318,19 +328,23 @@
 
 
 def group_rows_out(info, shared, last, d_rows, f_rows):
-    group, _, width = shared.shape
+    group = 4
+    rows, width = shared[0].shape
     f_own = f_rows // group
     cols = width // group
     count = width // f_own
 
-    def body(info, shared, last, up, down, qkv, proj):
+    def body(info, s0, s2, s13, l0, l2, l13, up, down, qkv, proj, shared, last):
+        for all_parts, p0, p2, p13 in ((shared, s0, s2, s13), (last, l0, l2, l13)):
+            all_parts[0], all_parts[2] = p0[...].astype(f32), p2[...].astype(f32)
+            all_parts[1], all_parts[3] = p13[0].astype(f32), p13[1].astype(f32)
         for a in range(group):
-            part = shared[info[8] ^ a].astype(f32)
+            part = shared[info[8] ^ a]
             for d in range(count):
                 at = d * f_rows + a * f_own
                 up[:, at : at + f_own] = part[:d_rows, d * f_own : (d + 1) * f_own]
             down[a * f_own : (a + 1) * f_own, :] = part[d_rows:, :]
-            part = last[info[8] ^ a].astype(f32)
+            part = last[info[8] ^ a]
             for i in range(3):
                 at = i * width + a * cols
                 qkv[:, at : at + cols] = part[:, i * cols : (i + 1) * cols]
@@ -342,15 +356,16 @@
         shape((d_rows, 3 * width), f32),
         shape((d_rows, width), f32),
     ]
+    operands = [*shared, *last]
     return kernel_call(
         body,
         1,
-        [SCALARS, full(shared.shape), full(last.shape)],
+        [SCALARS] + [full(o.shape) for o in operands],
         [full(o.shape) for o in outs],
         outs,
-        [],
+        [pltpu.VMEM((group, rows, width), f32), pltpu.VMEM((group, d_rows, width), f32)],
         0,
-        [info, shared, last],
+        [info, *operands],
     )
 
 
@@ -473,9 +488,11 @@
     blocks, cap, rows = table.shape
     width = own.shape[1]
 
-    def body(own, got, bias, tab, gate, add, tok, line, send, keep, sums):
+    def body(own, got, bias, tab, *refs):
+        gate, (add, tok, line, send, keep, sums) = refs[:-6], refs[-6:]
         slots = (own[...] + got[...].astype(f32) + bias[...]).astype(bf16)
-        value = add[...] + gate[0] * dot(tab[0], slots, 0, 0)
+        value = dot(tab[0], slots, 0, 0)
+        value = add[...] + (gate[0][0] * value if gate else value)
         first = (pl.program_id(0) == 0).astype(f32)
         sums[0] = jnp.sum(
             tok[0].astype(f32) * (value + first * line[...]), axis=0, keepdims=True
@@ -489,7 +506,7 @@
                 else:
                     keep[k // 2] = value
 
-    operands = [own, got, bias, table, gates, addend, tokens, line]
+    operands = [own, got, bias, table, *gates, addend, tokens, line]
     return kernel_call(
         body,
         blocks,
@@ -498,7 +515,9 @@
             pl.BlockSpec((cap, width), lambda i: (i, 0)),
             full((1, width)),
             pl.BlockSpec((1, cap, rows), lambda i: (i, 0, 0)),
-            pl.BlockSpec((1, rows, 1), lambda i: (i, 0, 0)),
+        ]
+        + [pl.BlockSpec((1, rows, 1), lambda i: (i, 0, 0))] * len(gates)
+        + [
             pl.BlockSpec((rows, width), lambda i: (i, 0)),
             pl.BlockSpec((1, rows, width), lambda i: (i, 0, 1)),
             full((1, width)),
@@ -525,10 +544,10 @@
     seen = jnp.zeros((1, blocks * rows), jnp.int32)
     for j in range(blocks):
         seen = jnp.where((lanes == j) & (info[10 + j] == own), 1, seen)
-    scores = dot(query, key, 1, 1) * (HEAD_DIM ** (-0.5))
+    scores = dot(query * bf16(HEAD_DIM ** (-0.5)), key, 1, 1)
     masked = jnp.where(seen == 1, scores, -1e30)
     exponent = jnp.exp(masked - jnp.max(masked, axis=-1, keepdims=True))
-    return exponent / jnp.sum(exponent, axis=-1, keepdims=True)
+    return exponent * (1.0 / jnp.sum(exponent, axis=-1, keepdims=True))
 
 
 def attention(info, projected, blocks, cols_own):
@@ -846,10 +865,10 @@
 
     def body(info, act, grad, bs, ss, ds, dk, us, uk, values):
         step = pl.program_id(0)
-        block = info[14 + step]
-        at = pl.multiple_of(block * units, 128)
-        rdown = dot(act[:, pl.ds(at, units)], ss[...], 0, 0)
-        values[...] = dot(bs[...], grad[:, pl.ds(at, units)], 0, 0)
+        slot = step ^ info[14]
+        at = pl.multiple_of(step * units, 128)
+        rdown = dot(act[...], ss[...], 0, 0)
+        values[...] = dot(bs[...], grad[...], 0, 0)
         for r in range(pairs):
             for j in range(2):
                 row = pl.multiple_of(info[18 + 2 * r + j] * piece, piece)
@@ -859,7 +878,7 @@
                 else:
                     uk[r // 2, j * piece : (j + 1) * piece, pl.ds(at, units)] = value
 
-            @pl.when(step == r)
+            @pl.when(slot == r)
             def _():
                 if r % 2 == 1:
                     ds[r // 2] = rdown.astype(bf16)
@@ -876,7 +895,9 @@
     return kernel_call(
         body,
         pairs,
-        [SCALARS] + [full(o.shape) for o in operands],
+        [SCALARS]
+        + [pl.BlockSpec((total, units), lambda i: (0, i))] * 2
+        + [full(o.shape) for o in operands[2:]],
         [full(o.shape) for o in outs],
         outs,
         [pltpu.VMEM((width, units), f32)],
@@ -1031,7 +1052,7 @@
             jnp.stack([position] * 9 + [side]).astype(jnp.int32),
             proj_weight,
             qkv_weight,
-            [b[None] for b in bias_list],
+            bias_list,
             up_weight,
             down_weight,
             routed_up[0],
@@ -1305,7 +1326,7 @@
         pair_swap(back_theirs),
         zero_line,
         table,
-        jnp.ones((group, rows, 1), f32),
+        (),
         shared_back,
         both,
         zero_line,
@@ -1325,7 +1346,7 @@
     if copies == 8:
         down_far = dp_swap((down_keep[1] + down_first[1].astype(f32)).astype(bf16), 4)
         up_first = dp_swap(tied(up_send, down_first), 1)
-        due_tail = (out_got, down_far, up_first)
+        due_tail = (down_far, up_first)
     away, stay, back_send, back_keep, sums_a, lines = tail_grads(
         info, both, tied(hidden_a, *due_tail), grad_projected, attended, grad_attn, qkv_own
     )
@@ -1401,7 +1422,7 @@
         out_got,
         rdownb_line,
         table,
-        gates,
+        (gates,),
         shared_parts,
         both,
         downb_line,
@@ -1436,6 +1457,8 @@
         concat_axis=0,
         tiled=True,
     )
+    if copies == 8:
+        mod_got = tied(mod_got, last_second)
     mod_all = mod_got[:, :, :mod_width].reshape(copies * slots, mod_width)
     line_sums = jnp.sum(mod_got[:, :, mod_width:].astype(f32), axis=0).reshape(-1)
     ada_grad = mm("sd,sm->dm", act_parts, mod_all)
@@ -1447,19 +1470,21 @@
     )
     cond_parts = mm("sm,dm->sd", mod_all, ada_weight).reshape(copies, slots, d_rows)
     after = cond_parts
-    got_a, combined_got = tied(got_a, after), tied(combined_got, after)
+    cond_got = lax.all_to_all(cond_parts, "dp", split_axis=0, concat_axis=0, tiled=True)
+    cond_got = tied(cond_got, got_a, combined_got)
     combined = combined_near + combined_got.astype(f32) + downb_line
     output = (residual_mid + gate_b * combined).astype(bf16)
     grad_hidden_a = near_a + got_a.astype(f32)
     normed_a, inv_std_a = norm_parts(tokens.astype(f32))
     tokens_grad = grad_mid + norm_back(grad_hidden_a * (1.0 + scale_a), normed_a, inv_std_a)
     if copies == 8:
-        last_second = tied(last_second, after)
         last_third = dp_swap(last_second[1].astype(bf16), 2)
         last_sums = last_second[0] + last_third.astype(f32)
         rup_sums = tied(rup_sums, after)
+    if copies == 8:
+        cond_got = tied(cond_got, last_third)
     grad_cond_act = (
-        lax.all_to_all(cond_parts, "dp", split_axis=0, concat_axis=0, tiled=True)
+        cond_got
         .transpose(1, 0, 2)
         .reshape(slots, width)
     )
@@ -1470,8 +1495,8 @@
 
     rup_got = pair_swap(rup_sums[d_rows:].astype(bf16))
     rdown_got = pair_swap(rdown_sums[keep:].astype(bf16))
-    shared_all = gather_group(shared_rows.astype(bf16))
-    last_all = gather_group(last_sums.astype(bf16))
+    shared_all = exchange_group(shared_rows.astype(bf16))
+    last_all = exchange_group(last_sums.astype(bf16))
     if copies == 8:
         rup_rows, rdown_rows = routed_rows(info, rup_sums, rup_got, rdown_sums, rdown_got, keep)
         up_rows, down_rows, qkv_rows, proj_rows = group_rows_out(
@@ -1484,7 +1509,8 @@
             first_side, jnp.concatenate([kept, back]), jnp.concatenate([back, kept])
         )
         shared_all, last_all = (
-            in_order(v, position).astype(f32) for v in (shared_all, last_all)
+            in_order(jnp.stack([v[0], v[2][0], v[1], v[2][1]]), position).astype(f32)
+            for v in (shared_all, last_all)
         )
         up_rows = (
             shared_all[:, :d_rows]

time: 403 us -> 396 us (0.983)
  waiting for transfers between devices: 114 us -> 104 us
    all_to_all x1, waiting for transfers between devices: 10.2 us -> 0.01 us  [body(): lax.all_to_all(jnp.concatenate([jnp.broadcast_to(grad_modulation[None], (...]
    ppermute x24, waiting for transfers between devices: 24.6 us -> 16 us  [swap(): return lax.ppermute(value, 'expert', [(i, i ^ mask) for i in range(size)])]
    ppermute x30, waiting for transfers between devices: 63.9 us -> 72.5 us  [dp_swap(): return lax.ppermute(value, 'dp', [(i, i ^ mask) for i in range(copies)])]
  transfers between devices with their start and end apart: 65 -> 65, of which waited for: 22 -> 20; matrix products, arithmetic and copies ran while one was open for 15% -> 17% of each run, Pallas kernels for 32% -> 32%
where the time goes in v4:
time: 396 us; the launch traced here: 391 us
  Pallas kernels  133 us (34%)
  waiting for transfers between devices  104 us (26%)
  starting transfers between devices  76.6 us (19%)
  other arithmetic  43.9 us (11%)
  local copies, waits for them, and re-layouts  27.7 us (7%)
  between operations  4.11 us (1%)
    pallas_call x14, Pallas kernels, kernel_call(): pl.pallas_call(body, grid=(grid,), in_specs=in_specs, out_specs=out_specs...  133 us
    ppermute x30, waiting for transfers between devices, dp_swap(): return lax.ppermute(value, 'dp', [(i, i ^ mask) for i in range(copies)])  72.5 us
    ppermute x30, starting transfers between devices, dp_swap(): return lax.ppermute(value, 'dp', [(i, i ^ mask) for i in range(copies)])  36.6 us
    ppermute x24, starting transfers between devices, swap(): return lax.ppermute(value, 'expert', [(i, i ^ mask) for i in range(size)])  16.5 us
    ppermute x24, waiting for transfers between devices, swap(): return lax.ppermute(value, 'expert', [(i, i ^ mask) for i in range(size)])  16 us
    all_to_all x1, waiting for transfers between devices, body(): lax.all_to_all(cond_act.reshape(slots, copies, d_rows).transpose(1, 0, 2)...  10.6 us
    ppermute x7, starting transfers between devices, hop(): lax.ppermute(value, 'dp', [(ring[i], ring[(i + way) % copies]) for i in r...  9.32 us
    unnamed x143, local copies, waits for them, and re-layouts  7.96 us
  transfers between devices with their start and end apart: 65, of which 20 were waited for; matrix products, arithmetic and copies ran while one was open for 17% of the time, Pallas kernels for 32%

profile of v4, /device:TPU:0, one launch (start us, length us, event | category | flops | bytes accessed | tf_op | source)
XLA Modules:
  0.0 391.2 jit_solution(16159495009606237300)
XLA Ops:
  27.4 10.6 %all-to-all-done = bf16[8,4,96]{2,1,0:T(4,128)(2,1)S(1)} async-done(((bf16[8,4,96]{2,1,0:T(4,128)(2,1)}), bf16[8,4,96]{2,1,0:T(4,128)(2,1)S(1)}, u32[]{:S(2)}, u32[]{:S(2)}) %all-to-all-start) | async-done | bytes 6176 | tf_op jit(solution)/shard_map/all_to_all | solution.py:1190
  45.9 3.5 collective-permute-done.6.refs_4_
  67.4 17.4 %collective-permute-done.13.refs_5_ = bf16[288,768]{1,0:T(8,128)(2,1)} collective-permute-done((bf16[288,768]{1,0:T(8,128)(2,1)}, bf16[288,768]{1,0:T(8,128)(2,1)}, u32[]{:S(2)}, u32[]{:S(2)}) %collective-permute-start.13) | collective-permute-done | bytes 442400 | tf_op jit(solution)/shard_map/ppermute | solution.py:70
  89.0 7.4 %shard_map.359 = (bf16[1024,768]{1,0:T(8,128)(2,1)}, bf16[1024,576]{1,0:T(8,128)(2,1)}, bf16[768,576]{1,0:T(8,128)(2,1)}, bf16[4,128,256]{2,1,0:T(8,128)(2,1)}, ...) custom-call(s32[32]{0:T(128)} %concatenate.38.info, ...), custom_call_target="tpu_custom_call" | custom-call | flops 905969664 | bytes 14135680 | tf_op jit(solution)/shard_map/pallas_call | solution.py:152
  96.4 3.8 collective-permute-start.19
  102.2 10.6 %shard_map.360.h0 = bf16[1024,192]{1,0:T(8,128)(2,1)} custom-call(s32[32]{0:T(128)} %concatenate.38.info, bf16[1024,576]{1,0:T(8,128)(2,1)} %get-tuple-element.108.own.every, bf16[1024,576]{1,0:T(8,128)(2,1)} %get-tuple-element.108.own.every), custom_call_target="tpu_custom_call" | custom-call | flops 805306368 | bytes 2752640 | tf_op jit(solution)/shard_map/pallas_call | solution.py:152
  114.6 3.6 collective-permute-done.20.refs_2_
  125.1 16.9 %collective-permute-done.19.s1 = bf16[512,768]{1,0:T(8,128)(2,1)S(1)} collective-permute-done((bf16[512,768]{1,0:T(8,128)(2,1)}, bf16[512,768]{1,0:T(8,128)(2,1)S(1)}, u32[]{:S(2)}, u32[]{:S(2)}) %collective-permute-start.19) | collective-permute-done | bytes 786464 | tf_op jit(solution)/shard_map/ppermute | solution.py:70
  145.5 9.1 %shard_map.361 = (bf16[1024,768]{1,0:T(8,128)(2,1)}, bf16[1024,768]{1,0:T(8,128)(2,1)}, bf16[512,768]{1,0:T(8,128)(2,1)}, f32[256,768]{1,0:T(8,128)}, f32[256,768]{1,0:T(8,128)}, /*index=5*/bf16[192,768]{1,0:T(8,128)(2,1)}) custom-call(s32[32]{0:T(128)} %concatenate.38.info, bf16[4,272,1536]{2,1,0:T(8,128)(2,1)} %pad_maximum_fusion.tok.more.refs_1_.refs_2_, ...), custom_call_target="tpu_custom_call" | custom-call | flops 1409286144 | bytes 14617728 | tf_op jit(solution)/shard_map/pallas_call | solution.py:152
  154.7 14.8 %shard_map.362 = (f32[1024,768]{1,0:T(8,128)}, f32[1024,768]{1,0:T(8,128)}, f32[4,192,768]{2,1,0:T(8,128)}, bf16[4,192,768]{2,1,0:T(8,128)(2,1)}, f32[1,768]{1,0:T(1,128)}) custom-call(s32[32]{0:T(128)} %concatenate.38.info, bf16[1024,768]{1,0:T(8,128)(2,1)} %get-tuple-element.122.hid, bf16[1024,768]{1,0:T(8,128)(2,1)} %get-tuple-element.123.gcl, ...), custom_call_target="tpu_custom_call" | custom-call | flops 7247757312 | bytes 16521344 | tf_op jit(solution)/shard_map/pallas_call | solution.py:152
  176.2 24.0 %shard_map.363 = (f32[512,768]{1,0:T(8,128)}, bf16[512,768]{1,0:T(8,128)(2,1)}, f32[512,768]{1,0:T(8,128)}, bf16[512,768]{1,0:T(8,128)(2,1)}, f32[4,1,384]{2,1,0...) custom-call(s32[32]{0:T(128)} %concatenate.38.info, ...), custom_call_target="tpu_custom_call" | custom-call | flops 9663676416 | bytes 22032512 | tf_op jit(solution)/shard_map/pallas_call | solution.py:152
  204.6 12.6 %shard_map.364 = (bf16[2,384,768]{2,1,0:T(8,128)(2,1)}, f32[2,384,768]{2,1,0:T(8,128)}, bf16[2,192,1536]{2,1,0:T(8,128)(2,1)}, f32[2,192,1536]{2,1,0:T(8,128)}) custom-call(s32[32]{0:T(128)} %concatenate.38.info, bf16[1024,1536]{1,0:T(8,128)(2,1)} %get-tuple-element.132.act, bf16[1024,1536]{1,0:T(8,128)(2,1)} %get-tuple-element.133.grad, ...), custom_call_target="tpu_custom_call" | custom-call | flops 4831838208 | bytes 16515200 | tf_op jit(solution)/shard_map/pallas_call | solution.py:152
  227.4 6.2 %shard_map.365 = (bf16[2,256,768]{2,1,0:T(8,128)(2,1)}, f32[2,256,768]{2,1,0:T(8,128)}, f32[4,1,768]{2,1,0:T(1,128)}) custom-call(f32[512,768]{1,0:T(8,128)} %get-tuple-element.142.own, bf16[512,768]{1,0:T(8,128)(2,1)} %copy-done.22, f32[1,768]{1,0:T(1,128)} %broadcast_in_dim.103.bias.refs_2_, bf16[4,128,256]{2,1,0:T(8,128)(2,1)} %get-tuple-element.114.tab, ...), custom_call_target="tpu_custom_call" | custom-call | flops 201326592 | bytes 11487232 | tf_op jit(solution)/shard_map/pallas_call | solution.py:152
  234.6 3.4 collective-permute-done.37
  257.9 3.7 shard_map.366
  264.0 8.1 %collective-permute-done.32 = bf16[384,768]{1,0:T(8,128)(2,1)} collective-permute-done((bf16[384,768]{1,0:T(8,128)(2,1)}, bf16[384,768]{1,0:T(8,128)(2,1)}, u32[]{:S(2)}, u32[]{:S(2)}) %collective-permute-start.32) | collective-permute-done | bytes 589856 | tf_op jit(solution)/shard_map/ppermute | solution.py:70
  279.9 18.3 %shard_map.367.gr = bf16[1024,576]{1,0:T(8,128)(2,1)} custom-call(s32[32]{0:T(128)} %concatenate.38.info, bf16[1024,576]{1,0:T(8,128)(2,1)} %get-tuple-element.108.own.every, bf16[1024,576]{1,0:T(8,128)(2,1)} %get-tuple-element.108.own.every, bf16[1024,768]{1,0:T(8,128)(2,1)} %copy-done.6, bf16[192,768]{1,0:T(8,128)(2,1)} %get-tuple-element.150.rel), custom_call_target="tpu_custom_call" | custom-call | flops 2315255808 | bytes 5406848 | tf_op jit(solution)/shard_map/pallas_call | solution.py:152
  298.2 9.5 %shard_map.368 = (bf16[4,96,768]{2,1,0:T(8,128)(2,1)}, f32[4,96,768]{2,1,0:T(8,128)}, bf16[2,256,768]{2,1,0:T(8,128)(2,1)}, f32[2,256,768]{2,1,0:T(8,128)}, f32[8,768]{1,0:T(8,128)}, /*index=5*/f32[1,1344]{1,0:T(1,128)}) custom-call(s32[32]{0:T(128)} %concatenate.38.info, bf16[4,272,1536]{2,1,0:T(8,128)(2,1)} %pad_maximum_fusion.tok.more.refs_1_.refs_2_, ...), custom_call_target="tpu_custom_call" | custom-call | flops 2113929216 | bytes 14284160 | tf_op jit(solution)/shard_map/pallas_call | solution.py:152
  309.3 6.1 %shard_map.369 = (bf16[2,256,768]{2,1,0:T(8,128)(2,1)}, f32[2,256,768]{2,1,0:T(8,128)}, f32[4,1,768]{2,1,0:T(1,128)}) custom-call(f32[512,768]{1,0:T(8,128)} %get-tuple-element.154.own, bf16[512,768]{1,0:T(8,128)(2,1)} %copy-done.21, f32[1,768]{1,0:T(1,128)} %get-tuple-element.209.bias, bf16[4,128,256]{2,1,0:T(8,128)(2,1)} %get-tuple-element.114.tab, ...), custom_call_target="tpu_custom_call" | custom-call | flops 201326592 | bytes 11491328 | tf_op jit(solution)/shard_map/pallas_call | solution.py:152
  323.0 3.5 all-to-all-start.2
  336.1 13.8 %collective-permute-done.50 = bf16[2,96,768]{2,1,0:T(8,128)(2,1)S(1)} collective-permute-done((bf16[2,96,768]{2,1,0:T(8,128)(2,1)S(1)}, bf16[2,96,768]{2,1,0:T(8,128)(2,1)S(1)}, u32[]{:S(2)}, u32[]{:S(2)}) %collective-permute-start.50) | collective-permute-done | bytes 294944 | tf_op jit(solution)/shard_map/ppermute | solution.py:70
  354.7 3.9 %all-to-all-start.3 = ((f32[8,4,96]{2,1,0:T(4,128)}), f32[8,4,96]{2,1,0:T(4,128)S(1)}, u32[]{:S(2)}, u32[]{:S(2)}) async-start(f32[8,4,96]{2,1,0:T(4,128)} %copy.85), calls=%async_computation.3 | async-start | bytes 32768 | tf_op jit(solution)/shard_map/all_to_all | solution.py:1473
  369.4 3.8 collective-permute-done.54.l2
  386.8 4.1 %shard_map.370 = (f32[96,3072]{1,0:T(8,128)}, f32[384,768]{1,0:T(8,128)}, f32[96,2304]{1,0:T(8,128)}, f32[96,768]{1,0:T(8,128)}) custom-call(s32[32]{0:T(128)} %concatenate.38.info, bf16[192,768]{1,0:T(8,128)(2,1)} %copy-done.5, bf16[192,768]{1,0:T(8,128)(2,1)} %copy-done.20, bf16[2,192,768]{2,1,0:T(8,128)(2,1)} %collective-permute-done.53.s13, ...), custom_call_target="tpu_custom_call" | custom-call | bytes 5308544 | tf_op jit(solution)/shard_map/pallas_call | solution.py:152
  (401 shorter events, 168.3 us)
Async XLA Ops:
  8.9 29.0 %collective-permute-start.2 = (bf16[112,576]{1,0:T(8,128)(2,1)}, bf16[112,576]{1,0:T(8,128)(2,1)}, u32[]{:S(2)}, u32[]{:S(2)}) collective-permute-start(bf16[112,576]{1,0:T(8,128)(2,1)} %get-tuple-element.100.refs_0_), channel_id=1, source_target_pairs={{0,8},{8,16},{16,24},{24,28},{28,20},{20,12},{12,4},{4,0},{1,9},{9... | collective-permute-start | bytes 387080 | tf_op jit(solution)/shard_map/ppermute | solution.py:119
  9.1 43.1 %collective-permute-start.7 = (bf16[288,768]{1,0:T(8,128)(2,1)}, bf16[288,768]{1,0:T(8,128)(2,1)S(1)}, u32[]{:S(2)}, u32[]{:S(2)}) collective-permute-start(bf16[288,768]{1,0:T(8,128)(2,1)} %get-tuple-element.115.refs_0_), channel_id=1, source_target_pairs={{0,16},{4,20},{8,24},{12,28},{16,0},{20,4},{24,8},{28,12},{1,17},{... | collective-permute-start | bytes 1327112 | tf_op jit(solution)/shard_map/ppermute | solution.py:70
  18.8 35.8 %collective-permute-start = (bf16[272,1536]{1,0:T(8,128)(2,1)}, bf16[272,1536]{1,0:T(8,128)(2,1)S(1)}, u32[]{:S(2)}, u32[]{:S(2)}) collective-permute-start(bf16[272,1536]{1,0:T(8,128)(2,1)} %get-tuple-element.198), channel_id=1, source_target_pairs={{0,2},{1,3},{2,0},{3,1},{4,6},{5,7},{6,4},{7,5},{8,10},{9,11},{10,... | collective-permute-start | bytes 2506760 | tf_op jit(solution)/shard_map/ppermute | solution.py:48
  25.4 31.5 %collective-permute-start.11 = (bf16[320,768]{1,0:T(8,128)(2,1)}, bf16[320,768]{1,0:T(8,128)(2,1)}, u32[]{:S(2)}, u32[]{:S(2)}) collective-permute-start(bf16[320,768]{1,0:T(8,128)(2,1)} %get-tuple-element.104), channel_id=1, source_target_pairs={{0,8},{4,12},{8,0},{12,4},{16,24},{20,28},{24,16},{28,20},{1,9},{5... | collective-permute-start | bytes 1474568 | tf_op jit(solution)/shard_map/ppermute | solution.py:70
  56.0 28.9 %collective-permute-start.1 = (bf16[2,272,1536]{2,1,0:T(8,128)(2,1)}, bf16[2,272,1536]{2,1,0:T(8,128)(2,1)}, u32[]{:S(2)}, u32[]{:S(2)}) collective-permute-start(bf16[2,272,1536]{2,1,0:T(8,128)(2,1)} %pad_maximum_fusion.1), channel_id=1, source_target_pairs={{0,1},{1,0},{2,3},{3,2},{4,5},{5,4},{6,7},{7,6},{8,9},{9,8},{10,11... | collective-permute-start | bytes 5013512 | tf_op jit(solution)/shard_map/ppermute | solution.py:48
  58.6 54.2 %collective-permute-start.21 = (bf16[288,768]{1,0:T(8,128)(2,1)S(1)}, bf16[288,768]{1,0:T(8,128)(2,1)}, u32[]{:S(2)}, u32[]{:S(2)}) collective-permute-start(bf16[288,768]{1,0:T(8,128)(2,1)S(1)} %copy-done.30), channel_id=1, source_target_pairs={{0,4},{4,0},{8,12},{12,8},{16,20},{20,16},{24,28},{28,24},{1,5},{5... | collective-permute-start | bytes 1327112 | tf_op jit(solution)/shard_map/ppermute | solution.py:70
  59.9 28.5 %collective-permute-start.14 = (bf16[112,576]{1,0:T(8,128)(2,1)}, bf16[112,576]{1,0:T(8,128)(2,1)}, u32[]{:S(2)}, u32[]{:S(2)}) collective-permute-start(bf16[112,576]{1,0:T(8,128)(2,1)} %collective-permute-done.9.refs_5_), channel_id=1, source_target_pairs={{0,8},{8,16},{16,24},{24,28},{28,20},{20,12},{12,4},{4,0},{1,9},{9... | collective-permute-start | bytes 387080 | tf_op jit(solution)/shard_map/ppermute | solution.py:119
  61.2 39.0 %collective-permute-start.15 = (bf16[288,768]{1,0:T(8,128)(2,1)}, bf16[288,768]{1,0:T(8,128)(2,1)}, u32[]{:S(2)}, u32[]{:S(2)}) collective-permute-start(bf16[288,768]{1,0:T(8,128)(2,1)} %copy-done.31), channel_id=1, source_target_pairs={{0,4},{4,0},{8,12},{12,8},{16,20},{20,16},{24,28},{28,24},{1,5},{5... | collective-permute-start | bytes 1327112 | tf_op jit(solution)/shard_map/ppermute | solution.py:70
  84.8 33.4 %collective-permute-start.20 = (bf16[448,768]{1,0:T(8,128)(2,1)}, bf16[448,768]{1,0:T(8,128)(2,1)S(1)}, u32[]{:S(2)}, u32[]{:S(2)}) collective-permute-start(bf16[448,768]{1,0:T(8,128)(2,1)} %get-tuple-element.126.refs_0_), channel_id=1, source_target_pairs={{0,16},{4,20},{8,24},{12,28},{16,0},{20,4},{24,8},{28,12},{1,17},{... | collective-permute-start | bytes 2064392 | tf_op jit(solution)/shard_map/ppermute | solution.py:70
  96.4 45.6 %collective-permute-start.19 = (bf16[512,768]{1,0:T(8,128)(2,1)}, bf16[512,768]{1,0:T(8,128)(2,1)S(1)}, u32[]{:S(2)}, u32[]{:S(2)}) collective-permute-start(bf16[512,768]{1,0:T(8,128)(2,1)} %get-tuple-element.111.s0), channel_id=1, source_target_pairs={{0,8},{4,12},{8,0},{12,4},{16,24},{20,28},{24,16},{28,20},{1,9},{5... | collective-permute-start | bytes 2359304 | tf_op jit(solution)/shard_map/ppermute | solution.py:70
  114.4 28.3 %collective-permute-start.28 = (bf16[320,768]{1,0:T(8,128)(2,1)}, bf16[320,768]{1,0:T(8,128)(2,1)}, u32[]{:S(2)}, u32[]{:S(2)}) collective-permute-start(bf16[320,768]{1,0:T(8,128)(2,1)} %collective-permute-done.11.refs_4_), channel_id=1, source_target_pairs={{0,16},{4,20},{8,24},{12,28},{16,0},{20,4},{24,8},{28,12},{1,17},{... | collective-permute-start | bytes 1474568 | tf_op jit(solution)/shard_map/ppermute | solution.py:70
  118.2 36.4 %collective-permute-start.24 = (bf16[448,768]{1,0:T(8,128)(2,1)S(1)}, bf16[448,768]{1,0:T(8,128)(2,1)S(1)}, u32[]{:S(2)}, u32[]{:S(2)}) collective-permute-start(bf16[448,768]{1,0:T(8,128)(2,1)S(1)} %collective-permute-done.20.refs_2_), channel_id=1, source_target_pairs={{0,4},{4,0},{8,12},{12,8},{16,20},{20,16},{24,28},{28,24},{1,5},{5... | collective-permute-start | bytes 2064392 | tf_op jit(solution)/shard_map/ppermute | solution.py:70
  121.7 32.9 %collective-permute-start.25 = (bf16[320,768]{1,0:T(8,128)(2,1)}, bf16[320,768]{1,0:T(8,128)(2,1)S(1)}, u32[]{:S(2)}, u32[]{:S(2)}) collective-permute-start(bf16[320,768]{1,0:T(8,128)(2,1)} %collective-permute-done.11.refs_4_), channel_id=1, source_target_pairs={{0,4},{4,0},{8,12},{12,8},{16,20},{20,16},{24,28},{28,24},{1,5},{5... | collective-permute-start | bytes 1474568 | tf_op jit(solution)/shard_map/ppermute | solution.py:70
  142.6 29.6 %collective-permute-start.27 = (bf16[448,768]{1,0:T(8,128)(2,1)}, bf16[448,768]{1,0:T(8,128)(2,1)}, u32[]{:S(2)}, u32[]{:S(2)}) collective-permute-start(bf16[448,768]{1,0:T(8,128)(2,1)} %get-tuple-element.126.refs_0_), channel_id=1, source_target_pairs={{0,4},{4,0},{8,12},{12,8},{16,20},{20,16},{24,28},{28,24},{1,5},{5... | collective-permute-start | bytes 2064392 | tf_op jit(solution)/shard_map/ppermute | solution.py:70
  144.2 28.0 %collective-permute-start.29 = (bf16[320,768]{1,0:T(8,128)(2,1)}, bf16[320,768]{1,0:T(8,128)(2,1)}, u32[]{:S(2)}, u32[]{:S(2)}) collective-permute-start(bf16[320,768]{1,0:T(8,128)(2,1)} %collective-permute-done.28.refs_6_), channel_id=1, source_target_pairs={{0,4},{4,0},{8,12},{12,8},{16,20},{20,16},{24,28},{28,24},{1,5},{5... | collective-permute-start | bytes 1474568 | tf_op jit(solution)/shard_map/ppermute | solution.py:70
  169.6 30.8 %collective-permute-start.30 = (bf16[4,192,768]{2,1,0:T(8,128)(2,1)}, bf16[4,192,768]{2,1,0:T(8,128)(2,1)S(1)}, u32[]{:S(2)}, u32[]{:S(2)}) collective-permute-start(bf16[4,192,768]{2,1,0:T(8,128)(2,1)} %get-tuple-element.124), channel_id=1, source_target_pairs={{0,8},{4,12},{8,0},{12,4},{16,24},{20,28},{24,16},{28,20},{1,9},{5... | collective-permute-start | bytes 3538952 | tf_op jit(solution)/shard_map/ppermute | solution.py:70
  200.2 26.3 %collective-permute-start.35 = (bf16[512,768]{1,0:T(8,128)(2,1)}, bf16[512,768]{1,0:T(8,128)(2,1)S(1)}, u32[]{:S(2)}, u32[]{:S(2)}) collective-permute-start(bf16[512,768]{1,0:T(8,128)(2,1)} %get-tuple-element.143), channel_id=1, source_target_pairs={{0,8},{4,12},{8,0},{12,4},{16,24},{20,28},{24,16},{28,20},{1,9},{5... | collective-permute-start | bytes 2359304 | tf_op jit(solution)/shard_map/ppermute | solution.py:70
  252.3 56.1 %collective-permute-start.42 = (bf16[512,768]{1,0:T(8,128)(2,1)}, bf16[512,768]{1,0:T(8,128)(2,1)S(1)}, u32[]{:S(2)}, u32[]{:S(2)}) collective-permute-start(bf16[512,768]{1,0:T(8,128)(2,1)} %get-tuple-element.155), channel_id=1, source_target_pairs={{0,8},{4,12},{8,0},{12,4},{16,24},{20,28},{24,16},{28,20},{1,9},{5... | collective-permute-start | bytes 2359304 | tf_op jit(solution)/shard_map/ppermute | solution.py:70
  253.8 133.0 %collective-permute-start.53 = (bf16[2,192,768]{2,1,0:T(8,128)(2,1)}, bf16[2,192,768]{2,1,0:T(8,128)(2,1)}, u32[]{:S(2)}, u32[]{:S(2)}) collective-permute-start(bf16[2,192,768]{2,1,0:T(8,128)(2,1)} %pad_maximum_fusion.4), channel_id=1, source_target_pairs={{0,1},{1,0},{2,3},{3,2},{4,5},{5,4},{6,7},{7,6},{8,9},{9,8},{10,11... | collective-permute-start | bytes 1769480 | tf_op jit(solution)/shard_map/ppermute | solution.py:48
  274.1 100.3 %collective-permute-start.60 = (bf16[128,768]{1,0:T(8,128)(2,1)}, bf16[128,768]{1,0:T(8,128)(2,1)}, u32[]{:S(2)}, u32[]{:S(2)}) collective-permute-start(bf16[128,768]{1,0:T(8,128)(2,1)} %slice.428), channel_id=1, source_target_pairs={{0,8},{4,12},{8,0},{12,4},{16,24},{20,28},{24,16},{28,20},{1,9},{5... | collective-permute-start | bytes 589832 | tf_op jit(solution)/shard_map/ppermute | solution.py:70
  276.5 50.0 %collective-permute-start.58 = (bf16[192,1536]{1,0:T(8,128)(2,1)}, bf16[192,1536]{1,0:T(8,128)(2,1)}, u32[]{:S(2)}, u32[]{:S(2)}) collective-permute-start(bf16[192,1536]{1,0:T(8,128)(2,1)} %fusion.17), channel_id=1, source_target_pairs={{0,16},{4,20},{8,24},{12,28},{16,0},{20,4},{24,8},{28,12},{1,17},{... | collective-permute-start | bytes 1769480 | tf_op jit(solution)/shard_map/ppermute | solution.py:70
  323.0 26.9 %all-to-all-start.2 = ((bf16[8,4,4864]{2,1,0:T(4,128)(2,1)}), bf16[8,4,4864]{2,1,0:T(4,128)(2,1)S(1)}, u32[]{:S(2)}, u32[]{:S(2)}) async-start(bf16[8,4,4864]{2,1,0:T(4,128)(2,1)} %pad_maximum_fusion.5), calls=%async_computation.2 | async-start | bytes 622592 | tf_op jit(solution)/shard_map/all_to_all | solution.py:1447
  332.7 46.8 %collective-permute-start.46 = (bf16[256,768]{1,0:T(8,128)(2,1)}, bf16[256,768]{1,0:T(8,128)(2,1)}, u32[]{:S(2)}, u32[]{:S(2)}) collective-permute-start(bf16[256,768]{1,0:T(8,128)(2,1)} %fusion.24), channel_id=1, source_target_pairs={{0,2},{1,3},{2,0},{3,1},{4,6},{5,7},{6,4},{7,5},{8,10},{9,11},{10,... | collective-permute-start | bytes 1179656 | tf_op jit(solution)/shard_map/ppermute | solution.py:48
  354.7 27.5 %all-to-all-start.3 = ((f32[8,4,96]{2,1,0:T(4,128)}), f32[8,4,96]{2,1,0:T(4,128)S(1)}, u32[]{:S(2)}, u32[]{:S(2)}) async-start(f32[8,4,96]{2,1,0:T(4,128)} %copy.85), calls=%async_computation.3 | async-start | bytes 32768 | tf_op jit(solution)/shard_map/all_to_all | solution.py:1473
  (107 other events, 1223.9 us)

commit v5 on v4

--- a/solution.py
+++ b/solution.py
@@ -1357,7 +1357,8 @@
         rdown_sums = down_keep[0] + down_first[0].astype(f32) + down_far.astype(f32)
         rup_sums = up_keep[0] + up_first[0].astype(f32) + up_far.astype(f32)
         last_first = stay + dp_swap(away, 1).astype(f32)
-        last_second = last_first[:2] + dp_swap(last_first[2:].astype(bf16), 4).astype(f32)
+        last_got = dp_swap(jnp.stack([last_first[1], last_first[3]]).astype(bf16), 2)
+        last_second = jnp.stack([last_first[0], last_first[2]]) + last_got.astype(f32)
     else:
 
         def scatter(value, each):
@@ -1478,7 +1479,7 @@
     normed_a, inv_std_a = norm_parts(tokens.astype(f32))
     tokens_grad = grad_mid + norm_back(grad_hidden_a * (1.0 + scale_a), normed_a, inv_std_a)
     if copies == 8:
-        last_third = dp_swap(last_second[1].astype(bf16), 2)
+        last_third = dp_swap(last_second[1].astype(bf16), 4)
         last_sums = last_second[0] + last_third.astype(f32)
         rup_sums = tied(rup_sums, after)
     if copies == 8:

time: 396 us -> 391 us (0.987)
  waiting for transfers between devices: 104 us -> 94.4 us
    ppermute x30, waiting for transfers between devices: 72.5 us -> 63.1 us  [dp_swap(): return lax.ppermute(value, 'dp', [(i, i ^ mask) for i in range(copies)])]
    unnamed x143 -> x145, local copies, waits for them, and re-layouts: 7.96 us -> 8.84 us
  transfers between devices with their start and end apart: 65 -> 65, of which waited for: 20 -> 21; matrix products, arithmetic and copies ran while one was open for 17% -> 17% of each run, Pallas kernels for 32% -> 33%
where the time goes in v5:
time: 391 us; the launch traced here: 386 us
  Pallas kernels  133 us (34%)
  waiting for transfers between devices  94.4 us (24%)
  starting transfers between devices  79.3 us (20%)
  other arithmetic  44.4 us (11%)
  local copies, waits for them, and re-layouts  28.6 us (7%)
  between operations  4.17 us (1%)
    pallas_call x14, Pallas kernels, kernel_call(): pl.pallas_call(body, grid=(grid,), in_specs=in_specs, out_specs=out_specs...  133 us
    ppermute x30, waiting for transfers between devices, dp_swap(): return lax.ppermute(value, 'dp', [(i, i ^ mask) for i in range(copies)])  63.1 us
    ppermute x30, starting transfers between devices, dp_swap(): return lax.ppermute(value, 'dp', [(i, i ^ mask) for i in range(copies)])  38.1 us
    ppermute x24, starting transfers between devices, swap(): return lax.ppermute(value, 'expert', [(i, i ^ mask) for i in range(size)])  16.3 us
    ppermute x24, waiting for transfers between devices, swap(): return lax.ppermute(value, 'expert', [(i, i ^ mask) for i in range(size)])  16.3 us
    all_to_all x1, waiting for transfers between devices, body(): lax.all_to_all(cond_act.reshape(slots, copies, d_rows).transpose(1, 0, 2)...  10.6 us
    ppermute x7, starting transfers between devices, hop(): lax.ppermute(value, 'dp', [(ring[i], ring[(i + way) % copies]) for i in r...  9.32 us
    unnamed x145, local copies, waits for them, and re-layouts  8.84 us
  transfers between devices with their start and end apart: 65, of which 21 were waited for; matrix products, arithmetic and copies ran while one was open for 17% of the time, Pallas kernels for 33%

profile of v5, /device:TPU:0, one launch (start us, length us, event | category | flops | bytes accessed | tf_op | source)
XLA Modules:
  0.0 386.0 jit_solution(12498152195887617606)
XLA Ops:
  27.4 10.6 %all-to-all-done = bf16[8,4,96]{2,1,0:T(4,128)(2,1)S(1)} async-done(((bf16[8,4,96]{2,1,0:T(4,128)(2,1)}), bf16[8,4,96]{2,1,0:T(4,128)(2,1)S(1)}, u32[]{:S(2)}, u32[]{:S(2)}) %all-to-all-start) | async-done | bytes 6176 | tf_op jit(solution)/shard_map/all_to_all | solution.py:1190
  45.9 3.5 collective-permute-done.6.refs_4_
  67.4 17.4 %collective-permute-done.13.refs_5_ = bf16[288,768]{1,0:T(8,128)(2,1)} collective-permute-done((bf16[288,768]{1,0:T(8,128)(2,1)}, bf16[288,768]{1,0:T(8,128)(2,1)}, u32[]{:S(2)}, u32[]{:S(2)}) %collective-permute-start.13) | collective-permute-done | bytes 442400 | tf_op jit(solution)/shard_map/ppermute | solution.py:70
  88.9 7.4 %shard_map.359 = (bf16[1024,768]{1,0:T(8,128)(2,1)}, bf16[1024,576]{1,0:T(8,128)(2,1)}, bf16[768,576]{1,0:T(8,128)(2,1)}, bf16[4,128,256]{2,1,0:T(8,128)(2,1)}, ...) custom-call(s32[32]{0:T(128)} %concatenate.38.info, ...), custom_call_target="tpu_custom_call" | custom-call | flops 905969664 | bytes 14135680 | tf_op jit(solution)/shard_map/pallas_call | solution.py:152
  96.3 3.8 collective-permute-start.19
  102.2 10.5 %shard_map.360.h0 = bf16[1024,192]{1,0:T(8,128)(2,1)} custom-call(s32[32]{0:T(128)} %concatenate.38.info, bf16[1024,576]{1,0:T(8,128)(2,1)} %get-tuple-element.108.own.every, bf16[1024,576]{1,0:T(8,128)(2,1)} %get-tuple-element.108.own.every), custom_call_target="tpu_custom_call" | custom-call | flops 805306368 | bytes 2752640 | tf_op jit(solution)/shard_map/pallas_call | solution.py:152
  114.6 3.6 collective-permute-done.20.refs_2_
  125.0 16.9 %collective-permute-done.19.s1 = bf16[512,768]{1,0:T(8,128)(2,1)S(1)} collective-permute-done((bf16[512,768]{1,0:T(8,128)(2,1)}, bf16[512,768]{1,0:T(8,128)(2,1)S(1)}, u32[]{:S(2)}, u32[]{:S(2)}) %collective-permute-start.19) | collective-permute-done | bytes 786464 | tf_op jit(solution)/shard_map/ppermute | solution.py:70
  145.4 9.1 %shard_map.361 = (bf16[1024,768]{1,0:T(8,128)(2,1)}, bf16[1024,768]{1,0:T(8,128)(2,1)}, bf16[512,768]{1,0:T(8,128)(2,1)}, f32[256,768]{1,0:T(8,128)}, f32[256,768]{1,0:T(8,128)}, /*index=5*/bf16[192,768]{1,0:T(8,128)(2,1)}) custom-call(s32[32]{0:T(128)} %concatenate.38.info, bf16[4,272,1536]{2,1,0:T(8,128)(2,1)} %pad_maximum_fusion.tok.more.refs_1_.refs_2_, ...), custom_call_target="tpu_custom_call" | custom-call | flops 1409286144 | bytes 14617728 | tf_op jit(solution)/shard_map/pallas_call | solution.py:152
  154.6 14.8 %shard_map.362 = (f32[1024,768]{1,0:T(8,128)}, f32[1024,768]{1,0:T(8,128)}, f32[4,192,768]{2,1,0:T(8,128)}, bf16[4,192,768]{2,1,0:T(8,128)(2,1)}, f32[1,768]{1,0:T(1,128)}) custom-call(s32[32]{0:T(128)} %concatenate.38.info, bf16[1024,768]{1,0:T(8,128)(2,1)} %get-tuple-element.122.hid, bf16[1024,768]{1,0:T(8,128)(2,1)} %get-tuple-element.123.gcl, ...), custom_call_target="tpu_custom_call" | custom-call | flops 7247757312 | bytes 16521344 | tf_op jit(solution)/shard_map/pallas_call | solution.py:152
  176.1 24.0 %shard_map.363 = (f32[512,768]{1,0:T(8,128)}, bf16[512,768]{1,0:T(8,128)(2,1)}, f32[512,768]{1,0:T(8,128)}, bf16[512,768]{1,0:T(8,128)(2,1)}, f32[4,1,384]{2,1,0...) custom-call(s32[32]{0:T(128)} %concatenate.38.info, ...), custom_call_target="tpu_custom_call" | custom-call | flops 9663676416 | bytes 22032512 | tf_op jit(solution)/shard_map/pallas_call | solution.py:152
  204.6 12.6 %shard_map.364 = (bf16[2,384,768]{2,1,0:T(8,128)(2,1)}, f32[2,384,768]{2,1,0:T(8,128)}, bf16[2,192,1536]{2,1,0:T(8,128)(2,1)}, f32[2,192,1536]{2,1,0:T(8,128)}) custom-call(s32[32]{0:T(128)} %concatenate.38.info, bf16[1024,1536]{1,0:T(8,128)(2,1)} %get-tuple-element.132.act, bf16[1024,1536]{1,0:T(8,128)(2,1)} %get-tuple-element.133.grad, ...), custom_call_target="tpu_custom_call" | custom-call | flops 4831838208 | bytes 16515200 | tf_op jit(solution)/shard_map/pallas_call | solution.py:152
  227.4 6.2 %shard_map.365 = (bf16[2,256,768]{2,1,0:T(8,128)(2,1)}, f32[2,256,768]{2,1,0:T(8,128)}, f32[4,1,768]{2,1,0:T(1,128)}) custom-call(f32[512,768]{1,0:T(8,128)} %get-tuple-element.142.own, bf16[512,768]{1,0:T(8,128)(2,1)} %copy-done.22, f32[1,768]{1,0:T(1,128)} %broadcast_in_dim.103.bias.refs_2_, bf16[4,128,256]{2,1,0:T(8,128)(2,1)} %get-tuple-element.114.tab, ...), custom_call_target="tpu_custom_call" | custom-call | flops 201326592 | bytes 11487232 | tf_op jit(solution)/shard_map/pallas_call | solution.py:152
  234.6 3.4 collective-permute-done.37
  257.9 3.7 shard_map.366
  264.0 8.1 %collective-permute-done.32 = bf16[384,768]{1,0:T(8,128)(2,1)} collective-permute-done((bf16[384,768]{1,0:T(8,128)(2,1)}, bf16[384,768]{1,0:T(8,128)(2,1)}, u32[]{:S(2)}, u32[]{:S(2)}) %collective-permute-start.32) | collective-permute-done | bytes 589856 | tf_op jit(solution)/shard_map/ppermute | solution.py:70
  279.7 18.2 %shard_map.367.gr = bf16[1024,576]{1,0:T(8,128)(2,1)} custom-call(s32[32]{0:T(128)} %concatenate.38.info, bf16[1024,576]{1,0:T(8,128)(2,1)} %get-tuple-element.108.own.every, bf16[1024,576]{1,0:T(8,128)(2,1)} %get-tuple-element.108.own.every, bf16[1024,768]{1,0:T(8,128)(2,1)} %copy-done.6, bf16[192,768]{1,0:T(8,128)(2,1)} %get-tuple-element.150.rel), custom_call_target="tpu_custom_call" | custom-call | flops 2315255808 | bytes 5406848 | tf_op jit(solution)/shard_map/pallas_call | solution.py:152
  298.0 9.4 %shard_map.368 = (bf16[4,96,768]{2,1,0:T(8,128)(2,1)}, f32[4,96,768]{2,1,0:T(8,128)}, bf16[2,256,768]{2,1,0:T(8,128)(2,1)}, f32[2,256,768]{2,1,0:T(8,128)}, f32[8,768]{1,0:T(8,128)}, /*index=5*/f32[1,1344]{1,0:T(1,128)}) custom-call(s32[32]{0:T(128)} %concatenate.38.info, bf16[4,272,1536]{2,1,0:T(8,128)(2,1)} %pad_maximum_fusion.tok.more.refs_1_.refs_2_, ...), custom_call_target="tpu_custom_call" | custom-call | flops 2113929216 | bytes 14284160 | tf_op jit(solution)/shard_map/pallas_call | solution.py:152
  309.0 6.1 %shard_map.369 = (bf16[2,256,768]{2,1,0:T(8,128)(2,1)}, f32[2,256,768]{2,1,0:T(8,128)}, f32[4,1,768]{2,1,0:T(1,128)}) custom-call(f32[512,768]{1,0:T(8,128)} %get-tuple-element.154.own, bf16[512,768]{1,0:T(8,128)(2,1)} %copy-done.21, f32[1,768]{1,0:T(1,128)} %get-tuple-element.215.bias, bf16[4,128,256]{2,1,0:T(8,128)(2,1)} %get-tuple-element.114.tab, ...), custom_call_target="tpu_custom_call" | custom-call | flops 201326592 | bytes 11491328 | tf_op jit(solution)/shard_map/pallas_call | solution.py:152
  322.8 3.5 all-to-all-start.2
  337.1 4.6 %collective-permute-done.50 = bf16[2,96,768]{2,1,0:T(8,128)(2,1)S(1)} collective-permute-done((bf16[2,96,768]{2,1,0:T(8,128)(2,1)S(1)}, bf16[2,96,768]{2,1,0:T(8,128)(2,1)S(1)}, u32[]{:S(2)}, u32[]{:S(2)}) %collective-permute-start.50) | collective-permute-done | bytes 294944 | tf_op jit(solution)/shard_map/ppermute | solution.py:70
  346.4 5.4 %all-to-all-start.3 = ((f32[8,4,96]{2,1,0:T(4,128)}), f32[8,4,96]{2,1,0:T(4,128)S(1)}, u32[]{:S(2)}, u32[]{:S(2)}) async-start(f32[8,4,96]{2,1,0:T(4,128)} %copy.85), calls=%async_computation.3 | async-start | bytes 32768 | tf_op jit(solution)/shard_map/all_to_all | solution.py:1474
  365.1 3.5 collective-permute-done.54.l2
  381.6 4.1 %shard_map.370 = (f32[96,3072]{1,0:T(8,128)}, f32[384,768]{1,0:T(8,128)}, f32[96,2304]{1,0:T(8,128)}, f32[96,768]{1,0:T(8,128)}) custom-call(s32[32]{0:T(128)} %concatenate.38.info, bf16[192,768]{1,0:T(8,128)(2,1)} %copy-done.5, bf16[192,768]{1,0:T(8,128)(2,1)} %copy-done.20, bf16[2,192,768]{2,1,0:T(8,128)(2,1)} %collective-permute-done.53.s13, ...), custom_call_target="tpu_custom_call" | custom-call | bytes 5308544 | tf_op jit(solution)/shard_map/pallas_call | solution.py:152
  (405 shorter events, 171.3 us)
Async XLA Ops:
  8.9 29.0 %collective-permute-start.2 = (bf16[112,576]{1,0:T(8,128)(2,1)}, bf16[112,576]{1,0:T(8,128)(2,1)}, u32[]{:S(2)}, u32[]{:S(2)}) collective-permute-start(bf16[112,576]{1,0:T(8,128)(2,1)} %get-tuple-element.100.refs_0_), channel_id=1, source_target_pairs={{0,8},{8,16},{16,24},{24,28},{28,20},{20,12},{12,4},{4,0},{1,9},{9... | collective-permute-start | bytes 387080 | tf_op jit(solution)/shard_map/ppermute | solution.py:119
  9.1 43.1 %collective-permute-start.7 = (bf16[288,768]{1,0:T(8,128)(2,1)}, bf16[288,768]{1,0:T(8,128)(2,1)S(1)}, u32[]{:S(2)}, u32[]{:S(2)}) collective-permute-start(bf16[288,768]{1,0:T(8,128)(2,1)} %get-tuple-element.115.refs_0_), channel_id=1, source_target_pairs={{0,16},{4,20},{8,24},{12,28},{16,0},{20,4},{24,8},{28,12},{1,17},{... | collective-permute-start | bytes 1327112 | tf_op jit(solution)/shard_map/ppermute | solution.py:70
  18.8 35.8 %collective-permute-start = (bf16[272,1536]{1,0:T(8,128)(2,1)}, bf16[272,1536]{1,0:T(8,128)(2,1)S(1)}, u32[]{:S(2)}, u32[]{:S(2)}) collective-permute-start(bf16[272,1536]{1,0:T(8,128)(2,1)} %get-tuple-element.202), channel_id=1, source_target_pairs={{0,2},{1,3},{2,0},{3,1},{4,6},{5,7},{6,4},{7,5},{8,10},{9,11},{10,... | collective-permute-start | bytes 2506760 | tf_op jit(solution)/shard_map/ppermute | solution.py:48
  25.4 31.5 %collective-permute-start.11 = (bf16[320,768]{1,0:T(8,128)(2,1)}, bf16[320,768]{1,0:T(8,128)(2,1)}, u32[]{:S(2)}, u32[]{:S(2)}) collective-permute-start(bf16[320,768]{1,0:T(8,128)(2,1)} %get-tuple-element.104), channel_id=1, source_target_pairs={{0,8},{4,12},{8,0},{12,4},{16,24},{20,28},{24,16},{28,20},{1,9},{5... | collective-permute-start | bytes 1474568 | tf_op jit(solution)/shard_map/ppermute | solution.py:70
  56.0 28.8 %collective-permute-start.1 = (bf16[2,272,1536]{2,1,0:T(8,128)(2,1)}, bf16[2,272,1536]{2,1,0:T(8,128)(2,1)}, u32[]{:S(2)}, u32[]{:S(2)}) collective-permute-start(bf16[2,272,1536]{2,1,0:T(8,128)(2,1)} %pad_maximum_fusion.1), channel_id=1, source_target_pairs={{0,1},{1,0},{2,3},{3,2},{4,5},{5,4},{6,7},{7,6},{8,9},{9,8},{10,11... | collective-permute-start | bytes 5013512 | tf_op jit(solution)/shard_map/ppermute | solution.py:48
  58.6 54.1 %collective-permute-start.21 = (bf16[288,768]{1,0:T(8,128)(2,1)S(1)}, bf16[288,768]{1,0:T(8,128)(2,1)}, u32[]{:S(2)}, u32[]{:S(2)}) collective-permute-start(bf16[288,768]{1,0:T(8,128)(2,1)S(1)} %copy-done.31), channel_id=1, source_target_pairs={{0,4},{4,0},{8,12},{12,8},{16,20},{20,16},{24,28},{28,24},{1,5},{5... | collective-permute-start | bytes 1327112 | tf_op jit(solution)/shard_map/ppermute | solution.py:70
  59.9 28.4 %collective-permute-start.14 = (bf16[112,576]{1,0:T(8,128)(2,1)}, bf16[112,576]{1,0:T(8,128)(2,1)}, u32[]{:S(2)}, u32[]{:S(2)}) collective-permute-start(bf16[112,576]{1,0:T(8,128)(2,1)} %collective-permute-done.9.refs_5_), channel_id=1, source_target_pairs={{0,8},{8,16},{16,24},{24,28},{28,20},{20,12},{12,4},{4,0},{1,9},{9... | collective-permute-start | bytes 387080 | tf_op jit(solution)/shard_map/ppermute | solution.py:119
  61.2 38.9 %collective-permute-start.15 = (bf16[288,768]{1,0:T(8,128)(2,1)}, bf16[288,768]{1,0:T(8,128)(2,1)}, u32[]{:S(2)}, u32[]{:S(2)}) collective-permute-start(bf16[288,768]{1,0:T(8,128)(2,1)} %copy-done.32), channel_id=1, source_target_pairs={{0,4},{4,0},{8,12},{12,8},{16,20},{20,16},{24,28},{28,24},{1,5},{5... | collective-permute-start | bytes 1327112 | tf_op jit(solution)/shard_map/ppermute | solution.py:70
  84.8 33.4 %collective-permute-start.20 = (bf16[448,768]{1,0:T(8,128)(2,1)}, bf16[448,768]{1,0:T(8,128)(2,1)S(1)}, u32[]{:S(2)}, u32[]{:S(2)}) collective-permute-start(bf16[448,768]{1,0:T(8,128)(2,1)} %get-tuple-element.126.refs_0_), channel_id=1, source_target_pairs={{0,16},{4,20},{8,24},{12,28},{16,0},{20,4},{24,8},{28,12},{1,17},{... | collective-permute-start | bytes 2064392 | tf_op jit(solution)/shard_map/ppermute | solution.py:70
  96.3 45.6 %collective-permute-start.19 = (bf16[512,768]{1,0:T(8,128)(2,1)}, bf16[512,768]{1,0:T(8,128)(2,1)S(1)}, u32[]{:S(2)}, u32[]{:S(2)}) collective-permute-start(bf16[512,768]{1,0:T(8,128)(2,1)} %get-tuple-element.111.s0), channel_id=1, source_target_pairs={{0,8},{4,12},{8,0},{12,4},{16,24},{20,28},{24,16},{28,20},{1,9},{5... | collective-permute-start | bytes 2359304 | tf_op jit(solution)/shard_map/ppermute | solution.py:70
  114.3 28.3 %collective-permute-start.28 = (bf16[320,768]{1,0:T(8,128)(2,1)}, bf16[320,768]{1,0:T(8,128)(2,1)}, u32[]{:S(2)}, u32[]{:S(2)}) collective-permute-start(bf16[320,768]{1,0:T(8,128)(2,1)} %collective-permute-done.11.refs_4_), channel_id=1, source_target_pairs={{0,16},{4,20},{8,24},{12,28},{16,0},{20,4},{24,8},{28,12},{1,17},{... | collective-permute-start | bytes 1474568 | tf_op jit(solution)/shard_map/ppermute | solution.py:70
  118.2 36.4 %collective-permute-start.24 = (bf16[448,768]{1,0:T(8,128)(2,1)S(1)}, bf16[448,768]{1,0:T(8,128)(2,1)S(1)}, u32[]{:S(2)}, u32[]{:S(2)}) collective-permute-start(bf16[448,768]{1,0:T(8,128)(2,1)S(1)} %collective-permute-done.20.refs_2_), channel_id=1, source_target_pairs={{0,4},{4,0},{8,12},{12,8},{16,20},{20,16},{24,28},{28,24},{1,5},{5... | collective-permute-start | bytes 2064392 | tf_op jit(solution)/shard_map/ppermute | solution.py:70
  121.6 32.9 %collective-permute-start.25 = (bf16[320,768]{1,0:T(8,128)(2,1)}, bf16[320,768]{1,0:T(8,128)(2,1)S(1)}, u32[]{:S(2)}, u32[]{:S(2)}) collective-permute-start(bf16[320,768]{1,0:T(8,128)(2,1)} %collective-permute-done.11.refs_4_), channel_id=1, source_target_pairs={{0,4},{4,0},{8,12},{12,8},{16,20},{20,16},{24,28},{28,24},{1,5},{5... | collective-permute-start | bytes 1474568 | tf_op jit(solution)/shard_map/ppermute | solution.py:70
  142.6 29.6 %collective-permute-start.27 = (bf16[448,768]{1,0:T(8,128)(2,1)}, bf16[448,768]{1,0:T(8,128)(2,1)}, u32[]{:S(2)}, u32[]{:S(2)}) collective-permute-start(bf16[448,768]{1,0:T(8,128)(2,1)} %get-tuple-element.126.refs_0_), channel_id=1, source_target_pairs={{0,4},{4,0},{8,12},{12,8},{16,20},{20,16},{24,28},{28,24},{1,5},{5... | collective-permute-start | bytes 2064392 | tf_op jit(solution)/shard_map/ppermute | solution.py:70
  144.1 28.0 %collective-permute-start.29 = (bf16[320,768]{1,0:T(8,128)(2,1)}, bf16[320,768]{1,0:T(8,128)(2,1)}, u32[]{:S(2)}, u32[]{:S(2)}) collective-permute-start(bf16[320,768]{1,0:T(8,128)(2,1)} %collective-permute-done.28.refs_6_), channel_id=1, source_target_pairs={{0,4},{4,0},{8,12},{12,8},{16,20},{20,16},{24,28},{28,24},{1,5},{5... | collective-permute-start | bytes 1474568 | tf_op jit(solution)/shard_map/ppermute | solution.py:70
  169.5 30.8 %collective-permute-start.30 = (bf16[4,192,768]{2,1,0:T(8,128)(2,1)}, bf16[4,192,768]{2,1,0:T(8,128)(2,1)S(1)}, u32[]{:S(2)}, u32[]{:S(2)}) collective-permute-start(bf16[4,192,768]{2,1,0:T(8,128)(2,1)} %get-tuple-element.124), channel_id=1, source_target_pairs={{0,8},{4,12},{8,0},{12,4},{16,24},{20,28},{24,16},{28,20},{1,9},{5... | collective-permute-start | bytes 3538952 | tf_op jit(solution)/shard_map/ppermute | solution.py:70
  200.2 26.4 %collective-permute-start.35 = (bf16[512,768]{1,0:T(8,128)(2,1)}, bf16[512,768]{1,0:T(8,128)(2,1)S(1)}, u32[]{:S(2)}, u32[]{:S(2)}) collective-permute-start(bf16[512,768]{1,0:T(8,128)(2,1)} %get-tuple-element.143), channel_id=1, source_target_pairs={{0,8},{4,12},{8,0},{12,4},{16,24},{20,28},{24,16},{28,20},{1,9},{5... | collective-permute-start | bytes 2359304 | tf_op jit(solution)/shard_map/ppermute | solution.py:70
  245.8 26.2 %collective-permute-start.32 = (bf16[384,768]{1,0:T(8,128)(2,1)}, bf16[384,768]{1,0:T(8,128)(2,1)}, u32[]{:S(2)}, u32[]{:S(2)}) collective-permute-start(bf16[384,768]{1,0:T(8,128)(2,1)} %fusion.16), channel_id=1, source_target_pairs={{0,16},{4,20},{8,24},{12,28},{16,0},{20,4},{24,8},{28,12},{1,17},{... | collective-permute-start | bytes 1769480 | tf_op jit(solution)/shard_map/ppermute | solution.py:70
  252.2 55.9 %collective-permute-start.42 = (bf16[512,768]{1,0:T(8,128)(2,1)}, bf16[512,768]{1,0:T(8,128)(2,1)S(1)}, u32[]{:S(2)}, u32[]{:S(2)}) collective-permute-start(bf16[512,768]{1,0:T(8,128)(2,1)} %get-tuple-element.155), channel_id=1, source_target_pairs={{0,8},{4,12},{8,0},{12,4},{16,24},{20,28},{24,16},{28,20},{1,9},{5... | collective-permute-start | bytes 2359304 | tf_op jit(solution)/shard_map/ppermute | solution.py:70
  253.8 127.9 %collective-permute-start.53 = (bf16[2,192,768]{2,1,0:T(8,128)(2,1)}, bf16[2,192,768]{2,1,0:T(8,128)(2,1)}, u32[]{:S(2)}, u32[]{:S(2)}) collective-permute-start(bf16[2,192,768]{2,1,0:T(8,128)(2,1)} %pad_maximum_fusion.4), channel_id=1, source_target_pairs={{0,1},{1,0},{2,3},{3,2},{4,5},{5,4},{6,7},{7,6},{8,9},{9,8},{10,11... | collective-permute-start | bytes 1769480 | tf_op jit(solution)/shard_map/ppermute | solution.py:48
  274.0 95.0 %collective-permute-start.60 = (bf16[128,768]{1,0:T(8,128)(2,1)}, bf16[128,768]{1,0:T(8,128)(2,1)}, u32[]{:S(2)}, u32[]{:S(2)}) collective-permute-start(bf16[128,768]{1,0:T(8,128)(2,1)} %slice.436), channel_id=1, source_target_pairs={{0,8},{4,12},{8,0},{12,4},{16,24},{20,28},{24,16},{28,20},{1,9},{5... | collective-permute-start | bytes 589832 | tf_op jit(solution)/shard_map/ppermute | solution.py:70
  276.4 49.9 %collective-permute-start.58 = (bf16[192,1536]{1,0:T(8,128)(2,1)}, bf16[192,1536]{1,0:T(8,128)(2,1)}, u32[]{:S(2)}, u32[]{:S(2)}) collective-permute-start(bf16[192,1536]{1,0:T(8,128)(2,1)} %fusion.17), channel_id=1, source_target_pairs={{0,16},{4,20},{8,24},{12,28},{16,0},{20,4},{24,8},{28,12},{1,17},{... | collective-permute-start | bytes 1769480 | tf_op jit(solution)/shard_map/ppermute | solution.py:70
  333.7 40.0 %collective-permute-start.46 = (bf16[256,768]{1,0:T(8,128)(2,1)}, bf16[256,768]{1,0:T(8,128)(2,1)}, u32[]{:S(2)}, u32[]{:S(2)}) collective-permute-start(bf16[256,768]{1,0:T(8,128)(2,1)} %fusion.24), channel_id=1, source_target_pairs={{0,2},{1,3},{2,0},{3,1},{4,6},{5,7},{6,4},{7,5},{8,10},{9,11},{10,... | collective-permute-start | bytes 1179656 | tf_op jit(solution)/shard_map/ppermute | solution.py:48
  346.4 30.0 %all-to-all-start.3 = ((f32[8,4,96]{2,1,0:T(4,128)}), f32[8,4,96]{2,1,0:T(4,128)S(1)}, u32[]{:S(2)}, u32[]{:S(2)}) async-start(f32[8,4,96]{2,1,0:T(4,128)} %copy.85), calls=%async_computation.3 | async-start | bytes 32768 | tf_op jit(solution)/shard_map/all_to_all | solution.py:1474
  (108 other events, 1206.3 us)
